TPU v7x, 32 devices: a whole 2x2x4 slice. The times are simulated.
32 devices in a mesh: dp: 8 (over z, y), mp: 4 (over x, core).
Axes of the slice: x: 2, y: 2, z: 4, core: 2. Of those that a mesh axis runs over, the one named last changes fastest.
Arguments:
- hot_ids: int32 [8192, 7], P('dp'), may hold values from 0 to 1023
- touched: int32 [8, 4, 256], P('dp', 'mp'), may hold values from 0 to 8191, as said below
- cold_items: int32 [8, 4, 2048], P('dp', 'mp'), may hold values from 0 to 255
- bag_counts: int32 [8, 4, 1024], P('dp', 'mp'), may hold values from 1 to 8, 2048 in all within a row
- owner_map: int32 [8192], replicated, may hold values from 0 to 8191, as said below
- grad_out: bfloat16 [8192, 256], P('dp'), may hold values from -6 to 6
- weight_in: bfloat16 [1024, 512], P(None, 'mp'), may hold values from -0.1875 to 0.1875
- bias_in: float32 [512], P('mp'), may hold values from -4 to 4
- weight_out: bfloat16 [512, 256], P('mp'), may hold values from -0.25 to 0.25
- hot_table: float32 [1024, 128], replicated, may hold values from -6 to 6
- hot_accum: float32 [1024, 128], replicated, may hold values from 0.25 to 4
- cold_table: float32 [8192, 128], P(('dp', 'mp')), may hold values from -6 to 6
- cold_accum: float32 [8192, 128], P(('dp', 'mp')), may hold values from 0.25 to 4
Outputs:
- hot_updated: float32 [1024, 128], replicated
- hot_accum_new: float32 [1024, 128], replicated
- cold_updated: float32 [8192, 128], P(('dp', 'mp'))
- cold_accum_new: float32 [8192, 128], P(('dp', 'mp'))
Inputs may be any that keep to these rules, and one draw needn't show every extreme that they name: owner_map is a permutation of the cold row ids: cold row g is stored in row owner_map[g] of cold_table. `touched`: the 256 ids of one device are distinct, and owner_map sends all of them to rows stored on devices with the same mp index as that device; at most 64 of them are stored on any one dp index, and exactly 64 on some.
All inputs are finite; a program needn't handle non-finite values.
Results may differ from a plain program's by a relative error of at most 0.0038.
Values may be sent and summed in bfloat16 or wider, within the bound.
No kernel may reach another device: no remote copies, remote signals or barrier semaphores. Data moves between devices by JAX's collectives and lax.ppermute only.
A program may use at most 64 MiB of HBM per device.

v0:
```python
import jax
import jax.numpy as jnp
from jax import lax
from jax.sharding import PartitionSpec as P

STEP_SIZE = 0.5
HIGHEST = lax.Precision.HIGHEST


def adagrad(table_rows, accum_rows, grad_rows):
    accum_new = accum_rows + grad_rows * grad_rows
    return (table_rows - STEP_SIZE * grad_rows / jnp.sqrt(accum_new), accum_new)


def silu_grad(pre_act, back_grad):
    sigmoid_val = jax.nn.sigmoid(pre_act)
    return (back_grad * sigmoid_val * (1.0 + pre_act * (1.0 - sigmoid_val))).astype(jnp.bfloat16)


def per_device(
    hot_ids,
    touched,
    cold_items,
    bag_counts,
    owner_map,
    grad_out,
    weight_in,
    bias_in,
    weight_out,
    hot_table,
    hot_accum,
    cold_table,
    cold_accum,
):
    dp_count = lax.axis_size("dp")
    mp_count = lax.axis_size("mp")
    slot_count = cold_table.shape[0]
    emb_width = cold_table.shape[1]
    samples = hot_ids.shape[0]
    fields = hot_ids.shape[1]
    hot_cols = fields * emb_width
    touch_count = touched.shape[2]
    capacity = 2 * touch_count // dp_count
    share_rows = samples // mp_count
    my_start = lax.axis_index("mp") * share_rows
    my_ids = touched[0, 0]
    stored_at = owner_map[my_ids]
    owner_dp = stored_at // (mp_count * slot_count)
    slot_index = stored_at % slot_count
    owner_hits = (owner_dp[:, None] == jnp.arange(dp_count, dtype=jnp.int32)[None, :]).astype(
        jnp.float32
    )
    touch_iota = jnp.arange(touch_count, dtype=jnp.int32)
    earlier = (touch_iota[:, None] > touch_iota[None, :]).astype(jnp.float32)
    before_mine = jnp.dot(earlier, owner_hits, precision=HIGHEST)
    rank_owner = jnp.sum(before_mine * owner_hits, axis=1).astype(jnp.int32)
    bucket_pos = owner_dp * capacity + rank_owner
    requests = (
        jnp.zeros((dp_count * capacity,), jnp.int32)
        .at[bucket_pos]
        .set(slot_index)
        .reshape(dp_count, capacity)
    )
    asked_slots = lax.all_to_all(requests, "dp", split_axis=0, concat_axis=0, tiled=True)
    rows_out = cold_table[asked_slots]
    rows_back = lax.all_to_all(rows_out, "dp", split_axis=0, concat_axis=0, tiled=True)
    fetched = rows_back.reshape(dp_count * capacity, emb_width)[bucket_pos]
    bag_sizes = bag_counts[0, 0]
    end_pos = jnp.cumsum(bag_sizes)
    start_pos = end_pos - bag_sizes
    items_here = cold_items[0, 0]
    item_pos = jnp.arange(items_here.shape[0], dtype=jnp.int32)
    member = (
        (item_pos[None, :] >= start_pos[:, None]) & (item_pos[None, :] < end_pos[:, None])
    ).astype(jnp.bfloat16)
    picks = (items_here[:, None] == touch_iota[None, :]).astype(jnp.bfloat16)
    count_mat = jnp.dot(member, picks, preferred_element_type=jnp.float32)
    pooled_part = jnp.dot(count_mat, fetched, precision=HIGHEST)
    my_hot_ids = lax.dynamic_slice_in_dim(hot_ids, my_start, share_rows, 0)
    full_in = lax.all_gather(weight_in, "mp", axis=1, tiled=True)
    full_out = lax.all_gather(weight_out, "mp", axis=0, tiled=True)
    full_bias = lax.all_gather(bias_in, "mp", axis=0, tiled=True)
    pooled_mine = lax.psum_scatter(pooled_part, "mp", scatter_dimension=0, tiled=True)
    my_grads = lax.dynamic_slice_in_dim(grad_out, my_start, share_rows, 0)
    hot_rows = hot_table[my_hot_ids].reshape(share_rows, hot_cols)
    inputs = jnp.concatenate([hot_rows, pooled_mine], axis=1).astype(jnp.bfloat16)
    pre_act = jnp.dot(inputs, full_in, preferred_element_type=jnp.float32) + full_bias
    back_grad = lax.dot_general(
        my_grads, full_out, (((1,), (1,)), ((), ())), preferred_element_type=jnp.float32
    )
    hidden_grad = silu_grad(pre_act, back_grad)
    input_grad = lax.dot_general(
        hidden_grad, full_in, (((1,), (1,)), ((), ())), preferred_element_type=jnp.float32
    )
    hot_part = jax.ops.segment_sum(
        input_grad[:, :hot_cols].reshape(share_rows * fields, emb_width),
        my_hot_ids.reshape(share_rows * fields),
        num_segments=hot_table.shape[0],
    )
    bag_grad = lax.all_gather(input_grad[:, hot_cols:], "mp", axis=0, tiled=True)
    touch_grad = lax.dot_general(count_mat, bag_grad, (((0,), (0,)), ((), ())), precision=HIGHEST)
    outgoing = (
        jnp.zeros((dp_count * capacity, emb_width), jnp.float32)
        .at[bucket_pos]
        .set(touch_grad)
        .reshape(dp_count, capacity, emb_width)
    )
    arrived = lax.all_to_all(outgoing, "dp", split_axis=0, concat_axis=0, tiled=True)
    cold_grad = jax.ops.segment_sum(
        arrived.reshape(-1, emb_width), asked_slots.reshape(-1), num_segments=slot_count
    )
    cold_updated, cold_accum_new = adagrad(cold_table, cold_accum, cold_grad)
    hot_grad = lax.psum(hot_part, ("dp", "mp"))
    hot_updated, hot_accum_new = adagrad(hot_table, hot_accum, hot_grad)
    return (hot_updated, hot_accum_new, cold_updated, cold_accum_new)


def solution(mesh):
    return jax.shard_map(
        per_device,
        mesh=mesh,
        in_specs=(
            P("dp", None),
            P("dp", "mp", None),
            P("dp", "mp", None),
            P("dp", "mp", None),
            P(),
            P("dp", None),
            P(None, "mp"),
            P("mp"),
            P("mp", None),
            P(),
            P(),
            P(("dp", "mp"), None),
            P(("dp", "mp"), None),
        ),
        out_specs=(P(), P(), P(("dp", "mp"), None), P(("dp", "mp"), None)),
        check_vma=False,
    )
```

profile of v0, /device:TPU:0, one launch (start us, length us, event | category | flops | bytes accessed | tf_op | source)
XLA Modules:
  0.0 244.5 jit_solution(4974534125762545410)
XLA Ops:
  7.2 0.7 compare_select_fusion.3
  8.0 2.0 gather_fusion.1
  10.0 0.2 fusion.8
  10.2 1.4 scatter_custom_fusion
  11.6 0.7 all_to_all.14
  12.3 7.3 %all-to-all-start = ((s32[8,1,64]{2,1,0:T(1,128)}), s32[8,1,64]{2,1,0:T(1,128)S(1)}, u32[]{:S(2)}, u32[]{:S(2)}) async-start(s32[8,1,64]{2,1,0:T(1,128)} %all_to_all.14), calls=%async_computation | async-start | bytes 8192 | tf_op jit(solution)/shard_map/all_to_all | solution.py:64
  19.6 0.3 reduce-window.9
  19.9 0.1 slice.13
  20.0 0.1 slice_reduce_fusion
  20.1 0.1 fusion.36
  20.2 5.8 %all-to-all-done = s32[8,1,64]{2,1,0:T(1,128)S(1)} async-done(((s32[8,1,64]{2,1,0:T(1,128)}), s32[8,1,64]{2,1,0:T(1,128)S(1)}, u32[]{:S(2)}, u32[]{:S(2)}) %all-to-all-start) | async-done | bytes 2080 | tf_op jit(solution)/shard_map/all_to_all | solution.py:64
  26.0 0.1 reshape.224
  26.1 1.6 gather_fusion.2
  27.8 3.4 %all-to-all-start.1 = ((f32[8,64,128]{2,1,0:T(8,128)}), f32[8,64,128]{2,1,0:T(8,128)S(1)}, u32[]{:S(2)}, u32[]{:S(2)}) async-start(f32[8,64,128]{2,1,0:T(8,128)} %bitcast.10), calls=%async_computation.1 | async-start | bytes 524288 | tf_op jit(solution)/shard_map/all_to_all | solution.py:66
  31.2 2.6 %fusion.1 = f32[1024,256]{1,0:T(8,128)S(1)} fusion(s32[1024]{0:T(1024)S(1)} %get-tuple-element.11, s32[1024]{0:T(1024)S(1)} %get-tuple-element.10, s32[2048]{0:T(1024)S(1)} %bitcast.43), kind=kOutput, calls=%fused_computation.11 | convolution fusion | flops 1080557568 | bytes 1064960 | tf_op jit(solution)/shard_map/dot_general | solution.py:77
  33.9 5.5 %all-to-all-done.1 = f32[8,64,128]{2,1,0:T(8,128)S(1)} async-done(((f32[8,64,128]{2,1,0:T(8,128)}), f32[8,64,128]{2,1,0:T(8,128)S(1)}, u32[]{:S(2)}, u32[]{:S(2)}) %all-to-all-start.1) | async-done | bytes 262176 | tf_op jit(solution)/shard_map/all_to_all | solution.py:66
  39.3 0.7 gather_fusion.3
  40.1 1.8 fusion.37
  41.9 0.7 all-gather.3.cloned.1.call-update
  42.7 0.7 compare_select_fusion
  43.4 0.1 copy.20
  43.5 0.2 reshape.208
  43.7 0.1 copy.19
  43.9 0.2 reshape.248
  44.1 3.2 %gather_fusion = bf16[1792,128]{1,0:T(8,128)(2,1)S(1)} fusion(f32[1024,128]{1,0:T(8,128)S(1)} %copy-done.1, s32[2048]{0:T(1024)S(1)} %pad_clamp_fusion), kind=kCustom, calls=%fused_computation | custom fusion | bytes 924672 | tf_op jit(solution)/shard_map/gather | solution.py:85
  47.3 0.5 reshape.199
  47.8 5.1 %all-gather = f32[4,1,128]{2,1,0:T(1,128)S(1)} all-gather(f32[1,1,128]{2,1,0:T(1,128)S(1)} %bitcast.42), channel_id=1, replica_groups=mesh['dp'=8,'mp'=4] {'mp'}, dimensions={0}, use_global_device_ids=true | all-gather | bytes 2560 | tf_op jit(solution)/shard_map/all_gather | solution.py:82
  52.9 5.8 %all_gather.12 = bf16[512,256]{1,0:T(8,128)(2,1)S(1)} all-gather(bf16[128,256]{1,0:T(8,128)(2,1)S(1)} %copy-done.6), channel_id=1, replica_groups=mesh['dp'=8,'mp'=4] {'mp'}, dimensions={0}, use_global_device_ids=true | all-gather | bytes 327680 | tf_op jit(solution)/shard_map/all_gather | solution.py:81
  58.7 3.5 %reduce-scatter.2.cloned.1.call-done = f32[256,128]{1,0:T(8,128)} async-done(((f32[1024,128]{1,0:T(8,128)}), f32[256,128]{1,0:T(8,128)}) %reduce-scatter.2.cloned.1.call-update) | async-done | bytes 131088 | tf_op jit(solution)/shard_map/reduce_scatter | solution.py:83
  62.2 0.9 convert.8
  63.1 17.5 %all-gather.3.cloned.1.call-done = bf16[1024,512]{1,0:T(8,128)(2,1)} async-done(((bf16[1024,128]{1,0:T(8,128)(2,1)}), bf16[1024,512]{1,0:T(8,128)(2,1)}) %all-gather.3.cloned.1.call-update) | async-done | bytes 1048592 | tf_op jit(solution)/shard_map/all_gather | solution.py:80
  80.6 2.5 %convolution_add_fusion = f32[256,512]{1,0:T(8,128)} fusion(bf16[1024,512]{1,0:T(8,128)(2,1)} %all-gather.3.cloned.1.call-done, bf16[256,128]{1,0:T(8,128)(2,1)S(1)} %convert.8, bf16[256,896]{1,0:T(8,128)(2,1)S(1)} %reshape.199, f32[512]{0:T(512)S(1)} %bitcast.41), kind=kOutput, calls=%fused_computation.15 | convolution fusion | flops 269615104 | bytes 2099200 | tf_op jit(solution)/shard_map/dot_general | solution.py:87
  83.0 2.0 fusion.7
  85.1 1.0 copy-done.3
  86.1 1.2 slice.26
  87.3 1.0 reshape.250
  88.3 12.6 %scatter_custom_fusion.1 = f32[1024,128]{1,0:T(8,128)} fusion(s32[1792]{0:T(1024)S(1)} %reshape.248, f32[1792,128]{1,0:T(8,128)} %reshape.250, f32[]{:T(128)} %constant.20.clone.1), kind=kCustom, calls=%fused_computation.37 | custom fusion | flops 229376 | bytes 524800 | tf_op jit(solution)/shard_map/scatter-add | solution.py:95
  101.0 7.4 %all_gather.15 = f32[1024,128]{1,0:T(8,128)S(1)} all-gather(f32[256,128]{1,0:T(8,128)S(1)} %slice-done), channel_id=1, replica_groups=mesh['dp'=8,'mp'=4] {'mp'}, dimensions={0}, use_global_device_ids=true | all-gather | bytes 655360 | tf_op jit(solution)/shard_map/all_gather | solution.py:100
  108.4 1.8 fusion.38
  110.2 1.8 scatter_custom_fusion.2
  112.0 5.5 %all-to-all-start.2 = ((f32[8,64,128]{2,1,0:T(8,128)}), f32[8,64,128]{2,1,0:T(8,128)S(1)}, u32[]{:S(2)}, u32[]{:S(2)}) async-start(f32[8,64,128]{2,1,0:T(8,128)} %bitcast.14), calls=%async_computation.3 | async-start | bytes 524288 | tf_op jit(solution)/shard_map/all_to_all | solution.py:108
  117.5 0.5 broadcast.178
  118.0 0.7 reduce.5
  118.7 0.1 reshape.264
  118.8 113.1 %all-reduce.2.cloned.1.call-done = f32[1024,128]{1,0:T(8,128)} async-done(((f32[1024,128]{1,0:T(8,128)}), f32[1024,128]{1,0:T(8,128)}) %all-reduce.2.cloned.1.call-update) | async-done | bytes 524304 | tf_op jit(solution)/shard_map/psum | solution.py:113
  231.9 2.1 multiply_subtract_fusion
  234.0 3.2 %scatter_custom_fusion.3 = f32[256,128]{1,0:T(8,128)S(1)} fusion(s32[512]{0:T(512)S(1)} %reshape.264, f32[512,128]{1,0:T(8,128)S(1)} %bitcast.31, f32[]{:T(128)} %constant.20.clone.1), kind=kCustom, calls=%fused_computation.44 | custom fusion | flops 65536 | bytes 131076 | tf_op jit(solution)/shard_map/scatter-add | solution.py:109
  237.3 0.7 multiply_subtract_fusion.1
  (36 shorter events, 0.3 us)
Async XLA Ops:
  7.2 75.9 %copy-start = (bf16[1024,256]{1,0:T(8,128)(2,1)S(1)}, bf16[1024,256]{1,0:T(8,128)(2,1)}, u32[]{:S(2)}) copy-start(bf16[1024,256]{1,0:T(8,128)(2,1)} %param.18) | copy-start | bytes 1572868
  7.2 12.4 %copy-start.7 = (s32[1,1,1024]{2,1,0:T(1,128)S(1)}, s32[1,1,1024]{2,1,0:T(1,128)}, u32[]{:S(2)}) copy-start(s32[1,1,1024]{2,1,0:T(1,128)} %param.16) | copy-start | bytes 12292
  7.2 18.9 %copy-start.2 = (f32[256,128]{1,0:T(8,128)S(1)}, f32[256,128]{1,0:T(8,128)}, u32[]{:S(2)}) copy-start(f32[256,128]{1,0:T(8,128)} %param.24) | copy-start | bytes 393220
  12.3 13.7 %all-to-all-start = ((s32[8,1,64]{2,1,0:T(1,128)}), s32[8,1,64]{2,1,0:T(1,128)S(1)}, u32[]{:S(2)}, u32[]{:S(2)}) async-start(s32[8,1,64]{2,1,0:T(1,128)} %all_to_all.14), calls=%async_computation | async-start | bytes 8192 | tf_op jit(solution)/shard_map/all_to_all | solution.py:64
  26.1 5.1 %copy-start.9 = (s32[1,1,2048]{2,1,0:T(1,128)S(1)}, s32[1,1,2048]{2,1,0:T(1,128)}, u32[]{:S(2)}) copy-start(s32[1,1,2048]{2,1,0:T(1,128)} %param.15) | copy-start | bytes 24580
  27.8 11.6 %all-to-all-start.1 = ((f32[8,64,128]{2,1,0:T(8,128)}), f32[8,64,128]{2,1,0:T(8,128)S(1)}, u32[]{:S(2)}, u32[]{:S(2)}) async-start(f32[8,64,128]{2,1,0:T(8,128)} %bitcast.10), calls=%async_computation.1 | async-start | bytes 524288 | tf_op jit(solution)/shard_map/all_to_all | solution.py:66
  31.2 31.0 %reduce-scatter.2.cloned.1.call-start = ((), (), s32[]{:S(2)}) async-start(), calls=%async_computation.4 | async-start | bytes 655360 | tf_op jit(solution)/shard_map/reduce_scatter | solution.py:83
  41.8 2.3 copy-start.1
  41.9 38.7 %all-gather.3.cloned.1.call-start = ((), (), s32[]{:S(2)}) async-start(), calls=%async_computation.5 | async-start | bytes 1310720 | tf_op jit(solution)/shard_map/all_gather | solution.py:80
  42.6 189.3 %all-reduce.2.cloned.1.call-start = ((), (), s32[]{:S(2)}) async-start(), calls=%async_computation.6 | async-start | bytes 1048576 | tf_op jit(solution)/shard_map/psum | solution.py:113
  44.1 3.7 %copy-start.8 = (f32[128]{0:T(128)S(1)}, f32[128]{0:T(128)}, u32[]{:S(2)}) copy-start(f32[128]{0:T(128)} %param.20) | copy-start | bytes 1540
  44.1 8.8 %copy-start.6 = (bf16[128,256]{1,0:T(8,128)(2,1)S(1)}, bf16[128,256]{1,0:T(8,128)(2,1)}, u32[]{:S(2)}) copy-start(bf16[128,256]{1,0:T(8,128)(2,1)} %param.21) | copy-start | bytes 196612
  85.1 1.0 copy-start.3
  87.3 13.7 %slice-start = ((f32[256,1024]{1,0:T(8,128)}), f32[256,128]{1,0:T(8,128)S(1)}, s32[]{:S(2)}) async-start(f32[256,1024]{1,0:T(8,128)} %copy-done.3), calls=%async_computation.7 | async-start | bytes 262144 | tf_op jit(solution)/shard_map/slice | solution.py:100
  108.4 123.5 %copy-start.4 = (f32[1024,128]{1,0:T(8,128)S(1)}, f32[1024,128]{1,0:T(8,128)}, u32[]{:S(2)}) copy-start(f32[1024,128]{1,0:T(8,128)} %param.23) | copy-start | bytes 1572868
  112.0 122.0 %all-to-all-start.2 = ((f32[8,64,128]{2,1,0:T(8,128)}), f32[8,64,128]{2,1,0:T(8,128)S(1)}, u32[]{:S(2)}, u32[]{:S(2)}) async-start(f32[8,64,128]{2,1,0:T(8,128)} %bitcast.14), calls=%async_computation.3 | async-start | bytes 524288 | tf_op jit(solution)/shard_map/all_to_all | solution.py:108
  118.8 118.5 %copy-start.5 = (f32[256,128]{1,0:T(8,128)S(1)}, f32[256,128]{1,0:T(8,128)}, u32[]{:S(2)}) copy-start(f32[256,128]{1,0:T(8,128)} %param.25) | copy-start | bytes 393220
Sparse Core Ops, SparseCore 0:
  42.0 20.1 reduce-scatter.1
  63.8 16.7 all-gather.2
  101.1 130.7 all-reduce.1
where the time goes:
time: 245 us
  waiting for transfers between devices  146 us (60%)
  other arithmetic  22.2 us (9%)
  blocking collectives  18.3 us (7%)
  local copies, waits for them, and re-layouts  16.7 us (7%)
  starting transfers between devices  16.4 us (7%)
  between operations  14 us (6%)
  matrix products  10.9 us (4%)
    psum x1, waiting for transfers between devices, per_device(): hot_grad = lax.psum(hot_part, ('dp', 'mp'))  113 us
    all_gather x1, waiting for transfers between devices, per_device(): full_in = lax.all_gather(weight_in, 'mp', axis=1, tiled=True)  17.5 us
    scatter-add x1, other arithmetic, per_device(): jax.ops.segment_sum(input_grad[:, :hot_cols].reshape(share_rows * fields,...  12.6 us
    all_gather x1, blocking collectives, per_device(): lax.all_gather(input_grad[:, hot_cols:], 'mp', axis=0, tiled=True)  7.36 us
    all_to_all x1, starting transfers between devices, per_device(): lax.all_to_all(requests, 'dp', split_axis=0, concat_axis=0, tiled=True)  7.31 us
    all_to_all x1, waiting for transfers between devices, per_device(): lax.all_to_all(requests, 'dp', split_axis=0, concat_axis=0, tiled=True)  5.84 us
    all_gather x1, blocking collectives, per_device(): full_out = lax.all_gather(weight_out, 'mp', axis=0, tiled=True)  5.83 us
    all_to_all x1, starting transfers between devices, per_device(): lax.all_to_all(outgoing, 'dp', split_axis=0, concat_axis=0, tiled=True)  5.52 us
  transfers between devices with their start and end apart: 6, of which 5 were waited for; matrix products, arithmetic and copies ran while one was open for 7% of the time, Pallas kernels for 0%

commit v1 on v0

v1 whole, which is shorter than its diff:
```python
import jax
import jax.numpy as jnp
from jax import lax
from jax.experimental import pallas as pl
from jax.experimental.pallas import tpu as pltpu
from jax.sharding import PartitionSpec as P

STEP_SIZE = 0.5
F32 = jnp.float32
BF16 = jnp.bfloat16
I32 = jnp.int32


def adagrad(table_rows, accum_rows, grad_rows):
    accum_new = accum_rows + grad_rows * grad_rows
    return (table_rows - STEP_SIZE * grad_rows / jnp.sqrt(accum_new), accum_new)


def loop(count, body, init):
    if count <= 16:
        for i in range(count):
            init = body(i, init)
        return init
    return lax.fori_loop(0, count, body, init)


def hi_lo(x):
    hi = x.astype(BF16)
    lo = (x - hi.astype(F32)).astype(BF16)
    return jnp.concatenate([hi, lo], axis=1)


def sum_halves(x):
    half = x.shape[1] // 2
    return x[:, :half] + x[:, half:]


def dot(a, b, dims=(((1,), (0,)), ((), ()))):
    return lax.dot_general(a, b, dims, preferred_element_type=F32)


NT = (((1,), (1,)), ((), ()))


def iota(shape, dim, dtype=I32):
    r = lax.broadcasted_iota(I32, shape, dim)
    return r if dtype == I32 else r.astype(dtype)


VM = pl.BlockSpec(memory_space=pltpu.VMEM)


def call(body, outs, ins, scratch=(), late=()):
    avals = [
        pltpu.VMEM(shape, dtype) if stay else jax.ShapeDtypeStruct(shape, dtype)
        for shape, dtype, stay in outs
    ]
    return pl.pallas_call(
        body,
        out_shape=avals,
        in_specs=[VM] * len(ins),
        out_specs=[VM] * len(outs),
        scratch_shapes=scratch,
        compiler_params=pltpu.CompilerParams(vmem_limit_bytes=16 * 1024 * 1024),
    )(
        *[
            pltpu.with_memory_space_constraint(x, pltpu.HBM if i in late else pltpu.VMEM)
            for i, x in enumerate(ins)
        ]
    )


def column(row):
    return jnp.broadcast_to(row, (8, row.shape[1])).T[:, 0:1]


def cast_kernel(table_ref, out_ref):
    out_ref[...] = table_ref[...].astype(BF16)


def spread_kernel(table_ref, out_ref):
    table = table_ref[...].astype(BF16)
    for o in range(out_ref.shape[0]):
        out_ref[o] = table


def pack_rows(d_in, out_width, hidden, emb, item_rows):
    starts = [0, d_in, d_in + out_width // emb * hidden]
    starts.append(starts[-1] + -(-item_rows // 16) * 16)
    starts.append(starts[-1] + 16)
    return starts + [starts[-1] + 16]


def prep_kernel(at, w_ref, v_ref, items_ref, sizes_ref, bias_ref, out_ref):
    hidden, width = v_ref.shape
    emb = out_ref.shape[1]
    out_ref[at[0] : at[1], :] = w_ref[...]
    for j in range(width // emb):
        out_ref[at[1] + j * hidden : at[1] + (j + 1) * hidden, :] = v_ref[
            :, j * emb : (j + 1) * emb
        ]

    def padded(x, rows):
        if x.shape[0] == rows:
            return x
        return jnp.concatenate([x, jnp.zeros((rows - x.shape[0], emb), F32)], axis=0)

    items = items_ref[...].astype(F32)
    out_ref[at[2] : at[3], :] = padded(items, at[3] - at[2]).astype(BF16)
    out_ref[at[3] : at[4], :] = padded(sizes_ref[...].astype(F32), 16).astype(BF16)
    bias = bias_ref[...]
    hi = bias.astype(BF16).astype(F32)
    mid = (bias - hi).astype(BF16).astype(F32)
    low = bias - hi - mid
    out_ref[at[4] : at[5], :] = padded(jnp.concatenate([hi, mid, low], axis=0), 16).astype(BF16)


def local_kernel(
    mp_count, slots, share, fields, map_ref, ids_ref, hot_ids_ref, hot_ref, pos_ref, rows_ref
):
    touch = ids_ref.shape[1]
    map_rows, lanes = map_ref.shape
    ids_col = column(ids_ref[...])
    in_row = (iota((touch, map_rows), 1) == ids_col // lanes).astype(F32)
    picked = lax.dot_general(
        in_row, map_ref[...].astype(F32), (((1,), (0,)), ((), ())),
        precision=lax.Precision.HIGHEST, preferred_element_type=F32,
    )
    in_lane = iota((touch, lanes), 1) == ids_col % lanes
    stored = jnp.sum(jnp.where(in_lane, picked, 0.0), axis=1, keepdims=True).astype(I32)
    stored = jnp.broadcast_to(stored, (touch, lanes))
    pos_ref[...] = stored // (mp_count * slots) * slots + stored % slots
    hot_rows, emb = hot_ref.shape
    hot = hot_ref[...].astype(BF16)
    my = lax.axis_index("mp")
    lane = iota((share, hot_rows), 1)
    for f in range(fields):
        mine = hot_ids_ref[f : f + 1, pl.ds(pl.multiple_of(my * share, share), share)]
        hit = (lane == column(mine)).astype(F32).astype(BF16)
        rows_ref[:, f * emb : (f + 1) * emb] = dot(hit, hot).astype(BF16)


def count_kernel(
    share, touch, at, item_rows, count_rows, p0, p1, p2, p3, cnt_ref, cntt_ref,
    items_ref, starts_ref, ends_ref, acc_ref,
):
    lanes = p0.shape[1]
    my = lax.axis_index("mp")
    per = share // lanes
    step = 2
    chunk = step * lanes
    sub_t = iota((touch, lanes), 0, F32)
    sub_i = iota((chunk, share), 0, F32)
    upto = (iota((lanes, lanes), 0) <= iota((lanes, lanes), 1)).astype(F32).astype(BF16)
    bounds = []
    for k, pack in enumerate((p0, p1, p2, p3)):
        sizes = pack[at[3] : at[4], :]
        ends = dot(sizes, upto)[:count_rows]
        sizes = sizes.astype(F32)[:count_rows]
        totals = jnp.broadcast_to(jnp.sum(sizes, axis=1, keepdims=True), ends.shape)
        row = iota(ends.shape, 0)
        for r in range(count_rows - 1):
            ends = ends + jnp.where(row > r, totals[r : r + 1, :], 0.0)
        ends_ref[k] = ends
        starts_ref[k] = ends - sizes
        items_ref[k] = pack[at[2] : at[3], :].astype(F32)[:item_rows]

    def rows_of(ref, k):
        return jnp.concatenate([ref[k, pl.ds(my * per + j, 1), :] for j in range(per)], axis=1)

    for k in range(4):
        starts = rows_of(starts_ref, k)
        ends = rows_of(ends_ref, k)
        low = jnp.min(starts).astype(I32)
        high = jnp.max(ends).astype(I32)
        bounds.append((starts, ends, low // chunk, (high + chunk - 1) // chunk))
    for k, (starts, ends, first, last) in enumerate(bounds):
        acc_ref[...] = jnp.zeros_like(acc_ref)

        def body(c, carry):
            pick = jnp.concatenate(
                [
                    (sub_t == items_ref[k, pl.ds(c * step + j, 1), :]).astype(F32).astype(BF16)
                    for j in range(step)
                ],
                axis=1,
            )
            pos = sub_i + (c * chunk).astype(F32)
            memb = ((pos >= starts) & (pos < ends)).astype(F32).astype(BF16)
            acc_ref[...] += dot(pick, memb)
            return carry

        lax.fori_loop(first, last, body, 0)
        counts_t = acc_ref[...]
        cntt_ref[k * touch : (k + 1) * touch, :] = counts_t.astype(BF16)
        cnt_ref[:, k * touch : (k + 1) * touch] = counts_t.T.astype(BF16)


def pre_kernel(
    share, at, hidden, p0, p1, p2, p3, grads_ref, rows_ref, wt_ref, tail_ref, pre_ref, back_ref
):
    my = lax.axis_index("mp")
    emb = p0.shape[1]
    hot_cols = rows_ref.shape[1]
    grads = grads_ref[pl.ds(pl.multiple_of(my * share, share), share), :]
    rows = rows_ref[...]
    for k, p in enumerate((p0, p1, p2, p3)):
        cols = slice(k * hidden, (k + 1) * hidden)
        bias = jnp.sum(p[at[4] : at[5], :].astype(F32), axis=0, keepdims=True)
        pre_ref[:, cols] = dot(rows, p[:hot_cols, :]) + bias
        back = jnp.zeros((share, hidden), F32)
        for j in range(grads.shape[1] // emb):
            piece = p[at[1] + j * hidden : at[1] + (j + 1) * hidden, :]
            back = back + dot(grads[:, j * emb : (j + 1) * emb], piece, NT)
        back_ref[:, cols] = back
        tail_ref[:, cols] = p[hot_cols : at[1], :]
        wt_ref[cols, :] = p[: at[1], :].astype(F32).T.astype(BF16)


def fetch_kernel(pos_ref, table_ref, out_ref):
    owners, slots, _ = table_ref.shape

    def body(o, acc):
        return acc + dot(hits(pos_ref, o * slots, slots), table_ref[o])

    out_ref[...] = loop(owners, body, jnp.zeros(out_ref.shape, F32)).astype(BF16)


def fetch_near_kernel(pos_ref, *refs):
    out_ref = refs[-1]
    slots = refs[0].shape[0]
    my = lax.axis_index("dp")
    acc = jnp.zeros(out_ref.shape, F32)
    for k, table in enumerate(refs[:-1]):
        acc = acc + dot(hits(pos_ref, (my ^ k) * slots, slots), table[...])
    out_ref[...] = acc.astype(BF16)


def hits(pos_ref, first, slots):
    rel = pos_ref[...] - first
    lane = iota(rel.shape, 1)
    lanes = rel.shape[1]
    return jnp.concatenate(
        [(lane + j * lanes == rel).astype(F32).astype(BF16) for j in range(slots // lanes)], axis=1
    )


def onehot_kernel(share, fields, slots, cap, ids_ref, pos_ref, out_ref, q_ref, srow_ref):
    my = lax.axis_index("mp")
    sub = iota((out_ref.shape[0], share), 0)
    for f in range(fields):
        mine = ids_ref[f : f + 1, pl.ds(pl.multiple_of(my * share, share), share)]
        out_ref[:, f * share : (f + 1) * share] = (sub == mine).astype(F32).astype(BF16)
    pos = pos_ref[...]
    touch, lanes = pos.shape
    row = pos.T[0:1, :]
    owner = row // slots
    before = iota((touch, touch), 0) < iota((touch, touch), 1)
    rank = jnp.sum(
        ((pos[:, 0:1] // slots == owner) & before).astype(F32), axis=0, keepdims=True
    )
    bucket = owner.astype(F32) * float(cap) + rank
    q_ref[...] = (iota(q_ref.shape, 0, F32) == bucket).astype(F32).astype(BF16)
    at_rank = (iota((touch, lanes), 1, F32) == column(rank)).astype(F32)
    mine = jnp.where(
        iota((srow_ref.shape[0], touch), 0) // 8 == owner, (row % slots).astype(F32), 0.0
    )
    srow_ref[...] = lax.dot_general(
        mine, at_rank, (((1,), (0,)), ((), ())),
        precision=lax.Precision.HIGHEST, preferred_element_type=F32,
    )


def main_kernel(
    fields, cnt_ref, f0, f1, f2, f3, pre_ref, back_ref, tail_ref, wt_ref, oht_ref,
    ig_ref, bag_ref, send_ref,
):
    touch, emb = f0.shape
    share = cnt_ref.shape[0]
    core = lax.axis_index("mp") % 2
    pooled = jnp.zeros((share, emb), F32)
    for k, f in enumerate((f0, f1, f2, f3)):
        pooled = pooled + dot(cnt_ref[:, k * touch : (k + 1) * touch], f[...])
    pre = pre_ref[...] + dot(pooled.astype(BF16), tail_ref[...])
    sig = jax.nn.sigmoid(pre)
    hidden = (back_ref[...] * sig * (1.0 + pre * (1.0 - sig))).astype(BF16)
    grad = dot(hidden, wt_ref[...])
    for f in range(fields):
        ig_ref[f * share : (f + 1) * share, :] = hi_lo(grad[:, f * emb : (f + 1) * emb])
    bag_ref[...] = hi_lo(grad[:, fields * emb :])
    half = send_ref.shape[0]
    first = pl.multiple_of((1 - core) * half, half)
    send_ref[...] = sum_halves(dot(oht_ref[pl.ds(first, half), :], ig_ref[...]))


def keep_kernel(oht_ref, ig_ref, bag_ref, cntt_ref, keep_ref, touch_send, touch_keep):
    half = keep_ref.shape[0]
    core = lax.axis_index("mp") % 2
    first = pl.multiple_of(core * half, half)
    keep_ref[...] = sum_halves(dot(oht_ref[pl.ds(first, half), :], ig_ref[...]))
    touch = touch_send.shape[1]
    for k in range(4):
        ref = touch_send if k % 2 else touch_keep
        rows = slice(k * touch, (k + 1) * touch)
        ref[k // 2] = sum_halves(dot(cntt_ref[rows, :], bag_ref[...]))


def add_kernel(a_ref, b_ref, out_ref):
    out_ref[...] = a_ref[...] + b_ref[...]


def pair_kernel(keep_ref, got_ref, mine_ref, give_ref):
    mine_ref[...] = keep_ref[0] + got_ref[0]
    give_ref[...] = keep_ref[1] + got_ref[1]


def fetch_kernel(pos_ref, table_ref, out_ref):
    owners, slots, emb = table_ref.shape
    touch, lanes = pos_ref.shape
    lane = iota((touch, lanes), 1)

    def body(o, acc):
        rel = pos_ref[...] - o * slots
        hit = jnp.concatenate(
            [
                (lane + j * lanes == rel).astype(F32).astype(BF16)
                for j in range(slots // lanes)
            ],
            axis=1,
        )
        return acc + dot(hit, table_ref[o])

    out_ref[...] = loop(owners, body, jnp.zeros((touch, emb), F32)).astype(BF16)


def reduce_kernel(parts_ref, out_ref):
    total = jnp.sum(parts_ref[...], axis=0, keepdims=True)
    out_ref[...] = jnp.broadcast_to(total, out_ref.shape)


def order_far_kernel(*refs):
    out_ref = refs[-1]
    far = lax.axis_index("dp") // 2
    for k, ref in enumerate(refs[:-1]):
        out_ref[far ^ k] = ref[0]


def order_near_kernel(*refs):
    out_ref = refs[-1]
    near = lax.axis_index("dp") % 2
    group = lax.axis_index("mp") // 2
    for k, ref in enumerate(refs[:-1]):
        for far in range(ref.shape[0]):
            out_ref[(far * 2 + (near ^ (k // 2))) * 2 + (group ^ (k % 2))] = ref[far]


def pack_kernel(cap, mine_ref, got_ref, q_ref, srow_ref, out_ref):
    owners = out_ref.shape[0]
    emb = out_ref.shape[2]
    rows = sum_halves(dot(q_ref[...], hi_lo(mine_ref[...] + got_ref[...])))
    out_ref[:, :cap, :] = rows.reshape(owners, cap, emb)
    out_ref[:, cap:, :] = srow_ref[...].reshape(owners, 8, emb)


def cold_kernel(cap, arrived_ref, table_ref, accum_ref, new_ref, acc_ref):
    slots, emb = table_ref.shape
    sub = iota((slots, cap), 0, F32)

    def body(d, acc):
        slot = arrived_ref[d, cap : cap + 1, :][:, :cap]
        hit = (sub == slot).astype(F32).astype(BF16)
        return acc + dot(hit, hi_lo(arrived_ref[d, :cap, :]))

    grad = sum_halves(loop(arrived_ref.shape[0], body, jnp.zeros((slots, 2 * emb), F32)))
    new_ref[...], acc_ref[...] = adagrad(table_ref[...], accum_ref[...], grad)


def final_kernel(mine_ref, theirs_ref, table_ref, accum_ref, new_ref, acc_ref):
    half = mine_ref.shape[0]
    core = lax.axis_index("mp") % 2
    for ref, c in ((mine_ref, core), (theirs_ref, 1 - core)):
        at = pl.ds(pl.multiple_of(c * half, half), half)
        new_ref[at, :], acc_ref[at, :] = adagrad(table_ref[at, :], accum_ref[at, :], ref[...])


def per_device(
    hot_ids,
    touched,
    cold_items,
    bag_counts,
    owner_map,
    grad_out,
    weight_in,
    bias_in,
    weight_out,
    hot_table,
    hot_accum,
    cold_table,
    cold_accum,
):
    dp_count = lax.axis_size("dp")
    mp_count = lax.axis_size("mp")
    slots, emb = cold_table.shape
    samples, fields = hot_ids.shape
    touch = touched.shape[2]
    items = cold_items.shape[2]
    d_in, hidden = weight_in.shape
    all_hidden = mp_count * hidden
    hot_rows = hot_table.shape[0]
    share = samples // mp_count
    cap = -(-(2 * touch // dp_count) // 8) * 8
    item_rows = items // emb
    count_rows = samples // emb
    both = ("dp", "mp")

    def swap(x, mask):
        return lax.ppermute(x, "mp", [(i, i ^ mask) for i in range(mp_count)])

    def far_swap(x, mask):
        return lax.ppermute(x, "dp", [(i, i ^ mask) for i in range(dp_count)])

    near = dp_count == 8 and mp_count == 4

    if near:
        (own,) = call(cast_kernel, [((slots, emb), BF16, True)], [cold_table], late=(0,))
        tables = [own] + [None] * 7
        for k in (4, 6, 2):
            tables[k] = far_swap(own, k)
        for k in (0, 4, 6, 2):
            tables[k + 1] = far_swap(tables[k], 1)
    else:
        (mine,) = call(
            spread_kernel, [((dp_count, slots, emb), BF16, False)], [cold_table], late=(0,)
        )
        tables = [lax.all_to_all(mine, "dp", split_axis=0, concat_axis=0, tiled=True)]

    at = pack_rows(d_in, weight_out.shape[1], hidden, emb, item_rows)
    (pack,) = call(
        lambda *r: prep_kernel(at, *r),
        [((at[-1], emb), BF16, True)],
        [
            weight_in,
            weight_out,
            cold_items.reshape(item_rows, emb),
            bag_counts.reshape(count_rows, emb),
            bias_in.reshape(1, hidden),
        ],
        late=range(5),
    )
    pack_far = swap(pack, 2)
    pack_near = swap(pack, 1)
    pack_cross = swap(pack_far, 1)
    packs = [pack, pack_near, pack_far, pack_cross]

    pos, rows = call(
        lambda *r: local_kernel(mp_count, slots, share, fields, *r),
        [((touch, emb), I32, True), ((share, fields * emb), BF16, True)],
        [owner_map.reshape(-1, emb), touched.reshape(1, touch), hot_ids.T, hot_table],
        late=range(4),
    )

    cnt, cntt = call(
        lambda *r: count_kernel(share, touch, at, item_rows, count_rows, *r),
        [
            ((share, mp_count * touch), BF16, True),
            ((mp_count * touch, share), BF16, True),
        ],
        packs,
        scratch=[
            pltpu.VMEM((mp_count, item_rows, emb), F32),
            pltpu.VMEM((mp_count, count_rows, emb), F32),
            pltpu.VMEM((mp_count, count_rows, emb), F32),
            pltpu.VMEM((touch, share), F32),
        ],
    )

    wt, tail, pre, back = call(
        lambda *r: pre_kernel(share, at, hidden, *r),
        [
            ((all_hidden, d_in), BF16, True),
            ((emb, all_hidden), BF16, True),
            ((share, all_hidden), F32, True),
            ((share, all_hidden), F32, True),
        ],
        [*packs, grad_out, rows],
        late=(4,),
    )

    (fetched,) = call(
        fetch_near_kernel if near else fetch_kernel,
        [((touch, emb), BF16, True)],
        [pos, *tables],
        late=() if near else (1,),
    )
    far = swap(fetched, 2)
    around = [fetched, swap(fetched, 1), far, swap(fetched, 3)]

    ids_late, _ = lax.optimization_barrier((hot_ids.T, fetched))
    oht, q_mat, slot_rows = call(
        lambda *r: onehot_kernel(share, fields, slots, cap, *r),
        [
            ((hot_rows, fields * share), BF16, True),
            ((dp_count * cap, touch), BF16, True),
            ((dp_count * 8, emb), F32, True),
        ],
        [ids_late, pos],
    )

    half_rows = hot_rows // 2
    ig, bag, hot_send = call(
        lambda *r: main_kernel(fields, *r),
        [
            ((fields * share, 2 * emb), BF16, True),
            ((share, 2 * emb), BF16, True),
            ((half_rows, emb), F32, True),
        ],
        [cnt, *around, pre, back, tail, wt, oht],
    )
    hot_got = swap(hot_send, 1)
    hot_keep, touch_send, touch_keep = call(
        keep_kernel,
        [
            ((half_rows, emb), F32, True),
            ((mp_count // 2, touch, emb), F32, True),
            ((mp_count // 2, touch, emb), F32, True),
        ],
        [oht, ig, bag, cntt],
    )

    group_size = dp_count * mp_count // 2
    rank_groups = [[g * 2 + c for g in range(group_size)] for c in range(2)]

    def exchange(x):
        return lax.all_to_all(
            x, both, split_axis=0, concat_axis=0, tiled=True, axis_index_groups=rank_groups
        )

    (chip,) = call(add_kernel, [((half_rows, emb), F32, True)], [hot_keep, hot_got])
    parts = exchange(chip.reshape(group_size, -1, emb))
    shard_shape = parts.shape if not near else (1, *parts.shape[1:])
    (shard,) = call(reduce_kernel, [(shard_shape, F32, True)], [parts])
    if near:
        pieces = [shard] + [far_swap(shard, 2 * k) for k in (1, 2, 3)]
        (line,) = call(order_far_kernel, [((4, *parts.shape[1:]), F32, True)], pieces)
        pieces = [line, swap(line, 2), far_swap(line, 1)]
        pieces.append(
            lax.ppermute(line, both, [(i, i ^ (mp_count + 2)) for i in range(dp_count * mp_count)])
        )
        (half,) = call(order_near_kernel, [(parts.shape, F32, True)], pieces)
        half = half.reshape(half_rows, emb)
    else:
        half = exchange(shard).reshape(half_rows, emb)
    other = swap(half, 1)
    hot_updated, hot_accum_new = call(
        final_kernel, [(hot_table.shape, F32, False)] * 2, [half, other, hot_table, hot_accum]
    )

    touch_got = swap(touch_send, 1)
    mine, give = call(pair_kernel, [((touch, emb), F32, True)] * 2, [touch_keep, touch_got])
    got = swap(give, 2)
    (outgoing,) = call(
        lambda *r: pack_kernel(cap, *r),
        [((dp_count, cap + 8, emb), F32, True)],
        [mine, got, q_mat, slot_rows],
    )
    arrived = lax.all_to_all(outgoing, "dp", split_axis=0, concat_axis=0, tiled=True)
    cold_updated, cold_accum_new = call(
        lambda *r: cold_kernel(cap, *r),
        [(cold_table.shape, F32, False)] * 2,
        [arrived, cold_table, cold_accum],
    )
    return (hot_updated, hot_accum_new, cold_updated, cold_accum_new)


def solution(mesh):
    return whole(mesh)


def whole(mesh):
    return jax.shard_map(
        per_device,
        mesh=mesh,
        in_specs=(
            P("dp", None),
            P("dp", "mp", None),
            P("dp", "mp", None),
            P("dp", "mp", None),
            P(),
            P("dp", None),
            P(None, "mp"),
            P("mp"),
            P("mp", None),
            P(),
            P(),
            P(("dp", "mp"), None),
            P(("dp", "mp"), None),
        ),
        out_specs=(P(), P(), P(("dp", "mp"), None), P(("dp", "mp"), None)),
        check_vma=False,
    )
```

time: 245 us -> 86.5 us (0.35)
  waiting for transfers between devices: 146 us -> 29.5 us
  other arithmetic: 22.2 us -> 0 us
  starting transfers between devices: 16.4 us -> 36.5 us
  Pallas kernels: 0 us -> 18.4 us
  blocking collectives: 18.3 us -> 0 us
  local copies, waits for them, and re-layouts: 16.7 us -> 0.78 us
  between operations: 14 us -> 0.84 us
  matrix products: 10.9 us -> 0 us
    psum x1 -> x0, waiting for transfers between devices: 113 us -> none  [per_device(): hot_grad = lax.psum(hot_part, ('dp', 'mp'))]
    ppermute x0 -> x23, waiting for transfers between devices: none -> 28.7 us  [the longest x11 15.6 us: swap(): return lax.ppermute(x, 'mp', [(i, i ^ mask) for i in range(mp_count)])]
    ppermute x0 -> x23, starting transfers between devices: none -> 25.3 us  [the longest x11 14.6 us: far_swap(): return lax.ppermute(x, 'dp', [(i, i ^ mask) for i in range(dp_count)])]
    pallas_call x0 -> x17, Pallas kernels: none -> 18.4 us  [call(): pl.pallas_call(body, out_shape=avals, in_specs=[VM] * len(ins), out_specs...]
    all_gather x3 -> x0, blocking collectives: 18.3 us -> none  [the longest x1 7.36 us: per_device(): lax.all_gather(input_grad[:, hot_cols:], 'mp', axis=0, tiled=True)]
    all_gather x1 -> x0, waiting for transfers between devices: 17.5 us -> none  [per_device(): full_in = lax.all_gather(weight_in, 'mp', axis=1, tiled=True)]
    scatter-add x2 -> x0, other arithmetic: 15.9 us -> none  [the longest x1 12.6 us: per_device(): jax.ops.segment_sum(input_grad[:, :hot_cols].reshape(share_rows * fields,...]
    dot_general x6 -> x0, matrix products: 10.9 us -> none  [the longest x1 2.62 us: per_device(): count_mat = jnp.dot(member, picks, preferred_element_type=jnp.float32)]
  transfers between devices with their start and end apart: 6 -> 25, of which waited for: 5 -> 14; matrix products, arithmetic and copies ran while one was open for 7% -> 0% of each run, Pallas kernels for 0% -> 16%
where the time goes in v1:
time: 86.5 us; the launch traced here: 86 us
  starting transfers between devices  36.5 us (42%)
  waiting for transfers between devices  29.5 us (34%)
  Pallas kernels  18.4 us (21%)
    pallas_call x17, Pallas kernels, call(): pl.pallas_call(body, out_shape=avals, in_specs=[VM] * len(ins), out_specs...  18.4 us
    ppermute x11, waiting for transfers between devices, swap(): return lax.ppermute(x, 'mp', [(i, i ^ mask) for i in range(mp_count)])  15.6 us
    ppermute x11, starting transfers between devices, far_swap(): return lax.ppermute(x, 'dp', [(i, i ^ mask) for i in range(dp_count)])  14.6 us
    ppermute x11, waiting for transfers between devices, far_swap(): return lax.ppermute(x, 'dp', [(i, i ^ mask) for i in range(dp_count)])  11.4 us
    ppermute x11, starting transfers between devices, swap(): return lax.ppermute(x, 'mp', [(i, i ^ mask) for i in range(mp_count)])  8.55 us
    all_to_all x1, starting transfers between devices, exchange(): lax.all_to_all(x, both, split_axis=0, concat_axis=0, tiled=True, axis_ind...  6.02 us
    all_to_all x1, starting transfers between devices, per_device(): lax.all_to_all(outgoing, 'dp', split_axis=0, concat_axis=0, tiled=True)  5.15 us
    ppermute x1, starting transfers between devices, per_device(): lax.ppermute(line, both, [(i, i ^ mp_count + 2) for i in range(dp_count *...  2.19 us
  transfers between devices with their start and end apart: 25, of which 14 were waited for; matrix products, arithmetic and copies ran while one was open for 0% of the time, Pallas kernels for 16%

profile of v1, /device:TPU:0, one launch (start us, length us, event | category | flops | bytes accessed | tf_op | source)
XLA Modules:
  0.0 86.0 jit_solution(17349884759200948292)
XLA Ops:
  0.6 1.0 %shard_map.160.r_0_ = bf16[1328,128]{1,0:T(8,128)(2,1)S(1)} custom-call(bf16[1024,128]{1,0:T(8,128)(2,1)} %r_0_.1, bf16[128,256]{1,0:T(8,128)(2,1)} %r_1_.2, s32[16,128]{1,0:T(8,128)} %bitcast.13, s32[8,128]{1,0:T(8,128)} %bitcast.14, f32[1,128]{1,0:T(1,128)} %bitcast.16), custom_call_target="tpu_custom_call" | custom-call | tf_op jit(solution)/shard_map/pallas_call | solution.py:58
  1.7 3.0 %collective-permute-start.8 = (bf16[1328,128]{1,0:T(8,128)(2,1)S(1)}, bf16[1328,128]{1,0:T(8,128)(2,1)S(1)}, u32[]{:S(2)}, u32[]{:S(2)}) collective-permute-start(bf16[1328,128]{1,0:T(8,128)(2,1)S(1)} %shard_map.160.r_0_), channel_id=1, source_target_pairs={{0,2},{1,3},{2,0},{3,1},{4,6},{5,7},{6,4},{7,5},{8,10},{9,11},{10,... | collective-permute-start | bytes 1019912 | tf_op jit(solution)/shard_map/ppermute | solution.py:417
  4.7 8.0 %collective-permute-done.8.r_2_ = bf16[1328,128]{1,0:T(8,128)(2,1)S(1)} collective-permute-done((bf16[1328,128]{1,0:T(8,128)(2,1)S(1)}, bf16[1328,128]{1,0:T(8,128)(2,1)S(1)}, u32[]{:S(2)}, u32[]{:S(2)}) %collective-permute-start.8) | collective-permute-done | bytes 340000 | tf_op jit(solution)/shard_map/ppermute | solution.py:417
  12.7 0.9 %shard_map.157.refs_0_ = bf16[256,128]{1,0:T(8,128)(2,1)S(1)} custom-call(f32[256,128]{1,0:T(8,128)} %r_1_.3), custom_call_target="tpu_custom_call" | custom-call | tf_op jit(solution)/shard_map/pallas_call | solution.py:58
  13.6 3.9 %collective-permute-start.5 = (bf16[256,128]{1,0:T(8,128)(2,1)S(1)}, bf16[256,128]{1,0:T(8,128)(2,1)S(1)}, u32[]{:S(2)}, u32[]{:S(2)}) collective-permute-start(bf16[256,128]{1,0:T(8,128)(2,1)S(1)} %shard_map.157.refs_0_), channel_id=1, source_target_pairs={{0,24},{4,28},{8,16},{12,20},{16,8},{20,12},{24,0},{28,4},{1,25},{... | collective-permute-start | bytes 196616 | tf_op jit(solution)/shard_map/ppermute | solution.py:420
  17.5 0.6 collective-permute-start.1
  18.1 2.3 %collective-permute-done.5.refs_6_ = bf16[256,128]{1,0:T(8,128)(2,1)S(1)} collective-permute-done((bf16[256,128]{1,0:T(8,128)(2,1)S(1)}, bf16[256,128]{1,0:T(8,128)(2,1)S(1)}, u32[]{:S(2)}, u32[]{:S(2)}) %collective-permute-start.5) | collective-permute-done | bytes 65568 | tf_op jit(solution)/shard_map/ppermute | solution.py:420
  20.4 1.5 %collective-permute-start = (bf16[256,128]{1,0:T(8,128)(2,1)S(1)}, bf16[256,128]{1,0:T(8,128)(2,1)S(1)}, u32[]{:S(2)}, u32[]{:S(2)}) collective-permute-start(bf16[256,128]{1,0:T(8,128)(2,1)S(1)} %shard_map.157.refs_0_), channel_id=1, source_target_pairs={{0,4},{4,0},{8,12},{12,8},{16,20},{20,16},{24,28},{28,24},{1,5},{5... | collective-permute-start | bytes 196616 | tf_op jit(solution)/shard_map/ppermute | solution.py:420
  21.9 1.6 %collective-permute-done.3.refs_4_ = bf16[256,128]{1,0:T(8,128)(2,1)S(1)} collective-permute-done((bf16[256,128]{1,0:T(8,128)(2,1)S(1)}, bf16[256,128]{1,0:T(8,128)(2,1)S(1)}, u32[]{:S(2)}, u32[]{:S(2)}) %collective-permute-start.3) | collective-permute-done | bytes 65568 | tf_op jit(solution)/shard_map/ppermute | solution.py:420
  23.6 1.5 %collective-permute-start.6 = (bf16[256,128]{1,0:T(8,128)(2,1)S(1)}, bf16[256,128]{1,0:T(8,128)(2,1)S(1)}, u32[]{:S(2)}, u32[]{:S(2)}) collective-permute-start(bf16[256,128]{1,0:T(8,128)(2,1)S(1)} %collective-permute-done.5.refs_6_), channel_id=1, source_target_pairs={{0,4},{4,0},{8,12},{12,8},{16,20},{20,16},{24,28},{28,24},{1,5},{5... | collective-permute-start | bytes 196616 | tf_op jit(solution)/shard_map/ppermute | solution.py:420
  25.1 0.5 collective-permute-start.4
  25.6 1.5 %collective-permute-start.2 = (bf16[256,128]{1,0:T(8,128)(2,1)S(1)}, bf16[256,128]{1,0:T(8,128)(2,1)S(1)}, u32[]{:S(2)}, u32[]{:S(2)}) collective-permute-start(bf16[256,128]{1,0:T(8,128)(2,1)S(1)} %collective-permute-done.1.refs_2_), channel_id=1, source_target_pairs={{0,4},{4,0},{8,12},{12,8},{16,20},{20,16},{24,28},{28,24},{1,5},{5... | collective-permute-start | bytes 196616 | tf_op jit(solution)/shard_map/ppermute | solution.py:420
  27.1 3.3 %shard_map.156 = (s32[256,128]{1,0:T(8,128)S(1)}, bf16[256,896]{1,0:T(8,128)(2,1)S(1)}) custom-call(s32[64,128]{1,0:T(8,128)} %bitcast.12, s32[1,256]{1,0:T(1,128)} %bitcast.15, s32[7,1024]{1,0:T(8,128)} %bitcast.10, f32[1024,128]{1,0:T(8,128)} %table_ref.3), custom_call_target="tpu_custom_call" | custom-call | tf_op jit(solution)/shard_map/pallas_call | solution.py:58
  30.5 0.1 collective-permute-done.2.refs_3_
  30.6 0.4 shard_map.158.r_1_
  31.0 0.4 collective-permute-start.12
  31.4 1.3 %collective-permute-start.11 = (bf16[256,128]{1,0:T(8,128)(2,1)S(1)}, bf16[256,128]{1,0:T(8,128)(2,1)S(1)}, u32[]{:S(2)}, u32[]{:S(2)}) collective-permute-start(bf16[256,128]{1,0:T(8,128)(2,1)S(1)} %shard_map.158.r_1_), channel_id=1, source_target_pairs={{0,2},{1,3},{2,0},{3,1},{4,6},{5,7},{6,4},{7,5},{8,10},{9,11},{10,... | collective-permute-start | bytes 196616 | tf_op jit(solution)/shard_map/ppermute | solution.py:417
  32.6 0.3 collective-permute-start.10
  32.9 0.8 copy-done.4
  33.7 1.7 %shard_map.159 = (bf16[1024,1792]{1,0:T(8,128)(2,1)S(1)}, bf16[512,256]{1,0:T(8,128)(2,1)S(1)}, f32[64,128]{1,0:T(8,128)S(1)}) custom-call(s32[7,1024]{1,0:T(8,128)S(1)} %bitcast.11, s32[256,128]{1,0:T(8,128)S(1)} %get-tuple-element.28.pos_ref.r_1_), custom_call_target="tpu_custom_call" | custom-call | tf_op jit(solution)/shard_map/pallas_call | solution.py:58
  35.5 2.7 %shard_map.161 = (bf16[256,1024]{1,0:T(8,128)(2,1)S(1)}, bf16[1024,256]{1,0:T(8,128)(2,1)S(1)}) custom-call(bf16[1328,128]{1,0:T(8,128)(2,1)S(1)} %shard_map.160.r_0_, bf16[1328,128]{1,0:T(8,128)(2,1)S(1)} %collective-permute-done.7.r_1_, bf16[1328,128]{1,0:T(8,128)(2,1)S(1)} %collective-permute-done.8.r_2_, bf16[1328,128]{1,0:T(8,128)(2,1)S(1)} %collective-permute-done.9.r_3_), custom_call_target="tpu_custom_call" | custom-call | tf_op jit(solution)/shard_map/pallas_call | solution.py:58
  38.2 1.9 %shard_map.162 = (bf16[512,1024]{1,0:T(8,128)(2,1)S(1)}, bf16[128,512]{1,0:T(8,128)(2,1)S(1)}, f32[256,512]{1,0:T(8,128)S(1)}, f32[256,512]{1,0:T(8,128)S(1)}) custom-call(bf16[1328,128]{1,0:T(8,128)(2,1)S(1)} %shard_map.160.r_0_, bf16[1328,128]{1,0:T(8,128)(2,1)S(1)} %collective-permute-done.7.r_1_, bf16[1328,128]{1,0:T(8,128)(2,1)S(1)} %collective-permute-done.8.r_2_, ...), custom_call_target="tpu_custom_call" | custom-call | tf_op jit(solution)/shard_map/pallas_call | solution.py:58
  40.1 1.5 %shard_map.163 = (bf16[1792,256]{1,0:T(8,128)(2,1)S(1)}, bf16[256,256]{1,0:T(8,128)(2,1)S(1)}, f32[512,128]{1,0:T(8,128)S(1)}) custom-call(bf16[256,1024]{1,0:T(8,128)(2,1)S(1)} %get-tuple-element.31.r_0_, bf16[256,128]{1,0:T(8,128)(2,1)S(1)} %shard_map.158.r_1_, bf16[256,128]{1,0:T(8,128)(2,1)S(1)} %collective-permute-done.10.r_2_, ...), custom_call_target="tpu_custom_call" | custom-call | tf_op jit(solution)/shard_map/pallas_call | solution.py:58
  41.6 0.7 collective-permute-start.13
  42.3 0.8 shard_map.164
  43.1 0.3 collective-permute-done.13.b_ref
  43.4 0.7 shard_map.165
  44.2 6.0 %all-to-all-start = ((f32[16,32,128]{2,1,0:T(8,128)}), f32[16,32,128]{2,1,0:T(8,128)S(1)}, u32[]{:S(2)}, u32[]{:S(2)}) async-start(f32[16,32,128]{2,1,0:T(8,128)} %bitcast.6), calls=%async_computation | async-start | bytes 524288 | tf_op jit(solution)/shard_map/all_to_all | solution.py:534
  50.2 0.1 collective-permute-start.21
  50.3 1.5 %collective-permute-done.21.got_ref = f32[2,256,128]{2,1,0:T(8,128)S(1)} collective-permute-done((f32[2,256,128]{2,1,0:T(8,128)S(1)}, f32[2,256,128]{2,1,0:T(8,128)S(1)}, u32[]{:S(2)}, u32[]{:S(2)}) %collective-permute-start.21) | collective-permute-done | bytes 262176 | tf_op jit(solution)/shard_map/ppermute | solution.py:417
  51.8 1.9 %collective-permute-start.22 = (f32[256,128]{1,0:T(8,128)S(1)}, f32[256,128]{1,0:T(8,128)S(1)}, u32[]{:S(2)}, u32[]{:S(2)}) collective-permute-start(f32[256,128]{1,0:T(8,128)S(1)} %get-tuple-element.47), channel_id=1, source_target_pairs={{0,2},{1,3},{2,0},{3,1},{4,6},{5,7},{6,4},{7,5},{8,10},{9,11},{10,... | collective-permute-start | bytes 393224 | tf_op jit(solution)/shard_map/ppermute | solution.py:417
  53.8 4.9 %collective-permute-done.22.r_1_ = f32[256,128]{1,0:T(8,128)S(1)} collective-permute-done((f32[256,128]{1,0:T(8,128)S(1)}, f32[256,128]{1,0:T(8,128)S(1)}, u32[]{:S(2)}, u32[]{:S(2)}) %collective-permute-start.22) | collective-permute-done | bytes 131104 | tf_op jit(solution)/shard_map/ppermute | solution.py:417
  58.6 1.0 %shard_map.171 = f32[8,72,128]{2,1,0:T(8,128)} custom-call(f32[256,128]{1,0:T(8,128)S(1)} %get-tuple-element.46.r_0_, f32[256,128]{1,0:T(8,128)S(1)} %collective-permute-done.22.r_1_, bf16[512,256]{1,0:T(8,128)(2,1)S(1)} %get-tuple-element.48.r_2_, f32[64,128]{1,0:T(8,128)S(1)} %get-tuple-element.49.r_3_), custom_call_target="tpu_custom_call" | custom-call | tf_op jit(solution)/shard_map/pallas_call | solution.py:58
  59.6 0.8 all-to-all-done.parts_ref
  60.4 5.2 %all-to-all-start.1 = ((f32[8,72,128]{2,1,0:T(8,128)}), f32[8,72,128]{2,1,0:T(8,128)S(1)}, u32[]{:S(2)}, u32[]{:S(2)}) async-start(f32[8,72,128]{2,1,0:T(8,128)} %shard_map.171), calls=%async_computation.1 | async-start | bytes 589824 | tf_op jit(solution)/shard_map/all_to_all | solution.py:566
  65.5 3.9 %collective-permute-start.16 = (f32[1,32,128]{2,1,0:T(8,128)S(1)}, f32[1,32,128]{2,1,0:T(8,128)S(1)}, u32[]{:S(2)}, u32[]{:S(2)}) collective-permute-start(f32[1,32,128]{2,1,0:T(8,128)S(1)} %shard_map.166.refs_0_), channel_id=1, source_target_pairs={{0,24},{4,28},{8,16},{12,20},{16,8},{20,12},{24,0},{28,4},{1,25},{... | collective-permute-start | bytes 49160 | tf_op jit(solution)/shard_map/ppermute | solution.py:420
  69.4 0.6 collective-permute-start.14
  70.1 4.7 %collective-permute-done.16.refs_3_ = f32[1,32,128]{2,1,0:T(8,128)S(1)} collective-permute-done((f32[1,32,128]{2,1,0:T(8,128)S(1)}, f32[1,32,128]{2,1,0:T(8,128)S(1)}, u32[]{:S(2)}, u32[]{:S(2)}) %collective-permute-start.16) | collective-permute-done | bytes 16416 | tf_op jit(solution)/shard_map/ppermute | solution.py:420
  74.8 1.4 %collective-permute-done.15.refs_2_ = f32[1,32,128]{2,1,0:T(8,128)S(1)} collective-permute-done((f32[1,32,128]{2,1,0:T(8,128)S(1)}, f32[1,32,128]{2,1,0:T(8,128)S(1)}, u32[]{:S(2)}, u32[]{:S(2)}) %collective-permute-start.15) | collective-permute-done | bytes 16416 | tf_op jit(solution)/shard_map/ppermute | solution.py:420
  76.2 2.2 %collective-permute-start.19 = (f32[4,32,128]{2,1,0:T(8,128)S(1)}, f32[4,32,128]{2,1,0:T(8,128)S(1)}, u32[]{:S(2)}, u32[]{:S(2)}) collective-permute-start(f32[4,32,128]{2,1,0:T(8,128)S(1)} %shard_map.167.refs_0_), channel_id=1, source_target_pairs={{0,6},{1,7},{2,4},{3,5},{4,2},{5,3},{6,0},{7,1},{8,14},{9,15},{10,... | collective-permute-start | bytes 196616 | tf_op jit(solution)/shard_map/ppermute | solution.py:547
  78.4 0.5 collective-permute-start.18
  78.9 0.8 collective-permute-start.17
  79.7 1.7 %collective-permute-done.19.refs_3_ = f32[4,32,128]{2,1,0:T(8,128)S(1)} collective-permute-done((f32[4,32,128]{2,1,0:T(8,128)S(1)}, f32[4,32,128]{2,1,0:T(8,128)S(1)}, u32[]{:S(2)}, u32[]{:S(2)}) %collective-permute-start.19) | collective-permute-done | bytes 65568 | tf_op jit(solution)/shard_map/ppermute | solution.py:547
  81.4 1.2 %collective-permute-done.18.refs_2_ = f32[4,32,128]{2,1,0:T(8,128)S(1)} collective-permute-done((f32[4,32,128]{2,1,0:T(8,128)S(1)}, f32[4,32,128]{2,1,0:T(8,128)S(1)}, u32[]{:S(2)}, u32[]{:S(2)}) %collective-permute-start.18) | collective-permute-done | bytes 65568 | tf_op jit(solution)/shard_map/ppermute | solution.py:420
  82.6 0.5 collective-permute-done.17.refs_1_
  83.3 1.1 %shard_map.172 = (f32[256,128]{1,0:T(8,128)}, f32[256,128]{1,0:T(8,128)}) custom-call(f32[8,72,128]{2,1,0:T(8,128)S(1)} %all-to-all-done.1.r_0_, f32[256,128]{1,0:T(8,128)S(1)} %copy-done.2, f32[256,128]{1,0:T(8,128)S(1)} %copy-done.3), custom_call_target="tpu_custom_call" | custom-call | tf_op jit(solution)/shard_map/pallas_call | solution.py:58
  84.4 0.4 collective-permute-done.20.theirs_ref
  84.8 1.2 %shard_map.169 = (f32[1024,128]{1,0:T(8,128)}, f32[1024,128]{1,0:T(8,128)}) custom-call(f32[512,128]{1,0:T(8,128)S(1)} %bitcast.9, f32[512,128]{1,0:T(8,128)S(1)} %collective-permute-done.20.theirs_ref, f32[1024,128]{1,0:T(8,128)S(1)} %copy-done, f32[1024,128]{1,0:T(8,128)S(1)} %copy-done.1), custom_call_target="tpu_custom_call" | custom-call | tf_op jit(solution)/shard_map/pallas_call | solution.py:58
  (29 shorter events, 0.2 us)
Async XLA Ops:
  1.7 11.0 %collective-permute-start.8 = (bf16[1328,128]{1,0:T(8,128)(2,1)S(1)}, bf16[1328,128]{1,0:T(8,128)(2,1)S(1)}, u32[]{:S(2)}, u32[]{:S(2)}) collective-permute-start(bf16[1328,128]{1,0:T(8,128)(2,1)S(1)} %shard_map.160.r_0_), channel_id=1, source_target_pairs={{0,2},{1,3},{2,0},{3,1},{4,6},{5,7},{6,4},{7,5},{8,10},{9,11},{10,... | collective-permute-start | bytes 1019912 | tf_op jit(solution)/shard_map/ppermute | solution.py:417
  4.7 30.7 %collective-permute-start.7 = (bf16[1328,128]{1,0:T(8,128)(2,1)S(1)}, bf16[1328,128]{1,0:T(8,128)(2,1)S(1)}, u32[]{:S(2)}, u32[]{:S(2)}) collective-permute-start(bf16[1328,128]{1,0:T(8,128)(2,1)S(1)} %shard_map.160.r_0_), channel_id=1, source_target_pairs={{0,1},{1,0},{2,3},{3,2},{4,5},{5,4},{6,7},{7,6},{8,9},{9,8},{10,11... | collective-permute-start | bytes 1019912 | tf_op jit(solution)/shard_map/ppermute | solution.py:417
  12.7 22.8 %collective-permute-start.9 = (bf16[1328,128]{1,0:T(8,128)(2,1)S(1)}, bf16[1328,128]{1,0:T(8,128)(2,1)S(1)}, u32[]{:S(2)}, u32[]{:S(2)}) collective-permute-start(bf16[1328,128]{1,0:T(8,128)(2,1)S(1)} %collective-permute-done.8.r_2_), channel_id=1, source_target_pairs={{0,1},{1,0},{2,3},{3,2},{4,5},{5,4},{6,7},{7,6},{8,9},{9,8},{10,11... | collective-permute-start | bytes 1019912 | tf_op jit(solution)/shard_map/ppermute | solution.py:417
  13.6 6.8 %collective-permute-start.5 = (bf16[256,128]{1,0:T(8,128)(2,1)S(1)}, bf16[256,128]{1,0:T(8,128)(2,1)S(1)}, u32[]{:S(2)}, u32[]{:S(2)}) collective-permute-start(bf16[256,128]{1,0:T(8,128)(2,1)S(1)} %shard_map.157.refs_0_), channel_id=1, source_target_pairs={{0,24},{4,28},{8,16},{12,20},{16,8},{20,12},{24,0},{28,4},{1,25},{... | collective-permute-start | bytes 196616 | tf_op jit(solution)/shard_map/ppermute | solution.py:420
  17.5 6.1 %collective-permute-start.3 = (bf16[256,128]{1,0:T(8,128)(2,1)S(1)}, bf16[256,128]{1,0:T(8,128)(2,1)S(1)}, u32[]{:S(2)}, u32[]{:S(2)}) collective-permute-start(bf16[256,128]{1,0:T(8,128)(2,1)S(1)} %shard_map.157.refs_0_), channel_id=1, source_target_pairs={{0,16},{4,20},{8,24},{12,28},{16,0},{20,4},{24,8},{28,12},{1,17},{... | collective-permute-start | bytes 196616 | tf_op jit(solution)/shard_map/ppermute | solution.py:420
  17.5 7.6 %collective-permute-start.1 = (bf16[256,128]{1,0:T(8,128)(2,1)S(1)}, bf16[256,128]{1,0:T(8,128)(2,1)S(1)}, u32[]{:S(2)}, u32[]{:S(2)}) collective-permute-start(bf16[256,128]{1,0:T(8,128)(2,1)S(1)} %shard_map.157.refs_0_), channel_id=1, source_target_pairs={{0,8},{4,12},{8,0},{12,4},{16,24},{20,28},{24,16},{28,20},{1,9},{5... | collective-permute-start | bytes 196616 | tf_op jit(solution)/shard_map/ppermute | solution.py:420
  20.4 5.2 %collective-permute-start = (bf16[256,128]{1,0:T(8,128)(2,1)S(1)}, bf16[256,128]{1,0:T(8,128)(2,1)S(1)}, u32[]{:S(2)}, u32[]{:S(2)}) collective-permute-start(bf16[256,128]{1,0:T(8,128)(2,1)S(1)} %shard_map.157.refs_0_), channel_id=1, source_target_pairs={{0,4},{4,0},{8,12},{12,8},{16,20},{20,16},{24,28},{28,24},{1,5},{5... | collective-permute-start | bytes 196616 | tf_op jit(solution)/shard_map/ppermute | solution.py:420
  23.6 6.9 %collective-permute-start.6 = (bf16[256,128]{1,0:T(8,128)(2,1)S(1)}, bf16[256,128]{1,0:T(8,128)(2,1)S(1)}, u32[]{:S(2)}, u32[]{:S(2)}) collective-permute-start(bf16[256,128]{1,0:T(8,128)(2,1)S(1)} %collective-permute-done.5.refs_6_), channel_id=1, source_target_pairs={{0,4},{4,0},{8,12},{12,8},{16,20},{20,16},{24,28},{28,24},{1,5},{5... | collective-permute-start | bytes 196616 | tf_op jit(solution)/shard_map/ppermute | solution.py:420
  25.1 5.3 %collective-permute-start.4 = (bf16[256,128]{1,0:T(8,128)(2,1)S(1)}, bf16[256,128]{1,0:T(8,128)(2,1)S(1)}, u32[]{:S(2)}, u32[]{:S(2)}) collective-permute-start(bf16[256,128]{1,0:T(8,128)(2,1)S(1)} %collective-permute-done.3.refs_4_), channel_id=1, source_target_pairs={{0,4},{4,0},{8,12},{12,8},{16,20},{20,16},{24,28},{28,24},{1,5},{5... | collective-permute-start | bytes 196616 | tf_op jit(solution)/shard_map/ppermute | solution.py:420
  25.6 5.0 %collective-permute-start.2 = (bf16[256,128]{1,0:T(8,128)(2,1)S(1)}, bf16[256,128]{1,0:T(8,128)(2,1)S(1)}, u32[]{:S(2)}, u32[]{:S(2)}) collective-permute-start(bf16[256,128]{1,0:T(8,128)(2,1)S(1)} %collective-permute-done.1.refs_2_), channel_id=1, source_target_pairs={{0,4},{4,0},{8,12},{12,8},{16,20},{20,16},{24,28},{28,24},{1,5},{5... | collective-permute-start | bytes 196616 | tf_op jit(solution)/shard_map/ppermute | solution.py:420
  31.0 9.1 %collective-permute-start.12 = (bf16[256,128]{1,0:T(8,128)(2,1)S(1)}, bf16[256,128]{1,0:T(8,128)(2,1)S(1)}, u32[]{:S(2)}, u32[]{:S(2)}) collective-permute-start(bf16[256,128]{1,0:T(8,128)(2,1)S(1)} %shard_map.158.r_1_), channel_id=1, source_target_pairs={{0,3},{1,2},{2,1},{3,0},{4,7},{5,6},{6,5},{7,4},{8,11},{9,10},{10,... | collective-permute-start | bytes 196616 | tf_op jit(solution)/shard_map/ppermute | solution.py:417
  31.4 8.7 %collective-permute-start.11 = (bf16[256,128]{1,0:T(8,128)(2,1)S(1)}, bf16[256,128]{1,0:T(8,128)(2,1)S(1)}, u32[]{:S(2)}, u32[]{:S(2)}) collective-permute-start(bf16[256,128]{1,0:T(8,128)(2,1)S(1)} %shard_map.158.r_1_), channel_id=1, source_target_pairs={{0,2},{1,3},{2,0},{3,1},{4,6},{5,7},{6,4},{7,5},{8,10},{9,11},{10,... | collective-permute-start | bytes 196616 | tf_op jit(solution)/shard_map/ppermute | solution.py:417
  32.6 7.5 %collective-permute-start.10 = (bf16[256,128]{1,0:T(8,128)(2,1)S(1)}, bf16[256,128]{1,0:T(8,128)(2,1)S(1)}, u32[]{:S(2)}, u32[]{:S(2)}) collective-permute-start(bf16[256,128]{1,0:T(8,128)(2,1)S(1)} %shard_map.158.r_1_), channel_id=1, source_target_pairs={{0,1},{1,0},{2,3},{3,2},{4,5},{5,4},{6,7},{7,6},{8,9},{9,8},{10,11... | collective-permute-start | bytes 196616 | tf_op jit(solution)/shard_map/ppermute | solution.py:417
  32.9 0.8 copy-start.4
  41.6 1.8 %collective-permute-start.13 = (f32[512,128]{1,0:T(8,128)S(1)}, f32[512,128]{1,0:T(8,128)S(1)}, u32[]{:S(2)}, u32[]{:S(2)}) collective-permute-start(f32[512,128]{1,0:T(8,128)S(1)} %get-tuple-element.41), channel_id=1, source_target_pairs={{0,1},{1,0},{2,3},{3,2},{4,5},{5,4},{6,7},{7,6},{8,9},{9,8},{10,11... | collective-permute-start | bytes 786440 | tf_op jit(solution)/shard_map/ppermute | solution.py:417
  42.3 41.0 %copy-start.2 = (f32[256,128]{1,0:T(8,128)S(1)}, f32[256,128]{1,0:T(8,128)}, u32[]{:S(2)}) copy-start(f32[256,128]{1,0:T(8,128)} %r_1_.3) | copy-start | bytes 393220
  42.3 41.0 %copy-start.3 = (f32[256,128]{1,0:T(8,128)S(1)}, f32[256,128]{1,0:T(8,128)}, u32[]{:S(2)}) copy-start(f32[256,128]{1,0:T(8,128)} %r_2_.1) | copy-start | bytes 393220
  43.1 41.7 %copy-start = (f32[1024,128]{1,0:T(8,128)S(1)}, f32[1024,128]{1,0:T(8,128)}, u32[]{:S(2)}) copy-start(f32[1024,128]{1,0:T(8,128)} %table_ref.3) | copy-start | bytes 1572868
  43.1 41.7 %copy-start.1 = (f32[1024,128]{1,0:T(8,128)S(1)}, f32[1024,128]{1,0:T(8,128)}, u32[]{:S(2)}) copy-start(f32[1024,128]{1,0:T(8,128)} %accum_ref.1) | copy-start | bytes 1572868
  44.2 16.2 %all-to-all-start = ((f32[16,32,128]{2,1,0:T(8,128)}), f32[16,32,128]{2,1,0:T(8,128)S(1)}, u32[]{:S(2)}, u32[]{:S(2)}) async-start(f32[16,32,128]{2,1,0:T(8,128)} %bitcast.6), calls=%async_computation | async-start | bytes 524288 | tf_op jit(solution)/shard_map/all_to_all | solution.py:534
  50.2 1.6 %collective-permute-start.21 = (f32[2,256,128]{2,1,0:T(8,128)S(1)}, f32[2,256,128]{2,1,0:T(8,128)S(1)}, u32[]{:S(2)}, u32[]{:S(2)}) collective-permute-start(f32[2,256,128]{2,1,0:T(8,128)S(1)} %get-tuple-element.45), channel_id=1, source_target_pairs={{0,1},{1,0},{2,3},{3,2},{4,5},{5,4},{6,7},{7,6},{8,9},{9,8},{10,11... | collective-permute-start | bytes 786440 | tf_op jit(solution)/shard_map/ppermute | solution.py:417
  51.8 6.8 %collective-permute-start.22 = (f32[256,128]{1,0:T(8,128)S(1)}, f32[256,128]{1,0:T(8,128)S(1)}, u32[]{:S(2)}, u32[]{:S(2)}) collective-permute-start(f32[256,128]{1,0:T(8,128)S(1)} %get-tuple-element.47), channel_id=1, source_target_pairs={{0,2},{1,3},{2,0},{3,1},{4,6},{5,7},{6,4},{7,5},{8,10},{9,11},{10,... | collective-permute-start | bytes 393224 | tf_op jit(solution)/shard_map/ppermute | solution.py:417
  60.4 22.9 %all-to-all-start.1 = ((f32[8,72,128]{2,1,0:T(8,128)}), f32[8,72,128]{2,1,0:T(8,128)S(1)}, u32[]{:S(2)}, u32[]{:S(2)}) async-start(f32[8,72,128]{2,1,0:T(8,128)} %shard_map.171), calls=%async_computation.1 | async-start | bytes 589824 | tf_op jit(solution)/shard_map/all_to_all | solution.py:566
  65.5 9.3 %collective-permute-start.16 = (f32[1,32,128]{2,1,0:T(8,128)S(1)}, f32[1,32,128]{2,1,0:T(8,128)S(1)}, u32[]{:S(2)}, u32[]{:S(2)}) collective-permute-start(f32[1,32,128]{2,1,0:T(8,128)S(1)} %shard_map.166.refs_0_), channel_id=1, source_target_pairs={{0,24},{4,28},{8,16},{12,20},{16,8},{20,12},{24,0},{28,4},{1,25},{... | collective-permute-start | bytes 49160 | tf_op jit(solution)/shard_map/ppermute | solution.py:420
  69.4 6.7 %collective-permute-start.15 = (f32[1,32,128]{2,1,0:T(8,128)S(1)}, f32[1,32,128]{2,1,0:T(8,128)S(1)}, u32[]{:S(2)}, u32[]{:S(2)}) collective-permute-start(f32[1,32,128]{2,1,0:T(8,128)S(1)} %shard_map.166.refs_0_), channel_id=1, source_target_pairs={{0,16},{4,20},{8,24},{12,28},{16,0},{20,4},{24,8},{28,12},{1,17},{... | collective-permute-start | bytes 49160 | tf_op jit(solution)/shard_map/ppermute | solution.py:420
  69.4 6.7 %collective-permute-start.14 = (f32[1,32,128]{2,1,0:T(8,128)S(1)}, f32[1,32,128]{2,1,0:T(8,128)S(1)}, u32[]{:S(2)}, u32[]{:S(2)}) collective-permute-start(f32[1,32,128]{2,1,0:T(8,128)S(1)} %shard_map.166.refs_0_), channel_id=1, source_target_pairs={{0,8},{4,12},{8,0},{12,4},{16,24},{20,28},{24,16},{28,20},{1,9},{5... | collective-permute-start | bytes 49160 | tf_op jit(solution)/shard_map/ppermute | solution.py:420
  76.2 5.2 %collective-permute-start.19 = (f32[4,32,128]{2,1,0:T(8,128)S(1)}, f32[4,32,128]{2,1,0:T(8,128)S(1)}, u32[]{:S(2)}, u32[]{:S(2)}) collective-permute-start(f32[4,32,128]{2,1,0:T(8,128)S(1)} %shard_map.167.refs_0_), channel_id=1, source_target_pairs={{0,6},{1,7},{2,4},{3,5},{4,2},{5,3},{6,0},{7,1},{8,14},{9,15},{10,... | collective-permute-start | bytes 196616 | tf_op jit(solution)/shard_map/ppermute | solution.py:547
  78.4 4.3 %collective-permute-start.18 = (f32[4,32,128]{2,1,0:T(8,128)S(1)}, f32[4,32,128]{2,1,0:T(8,128)S(1)}, u32[]{:S(2)}, u32[]{:S(2)}) collective-permute-start(f32[4,32,128]{2,1,0:T(8,128)S(1)} %shard_map.167.refs_0_), channel_id=1, source_target_pairs={{0,4},{4,0},{8,12},{12,8},{16,20},{20,16},{24,28},{28,24},{1,5},{5... | collective-permute-start | bytes 196616 | tf_op jit(solution)/shard_map/ppermute | solution.py:420
  78.9 4.3 %collective-permute-start.17 = (f32[4,32,128]{2,1,0:T(8,128)S(1)}, f32[4,32,128]{2,1,0:T(8,128)S(1)}, u32[]{:S(2)}, u32[]{:S(2)}) collective-permute-start(f32[4,32,128]{2,1,0:T(8,128)S(1)} %shard_map.167.refs_0_), channel_id=1, source_target_pairs={{0,2},{1,3},{2,0},{3,1},{4,6},{5,7},{6,4},{7,5},{8,10},{9,11},{10,... | collective-permute-start | bytes 196616 | tf_op jit(solution)/shard_map/ppermute | solution.py:417
  83.2 1.6 %collective-permute-start.20 = (f32[512,128]{1,0:T(8,128)S(1)}, f32[512,128]{1,0:T(8,128)S(1)}, u32[]{:S(2)}, u32[]{:S(2)}) collective-permute-start(f32[512,128]{1,0:T(8,128)S(1)} %bitcast.8), channel_id=1, source_target_pairs={{0,1},{1,0},{2,3},{3,2},{4,5},{5,4},{6,7},{7,6},{8,9},{9,8},{10,11... | collective-permute-start | bytes 786440 | tf_op jit(solution)/shard_map/ppermute | solution.py:417

commit v2 on v1

--- a/solution.py
+++ b/solution.py
@@ -40,6 +40,7 @@
 
 
 NT = (((1,), (1,)), ((), ()))
+TN = (((0,), (0,)), ((), ()))
 
 
 def iota(shape, dim, dtype=I32):
@@ -115,9 +116,7 @@
     out_ref[at[4] : at[5], :] = padded(jnp.concatenate([hi, mid, low], axis=0), 16).astype(BF16)
 
 
-def local_kernel(
-    mp_count, slots, share, fields, map_ref, ids_ref, hot_ids_ref, hot_ref, pos_ref, rows_ref
-):
+def place_kernel(mp_count, slots, map_ref, ids_ref, pos_ref):
     touch = ids_ref.shape[1]
     map_rows, lanes = map_ref.shape
     ids_col = column(ids_ref[...])
@@ -130,30 +129,20 @@
     stored = jnp.sum(jnp.where(in_lane, picked, 0.0), axis=1, keepdims=True).astype(I32)
     stored = jnp.broadcast_to(stored, (touch, lanes))
     pos_ref[...] = stored // (mp_count * slots) * slots + stored % slots
-    hot_rows, emb = hot_ref.shape
-    hot = hot_ref[...].astype(BF16)
-    my = lax.axis_index("mp")
-    lane = iota((share, hot_rows), 1)
-    for f in range(fields):
-        mine = hot_ids_ref[f : f + 1, pl.ds(pl.multiple_of(my * share, share), share)]
-        hit = (lane == column(mine)).astype(F32).astype(BF16)
-        rows_ref[:, f * emb : (f + 1) * emb] = dot(hit, hot).astype(BF16)
 
 
 def count_kernel(
-    share, touch, at, item_rows, count_rows, p0, p1, p2, p3, cnt_ref, cntt_ref,
+    share, touch, at, item_rows, count_rows, p0, p1, cnt_ref, cntt_ref,
     items_ref, starts_ref, ends_ref, acc_ref,
 ):
     lanes = p0.shape[1]
     my = lax.axis_index("mp")
     per = share // lanes
-    step = 2
-    chunk = step * lanes
+    block = min(item_rows, -(-3 * item_rows // 8))
     sub_t = iota((touch, lanes), 0, F32)
-    sub_i = iota((chunk, share), 0, F32)
     upto = (iota((lanes, lanes), 0) <= iota((lanes, lanes), 1)).astype(F32).astype(BF16)
-    bounds = []
-    for k, pack in enumerate((p0, p1, p2, p3)):
+    packs = (p0, p1)
+    for k, pack in enumerate(packs):
         sizes = pack[at[3] : at[4], :]
         ends = dot(sizes, upto)[:count_rows]
         sizes = sizes.astype(F32)[:count_rows]
@@ -168,29 +157,34 @@
     def rows_of(ref, k):
         return jnp.concatenate([ref[k, pl.ds(my * per + j, 1), :] for j in range(per)], axis=1)
 
-    for k in range(4):
+    bounds = []
+    for k in range(len(packs)):
         starts = rows_of(starts_ref, k)
         ends = rows_of(ends_ref, k)
-        low = jnp.min(starts).astype(I32)
-        high = jnp.max(ends).astype(I32)
-        bounds.append((starts, ends, low // chunk, (high + chunk - 1) // chunk))
+        first = jnp.min(starts).astype(I32) // lanes
+        last = (jnp.max(ends).astype(I32) + lanes - 1) // lanes
+        bounds.append((starts, ends, jnp.minimum(first, item_rows - block), last))
+
+    def counted(k, first, rows, starts, ends):
+        pick = jnp.concatenate(
+            [
+                (sub_t == items_ref[k, pl.ds(first + j, 1), :]).astype(F32).astype(BF16)
+                for j in range(rows)
+            ],
+            axis=1,
+        )
+        pos = iota((rows * lanes, share), 0, F32) + (first * lanes).astype(F32)
+        memb = ((pos >= starts) & (pos < ends)).astype(F32).astype(BF16)
+        return dot(pick, memb)
+
     for k, (starts, ends, first, last) in enumerate(bounds):
-        acc_ref[...] = jnp.zeros_like(acc_ref)
+        acc_ref[...] = counted(k, first, block, starts, ends)
 
         def body(c, carry):
-            pick = jnp.concatenate(
-                [
-                    (sub_t == items_ref[k, pl.ds(c * step + j, 1), :]).astype(F32).astype(BF16)
-                    for j in range(step)
-                ],
-                axis=1,
-            )
-            pos = sub_i + (c * chunk).astype(F32)
-            memb = ((pos >= starts) & (pos < ends)).astype(F32).astype(BF16)
-            acc_ref[...] += dot(pick, memb)
+            acc_ref[...] += counted(k, c, 1, starts, ends)
             return carry
 
-        lax.fori_loop(first, last, body, 0)
+        lax.fori_loop(first + block, last, body, 0)
         counts_t = acc_ref[...]
         cntt_ref[k * touch : (k + 1) * touch, :] = counts_t.astype(BF16)
         cnt_ref[:, k * touch : (k + 1) * touch] = counts_t.T.astype(BF16)
@@ -201,13 +195,13 @@
 ):
     my = lax.axis_index("mp")
     emb = p0.shape[1]
-    hot_cols = rows_ref.shape[1]
+    hot_cols = rows_ref.shape[0]
     grads = grads_ref[pl.ds(pl.multiple_of(my * share, share), share), :]
     rows = rows_ref[...]
     for k, p in enumerate((p0, p1, p2, p3)):
         cols = slice(k * hidden, (k + 1) * hidden)
         bias = jnp.sum(p[at[4] : at[5], :].astype(F32), axis=0, keepdims=True)
-        pre_ref[:, cols] = dot(rows, p[:hot_cols, :]) + bias
+        pre_ref[:, cols] = dot(rows, p[:hot_cols, :], TN) + bias
         back = jnp.zeros((share, hidden), F32)
         for j in range(grads.shape[1] // emb):
             piece = p[at[1] + j * hidden : at[1] + (j + 1) * hidden, :]
@@ -245,12 +239,18 @@
     )
 
 
-def onehot_kernel(share, fields, slots, cap, ids_ref, pos_ref, out_ref, q_ref, srow_ref):
+def onehot_kernel(
+    share, fields, slots, cap, ids_ref, pos_ref, hot_ref, out_ref, q_ref, srow_ref, rows_ref
+):
     my = lax.axis_index("mp")
+    emb = hot_ref.shape[1]
+    hot = hot_ref[...].T.astype(BF16)
     sub = iota((out_ref.shape[0], share), 0)
     for f in range(fields):
         mine = ids_ref[f : f + 1, pl.ds(pl.multiple_of(my * share, share), share)]
-        out_ref[:, f * share : (f + 1) * share] = (sub == mine).astype(F32).astype(BF16)
+        hit = (sub == mine).astype(F32).astype(BF16)
+        out_ref[:, f * share : (f + 1) * share] = hit
+        rows_ref[f * emb : (f + 1) * emb, :] = dot(hot, hit).astype(BF16)
     pos = pos_ref[...]
     touch, lanes = pos.shape
     row = pos.T[0:1, :]
@@ -272,15 +272,16 @@
 
 
 def main_kernel(
-    fields, cnt_ref, f0, f1, f2, f3, pre_ref, back_ref, tail_ref, wt_ref, oht_ref,
+    fields, cnta_ref, cntb_ref, f0, f1, f2, f3, pre_ref, back_ref, tail_ref, wt_ref, oht_ref,
     ig_ref, bag_ref, send_ref,
 ):
     touch, emb = f0.shape
-    share = cnt_ref.shape[0]
+    share = cnta_ref.shape[0]
     core = lax.axis_index("mp") % 2
     pooled = jnp.zeros((share, emb), F32)
     for k, f in enumerate((f0, f1, f2, f3)):
-        pooled = pooled + dot(cnt_ref[:, k * touch : (k + 1) * touch], f[...])
+        cnt = (cnta_ref, cntb_ref)[k // 2]
+        pooled = pooled + dot(cnt[:, k % 2 * touch : (k % 2 + 1) * touch], f[...])
     pre = pre_ref[...] + dot(pooled.astype(BF16), tail_ref[...])
     sig = jax.nn.sigmoid(pre)
     hidden = (back_ref[...] * sig * (1.0 + pre * (1.0 - sig))).astype(BF16)
@@ -293,7 +294,7 @@
     send_ref[...] = sum_halves(dot(oht_ref[pl.ds(first, half), :], ig_ref[...]))
 
 
-def keep_kernel(oht_ref, ig_ref, bag_ref, cntt_ref, keep_ref, touch_send, touch_keep):
+def keep_kernel(oht_ref, ig_ref, bag_ref, cntta_ref, cnttb_ref, keep_ref, touch_send, touch_keep):
     half = keep_ref.shape[0]
     core = lax.axis_index("mp") % 2
     first = pl.multiple_of(core * half, half)
@@ -301,8 +302,9 @@
     touch = touch_send.shape[1]
     for k in range(4):
         ref = touch_send if k % 2 else touch_keep
-        rows = slice(k * touch, (k + 1) * touch)
-        ref[k // 2] = sum_halves(dot(cntt_ref[rows, :], bag_ref[...]))
+        counts = (cntta_ref, cnttb_ref)[k // 2]
+        rows = slice(k % 2 * touch, (k % 2 + 1) * touch)
+        ref[k // 2] = sum_halves(dot(counts[rows, :], bag_ref[...]))
 
 
 def add_kernel(a_ref, b_ref, out_ref):
@@ -338,20 +340,27 @@
     out_ref[...] = jnp.broadcast_to(total, out_ref.shape)
 
 
-def order_far_kernel(*refs):
-    out_ref = refs[-1]
-    far = lax.axis_index("dp") // 2
-    for k, ref in enumerate(refs[:-1]):
-        out_ref[far ^ k] = ref[0]
-
-
-def order_near_kernel(*refs):
-    out_ref = refs[-1]
+def near_place(far, k):
     near = lax.axis_index("dp") % 2
     group = lax.axis_index("mp") // 2
+    return (far * 2 + (near ^ (k // 2))) * 2 + (group ^ (k % 2))
+
+
+def split_near_kernel(keep_ref, got_ref, *outs):
+    for k, ref in enumerate(outs):
+        for far in range(ref.shape[0]):
+            at = near_place(far, k)
+            ref[far] = keep_ref[at] + got_ref[at]
+
+
+def sum_kernel(a_ref, b_ref, c_ref, d_ref, out_ref):
+    out_ref[...] = (a_ref[...] + b_ref[...]) + (c_ref[...] + d_ref[...])
+
+
+def order_near_kernel(*refs):
     for k, ref in enumerate(refs[:-1]):
         for far in range(ref.shape[0]):
-            out_ref[(far * 2 + (near ^ (k // 2))) * 2 + (group ^ (k % 2))] = ref[far]
+            refs[-1][near_place(far, k)] = ref[far]
 
 
 def pack_kernel(cap, mine_ref, got_ref, q_ref, srow_ref, out_ref):
@@ -452,26 +461,39 @@
     pack_cross = swap(pack_far, 1)
     packs = [pack, pack_near, pack_far, pack_cross]
 
-    pos, rows = call(
-        lambda *r: local_kernel(mp_count, slots, share, fields, *r),
-        [((touch, emb), I32, True), ((share, fields * emb), BF16, True)],
-        [owner_map.reshape(-1, emb), touched.reshape(1, touch), hot_ids.T, hot_table],
-        late=range(4),
-    )
-
-    cnt, cntt = call(
-        lambda *r: count_kernel(share, touch, at, item_rows, count_rows, *r),
+    (pos,) = call(
+        lambda *r: place_kernel(mp_count, slots, *r),
+        [((touch, emb), I32, True)],
+        [owner_map.reshape(-1, emb), touched.reshape(1, touch)],
+        late=range(2),
+    )
+
+    def count(pair):
+        return call(
+            lambda *r: count_kernel(share, touch, at, item_rows, count_rows, *r),
+            [((share, 2 * touch), BF16, True), ((2 * touch, share), BF16, True)],
+            pair,
+            scratch=[
+                pltpu.VMEM((2, item_rows, emb), F32),
+                pltpu.VMEM((2, count_rows, emb), F32),
+                pltpu.VMEM((2, count_rows, emb), F32),
+                pltpu.VMEM((touch, share), F32),
+            ],
+        )
+
+    cnta, cntta = count(packs[:2])
+    cntb, cnttb = count(packs[2:])
+
+    oht, q_mat, slot_rows, rows = call(
+        lambda *r: onehot_kernel(share, fields, slots, cap, *r),
         [
-            ((share, mp_count * touch), BF16, True),
-            ((mp_count * touch, share), BF16, True),
+            ((hot_rows, fields * share), BF16, True),
+            ((dp_count * cap, touch), BF16, True),
+            ((dp_count * 8, emb), F32, True),
+            ((fields * emb, share), BF16, True),
         ],
-        packs,
-        scratch=[
-            pltpu.VMEM((mp_count, item_rows, emb), F32),
-            pltpu.VMEM((mp_count, count_rows, emb), F32),
-            pltpu.VMEM((mp_count, count_rows, emb), F32),
-            pltpu.VMEM((touch, share), F32),
-        ],
+        [hot_ids.T, pos, hot_table],
+        late=(0, 2),
     )
 
     wt, tail, pre, back = call(
@@ -493,18 +515,7 @@
         late=() if near else (1,),
     )
     far = swap(fetched, 2)
-    around = [fetched, swap(fetched, 1), far, swap(fetched, 3)]
-
-    ids_late, _ = lax.optimization_barrier((hot_ids.T, fetched))
-    oht, q_mat, slot_rows = call(
-        lambda *r: onehot_kernel(share, fields, slots, cap, *r),
-        [
-            ((hot_rows, fields * share), BF16, True),
-            ((dp_count * cap, touch), BF16, True),
-            ((dp_count * 8, emb), F32, True),
-        ],
-        [ids_late, pos],
-    )
+    around = [fetched, swap(fetched, 1), far, swap(far, 1)]
 
     half_rows = hot_rows // 2
     ig, bag, hot_send = call(
@@ -514,7 +525,7 @@
             ((share, 2 * emb), BF16, True),
             ((half_rows, emb), F32, True),
         ],
-        [cnt, *around, pre, back, tail, wt, oht],
+        [cnta, cntb, *around, pre, back, tail, wt, oht],
     )
     hot_got = swap(hot_send, 1)
     hot_keep, touch_send, touch_keep = call(
@@ -524,7 +535,7 @@
             ((mp_count // 2, touch, emb), F32, True),
             ((mp_count // 2, touch, emb), F32, True),
         ],
-        [oht, ig, bag, cntt],
+        [oht, ig, bag, cntta, cnttb],
     )
 
     group_size = dp_count * mp_count // 2
@@ -535,20 +546,32 @@
             x, both, split_axis=0, concat_axis=0, tiled=True, axis_index_groups=rank_groups
         )
 
-    (chip,) = call(add_kernel, [((half_rows, emb), F32, True)], [hot_keep, hot_got])
-    parts = exchange(chip.reshape(group_size, -1, emb))
-    shard_shape = parts.shape if not near else (1, *parts.shape[1:])
-    (shard,) = call(reduce_kernel, [(shard_shape, F32, True)], [parts])
+    def near_swap(x, k):
+        mask = k // 2 * mp_count + k % 2 * 2
+        return lax.ppermute(
+            x, both, [(i, i ^ mask) for i in range(dp_count * mp_count)]
+        )
+
     if near:
-        pieces = [shard] + [far_swap(shard, 2 * k) for k in (1, 2, 3)]
-        (line,) = call(order_far_kernel, [((4, *parts.shape[1:]), F32, True)], pieces)
-        pieces = [line, swap(line, 2), far_swap(line, 1)]
-        pieces.append(
-            lax.ppermute(line, both, [(i, i ^ (mp_count + 2)) for i in range(dp_count * mp_count)])
+        rows_each = half_rows // group_size
+        shape = (group_size, rows_each, emb)
+        line = (dp_count // 2, rows_each, emb)
+        pieces = call(
+            split_near_kernel,
+            [(line, F32, True)] * 4,
+            [hot_keep.reshape(shape), hot_got.reshape(shape)],
         )
-        (half,) = call(order_near_kernel, [(parts.shape, F32, True)], pieces)
+        pieces = [near_swap(x, k) if k else x for k, x in enumerate(pieces)]
+        (part,) = call(sum_kernel, [(line, F32, True)], pieces)
+        pieces = [far_swap(part, 2 * k) if k else part for k in range(4)]
+        (part,) = call(sum_kernel, [(line, F32, True)], pieces)
+        pieces = [near_swap(part, k) if k else part for k in range(4)]
+        (half,) = call(order_near_kernel, [(shape, F32, True)], pieces)
         half = half.reshape(half_rows, emb)
     else:
+        (chip,) = call(add_kernel, [((half_rows, emb), F32, True)], [hot_keep, hot_got])
+        parts = exchange(chip.reshape(group_size, -1, emb))
+        (shard,) = call(reduce_kernel, [(parts.shape, F32, True)], [parts])
         half = exchange(shard).reshape(half_rows, emb)
     other = swap(half, 1)
     hot_updated, hot_accum_new = call(

time: 86.5 us -> 87.1 us (level)
  waiting for transfers between devices: 29.5 us -> 36.7 us
  starting transfers between devices: 36.5 us -> 33.3 us
  Pallas kernels: 18.4 us -> 15.9 us
    ppermute x1 -> x6, waiting for transfers between devices: 1.67 us -> 8.41 us  [near_swap(): lax.ppermute(x, both, [(i, i ^ mask) for i in range(dp_count * mp_count)])]
    all_to_all x1 -> x0, starting transfers between devices: 6.02 us -> none  [exchange(): lax.all_to_all(x, both, split_axis=0, concat_axis=0, tiled=True, axis_ind...]
    ppermute x1 -> x6, starting transfers between devices: 2.19 us -> 7.12 us  [near_swap(): lax.ppermute(x, both, [(i, i ^ mask) for i in range(dp_count * mp_count)])]
    pallas_call x17 -> x18, Pallas kernels: 18.4 us -> 15.9 us  [call(): pl.pallas_call(body, out_shape=avals, in_specs=[VM] * len(ins), out_specs...]
    ppermute x11 -> x10, waiting for transfers between devices: 15.6 us -> 17.6 us  [swap(): return lax.ppermute(x, 'mp', [(i, i ^ mask) for i in range(mp_count)])]
    ppermute x11 -> x10, starting transfers between devices: 8.55 us -> 6.88 us  [swap(): return lax.ppermute(x, 'mp', [(i, i ^ mask) for i in range(mp_count)])]
    ppermute x11 -> x10, waiting for transfers between devices: 11.4 us -> 10.6 us  [far_swap(): return lax.ppermute(x, 'dp', [(i, i ^ mask) for i in range(dp_count)])]
    ppermute x11 -> x10, starting transfers between devices: 14.6 us -> 14.1 us  [far_swap(): return lax.ppermute(x, 'dp', [(i, i ^ mask) for i in range(dp_count)])]
  transfers between devices with their start and end apart: 25 -> 27, of which waited for: 14 -> 19; matrix products, arithmetic and copies ran while one was open for 0% -> 0% of each run, Pallas kernels for 16% -> 13%
where the time goes in v2:
time: 87.1 us; the launch traced here: 86.7 us
  waiting for transfers between devices  36.7 us (42%)
  starting transfers between devices  33.3 us (38%)
  Pallas kernels  15.9 us (18%)
    ppermute x10, waiting for transfers between devices, swap(): return lax.ppermute(x, 'mp', [(i, i ^ mask) for i in range(mp_count)])  17.6 us
    pallas_call x18, Pallas kernels, call(): pl.pallas_call(body, out_shape=avals, in_specs=[VM] * len(ins), out_specs...  15.9 us
    ppermute x10, starting transfers between devices, far_swap(): return lax.ppermute(x, 'dp', [(i, i ^ mask) for i in range(dp_count)])  14.1 us
    ppermute x10, waiting for transfers between devices, far_swap(): return lax.ppermute(x, 'dp', [(i, i ^ mask) for i in range(dp_count)])  10.6 us
    ppermute x6, waiting for transfers between devices, near_swap(): lax.ppermute(x, both, [(i, i ^ mask) for i in range(dp_count * mp_count)])  8.41 us
    ppermute x6, starting transfers between devices, near_swap(): lax.ppermute(x, both, [(i, i ^ mask) for i in range(dp_count * mp_count)])  7.12 us
    ppermute x10, starting transfers between devices, swap(): return lax.ppermute(x, 'mp', [(i, i ^ mask) for i in range(mp_count)])  6.88 us
    all_to_all x1, starting transfers between devices, per_device(): lax.all_to_all(outgoing, 'dp', split_axis=0, concat_axis=0, tiled=True)  5.2 us
  transfers between devices with their start and end apart: 27, of which 19 were waited for; matrix products, arithmetic and copies ran while one was open for 0% of the time, Pallas kernels for 13%

profile of v2, /device:TPU:0, one launch (start us, length us, event | category | flops | bytes accessed | tf_op | source)
XLA Modules:
  0.0 86.7 jit_solution(12480164736470016340)
XLA Ops:
  0.6 1.0 %shard_map.158.r_0_ = bf16[1328,128]{1,0:T(8,128)(2,1)S(1)} custom-call(bf16[1024,128]{1,0:T(8,128)(2,1)} %r_0_.1, bf16[128,256]{1,0:T(8,128)(2,1)} %r_1_.2, s32[16,128]{1,0:T(8,128)} %bitcast.15, s32[8,128]{1,0:T(8,128)} %bitcast.16, f32[1,128]{1,0:T(1,128)} %bitcast.18), custom_call_target="tpu_custom_call" | custom-call | tf_op jit(solution)/shard_map/pallas_call | solution.py:59
  1.7 3.0 %collective-permute-start.1 = (bf16[1328,128]{1,0:T(8,128)(2,1)S(1)}, bf16[1328,128]{1,0:T(8,128)(2,1)S(1)}, u32[]{:S(2)}, u32[]{:S(2)}) collective-permute-start(bf16[1328,128]{1,0:T(8,128)(2,1)S(1)} %shard_map.158.r_0_), channel_id=1, source_target_pairs={{0,2},{1,3},{2,0},{3,1},{4,6},{5,7},{6,4},{7,5},{8,10},{9,11},{10,... | collective-permute-start | bytes 1019912 | tf_op jit(solution)/shard_map/ppermute | solution.py:426
  4.7 8.0 %collective-permute-done.1.r_0_.r_2_ = bf16[1328,128]{1,0:T(8,128)(2,1)S(1)} collective-permute-done((bf16[1328,128]{1,0:T(8,128)(2,1)S(1)}, bf16[1328,128]{1,0:T(8,128)(2,1)S(1)}, u32[]{:S(2)}, u32[]{:S(2)}) %collective-permute-start.1) | collective-permute-done | bytes 340000 | tf_op jit(solution)/shard_map/ppermute | solution.py:426
  12.7 0.9 %shard_map.161.refs_0_ = bf16[256,128]{1,0:T(8,128)(2,1)S(1)} custom-call(f32[256,128]{1,0:T(8,128)} %r_1_.3), custom_call_target="tpu_custom_call" | custom-call | tf_op jit(solution)/shard_map/pallas_call | solution.py:59
  13.6 1.8 %collective-permute-start.4 = (bf16[256,128]{1,0:T(8,128)(2,1)S(1)}, bf16[256,128]{1,0:T(8,128)(2,1)S(1)}, u32[]{:S(2)}, u32[]{:S(2)}) collective-permute-start(bf16[256,128]{1,0:T(8,128)(2,1)S(1)} %shard_map.161.refs_0_), channel_id=1, source_target_pairs={{0,8},{4,12},{8,0},{12,4},{16,24},{20,28},{24,16},{28,20},{1,9},{5... | collective-permute-start | bytes 196616 | tf_op jit(solution)/shard_map/ppermute | solution.py:429
  15.4 2.6 %collective-permute-start.6 = (bf16[256,128]{1,0:T(8,128)(2,1)S(1)}, bf16[256,128]{1,0:T(8,128)(2,1)S(1)}, u32[]{:S(2)}, u32[]{:S(2)}) collective-permute-start(bf16[256,128]{1,0:T(8,128)(2,1)S(1)} %shard_map.161.refs_0_), channel_id=1, source_target_pairs={{0,16},{4,20},{8,24},{12,28},{16,0},{20,4},{24,8},{28,12},{1,17},{... | collective-permute-start | bytes 196616 | tf_op jit(solution)/shard_map/ppermute | solution.py:429
  18.2 1.7 %collective-permute-start.3 = (bf16[256,128]{1,0:T(8,128)(2,1)S(1)}, bf16[256,128]{1,0:T(8,128)(2,1)S(1)}, u32[]{:S(2)}, u32[]{:S(2)}) collective-permute-start(bf16[256,128]{1,0:T(8,128)(2,1)S(1)} %shard_map.161.refs_0_), channel_id=1, source_target_pairs={{0,4},{4,0},{8,12},{12,8},{16,20},{20,16},{24,28},{28,24},{1,5},{5... | collective-permute-start | bytes 196616 | tf_op jit(solution)/shard_map/ppermute | solution.py:429
  19.9 2.5 %collective-permute-done.6.refs_4_ = bf16[256,128]{1,0:T(8,128)(2,1)S(1)} collective-permute-done((bf16[256,128]{1,0:T(8,128)(2,1)S(1)}, bf16[256,128]{1,0:T(8,128)(2,1)S(1)}, u32[]{:S(2)}, u32[]{:S(2)}) %collective-permute-start.6) | collective-permute-done | bytes 65568 | tf_op jit(solution)/shard_map/ppermute | solution.py:429
  22.4 1.5 %collective-permute-start.5 = (bf16[256,128]{1,0:T(8,128)(2,1)S(1)}, bf16[256,128]{1,0:T(8,128)(2,1)S(1)}, u32[]{:S(2)}, u32[]{:S(2)}) collective-permute-start(bf16[256,128]{1,0:T(8,128)(2,1)S(1)} %collective-permute-done.4.refs_2_), channel_id=1, source_target_pairs={{0,4},{4,0},{8,12},{12,8},{16,20},{20,16},{24,28},{28,24},{1,5},{5... | collective-permute-start | bytes 196616 | tf_op jit(solution)/shard_map/ppermute | solution.py:429
  24.1 1.5 %collective-permute-start.7 = (bf16[256,128]{1,0:T(8,128)(2,1)S(1)}, bf16[256,128]{1,0:T(8,128)(2,1)S(1)}, u32[]{:S(2)}, u32[]{:S(2)}) collective-permute-start(bf16[256,128]{1,0:T(8,128)(2,1)S(1)} %collective-permute-done.6.refs_4_), channel_id=1, source_target_pairs={{0,4},{4,0},{8,12},{12,8},{16,20},{20,16},{24,28},{28,24},{1,5},{5... | collective-permute-start | bytes 196616 | tf_op jit(solution)/shard_map/ppermute | solution.py:429
  25.6 0.5 collective-permute-start.9
  26.1 1.4 %shard_map.156.r_1_.pos_ref = s32[256,128]{1,0:T(8,128)S(1)} custom-call(s32[64,128]{1,0:T(8,128)} %bitcast.13, s32[1,256]{1,0:T(1,128)} %bitcast.17), custom_call_target="tpu_custom_call" | custom-call | tf_op jit(solution)/shard_map/pallas_call | solution.py:59
  27.5 0.9 collective-permute-done.7.refs_5_
  28.4 1.5 %collective-permute-done.9.refs_7_ = bf16[256,128]{1,0:T(8,128)(2,1)S(1)} collective-permute-done((bf16[256,128]{1,0:T(8,128)(2,1)S(1)}, bf16[256,128]{1,0:T(8,128)(2,1)S(1)}, u32[]{:S(2)}, u32[]{:S(2)}) %collective-permute-start.9) | collective-permute-done | bytes 65568 | tf_op jit(solution)/shard_map/ppermute | solution.py:429
  29.9 0.4 shard_map.162.r_2_
  30.3 1.6 %collective-permute-start.11 = (bf16[256,128]{1,0:T(8,128)(2,1)S(1)}, bf16[256,128]{1,0:T(8,128)(2,1)S(1)}, u32[]{:S(2)}, u32[]{:S(2)}) collective-permute-start(bf16[256,128]{1,0:T(8,128)(2,1)S(1)} %shard_map.162.r_2_), channel_id=1, source_target_pairs={{0,2},{1,3},{2,0},{3,1},{4,6},{5,7},{6,4},{7,5},{8,10},{9,11},{10,... | collective-permute-start | bytes 196616 | tf_op jit(solution)/shard_map/ppermute | solution.py:426
  31.9 2.8 %collective-permute-done.11.r_4_ = bf16[256,128]{1,0:T(8,128)(2,1)S(1)} collective-permute-done((bf16[256,128]{1,0:T(8,128)(2,1)S(1)}, bf16[256,128]{1,0:T(8,128)(2,1)S(1)}, u32[]{:S(2)}, u32[]{:S(2)}) %collective-permute-start.11) | collective-permute-done | bytes 65568 | tf_op jit(solution)/shard_map/ppermute | solution.py:426
  34.6 2.5 %shard_map.157 = (bf16[1024,1792]{1,0:T(8,128)(2,1)S(1)}, bf16[512,256]{1,0:T(8,128)(2,1)S(1)}, f32[64,128]{1,0:T(8,128)S(1)}, bf16[896,256]{1,0:T(8,128)(2,1)S(1)}) custom-call(s32[7,1024]{1,0:T(8,128)} %bitcast.14, s32[256,128]{1,0:T(8,128)S(1)} %shard_map.156.r_1_.pos_ref, f32[1024,128]{1,0:T(8,128)} %table_ref.3), custom_call_target="tpu_custom_call" | custom-call | tf_op jit(solution)/shard_map/pallas_call | solution.py:59
  37.2 1.0 %shard_map.159 = (bf16[256,512]{1,0:T(8,128)(2,1)S(1)}, bf16[512,256]{1,0:T(8,128)(2,1)S(1)}) custom-call(bf16[1328,128]{1,0:T(8,128)(2,1)S(1)} %shard_map.158.r_0_, bf16[1328,128]{1,0:T(8,128)(2,1)S(1)} %collective-permute-done.r_1_), custom_call_target="tpu_custom_call" | custom-call | tf_op jit(solution)/shard_map/pallas_call | solution.py:59
  38.2 1.0 %shard_map.160 = (bf16[256,512]{1,0:T(8,128)(2,1)S(1)}, bf16[512,256]{1,0:T(8,128)(2,1)S(1)}) custom-call(bf16[1328,128]{1,0:T(8,128)(2,1)S(1)} %collective-permute-done.1.r_0_.r_2_, bf16[1328,128]{1,0:T(8,128)(2,1)S(1)} %collective-permute-done.2.r_1_.r_3_), custom_call_target="tpu_custom_call" | custom-call | tf_op jit(solution)/shard_map/pallas_call | solution.py:59
  39.3 1.9 %shard_map.163 = (bf16[512,1024]{1,0:T(8,128)(2,1)S(1)}, bf16[128,512]{1,0:T(8,128)(2,1)S(1)}, f32[256,512]{1,0:T(8,128)S(1)}, f32[256,512]{1,0:T(8,128)S(1)}) custom-call(bf16[1328,128]{1,0:T(8,128)(2,1)S(1)} %shard_map.158.r_0_, bf16[1328,128]{1,0:T(8,128)(2,1)S(1)} %collective-permute-done.r_1_, bf16[1328,128]{1,0:T(8,128)(2,1)S(1)} %collective-permute-done.1.r_0_.r_2_, ...), custom_call_target="tpu_custom_call" | custom-call | tf_op jit(solution)/shard_map/pallas_call | solution.py:59
  41.2 1.5 %shard_map.164 = (bf16[1792,256]{1,0:T(8,128)(2,1)S(1)}, bf16[256,256]{1,0:T(8,128)(2,1)S(1)}, f32[512,128]{1,0:T(8,128)S(1)}) custom-call(bf16[256,512]{1,0:T(8,128)(2,1)S(1)} %get-tuple-element.33.r_0_, bf16[256,512]{1,0:T(8,128)(2,1)S(1)} %get-tuple-element.34.r_1_, bf16[256,128]{1,0:T(8,128)(2,1)S(1)} %shard_map.162.r_2_, ...), custom_call_target="tpu_custom_call" | custom-call | tf_op jit(solution)/shard_map/pallas_call | solution.py:59
  42.7 0.8 shard_map.165
  43.5 0.6 collective-permute-start.24
  44.2 1.1 %collective-permute-done.24.got_ref = f32[2,256,128]{2,1,0:T(8,128)S(1)} collective-permute-done((f32[2,256,128]{2,1,0:T(8,128)S(1)}, f32[2,256,128]{2,1,0:T(8,128)S(1)}, u32[]{:S(2)}, u32[]{:S(2)}) %collective-permute-start.24) | collective-permute-done | bytes 262176 | tf_op jit(solution)/shard_map/ppermute | solution.py:426
  45.3 1.6 %collective-permute-start.25 = (f32[256,128]{1,0:T(8,128)S(1)}, f32[256,128]{1,0:T(8,128)S(1)}, u32[]{:S(2)}, u32[]{:S(2)}) collective-permute-start(f32[256,128]{1,0:T(8,128)S(1)} %get-tuple-element.55), channel_id=1, source_target_pairs={{0,2},{1,3},{2,0},{3,1},{4,6},{5,7},{6,4},{7,5},{8,10},{9,11},{10,... | collective-permute-start | bytes 393224 | tf_op jit(solution)/shard_map/ppermute | solution.py:426
  46.9 4.3 %collective-permute-done.25.r_1_ = f32[256,128]{1,0:T(8,128)S(1)} collective-permute-done((f32[256,128]{1,0:T(8,128)S(1)}, f32[256,128]{1,0:T(8,128)S(1)}, u32[]{:S(2)}, u32[]{:S(2)}) %collective-permute-start.25) | collective-permute-done | bytes 131104 | tf_op jit(solution)/shard_map/ppermute | solution.py:426
  51.1 0.9 %shard_map.172 = f32[8,72,128]{2,1,0:T(8,128)} custom-call(f32[256,128]{1,0:T(8,128)S(1)} %get-tuple-element.54.r_0_, f32[256,128]{1,0:T(8,128)S(1)} %collective-permute-done.25.r_1_, bf16[512,256]{1,0:T(8,128)(2,1)S(1)} %get-tuple-element.56.r_2_, f32[64,128]{1,0:T(8,128)S(1)} %get-tuple-element.57.r_3_), custom_call_target="tpu_custom_call" | custom-call | tf_op jit(solution)/shard_map/pallas_call | solution.py:59
  52.1 5.2 %all-to-all-start = ((f32[8,72,128]{2,1,0:T(8,128)}), f32[8,72,128]{2,1,0:T(8,128)S(1)}, u32[]{:S(2)}, u32[]{:S(2)}) async-start(f32[8,72,128]{2,1,0:T(8,128)} %shard_map.172), calls=%async_computation | async-start | bytes 589824 | tf_op jit(solution)/shard_map/all_to_all | solution.py:589
  57.3 1.6 %collective-permute-start.14 = (f32[4,32,128]{2,1,0:T(8,128)S(1)}, f32[4,32,128]{2,1,0:T(8,128)S(1)}, u32[]{:S(2)}, u32[]{:S(2)}) collective-permute-start(f32[4,32,128]{2,1,0:T(8,128)S(1)} %get-tuple-element.47), channel_id=1, source_target_pairs={{0,2},{1,3},{2,0},{3,1},{4,6},{5,7},{6,4},{7,5},{8,10},{9,11},{10,... | collective-permute-start | bytes 196616 | tf_op jit(solution)/shard_map/ppermute | solution.py:551
  58.9 2.0 %collective-permute-start.15 = (f32[4,32,128]{2,1,0:T(8,128)S(1)}, f32[4,32,128]{2,1,0:T(8,128)S(1)}, u32[]{:S(2)}, u32[]{:S(2)}) collective-permute-start(f32[4,32,128]{2,1,0:T(8,128)S(1)} %get-tuple-element.48), channel_id=1, source_target_pairs={{0,4},{1,5},{2,6},{3,7},{4,0},{5,1},{6,2},{7,3},{8,12},{9,13},{10,... | collective-permute-start | bytes 196616 | tf_op jit(solution)/shard_map/ppermute | solution.py:551
  60.9 0.8 collective-permute-done.14.b_ref
  61.7 3.1 %collective-permute-done.15.c_ref = f32[4,32,128]{2,1,0:T(8,128)S(1)} collective-permute-done((f32[4,32,128]{2,1,0:T(8,128)S(1)}, f32[4,32,128]{2,1,0:T(8,128)S(1)}, u32[]{:S(2)}, u32[]{:S(2)}) %collective-permute-start.15) | collective-permute-done | bytes 65568 | tf_op jit(solution)/shard_map/ppermute | solution.py:551
  64.8 1.4 %collective-permute-done.16.d_ref = f32[4,32,128]{2,1,0:T(8,128)S(1)} collective-permute-done((f32[4,32,128]{2,1,0:T(8,128)S(1)}, f32[4,32,128]{2,1,0:T(8,128)S(1)}, u32[]{:S(2)}, u32[]{:S(2)}) %collective-permute-start.16) | collective-permute-done | bytes 65568 | tf_op jit(solution)/shard_map/ppermute | solution.py:551
  66.2 1.6 %collective-permute-start.17 = (f32[4,32,128]{2,1,0:T(8,128)S(1)}, f32[4,32,128]{2,1,0:T(8,128)S(1)}, u32[]{:S(2)}, u32[]{:S(2)}) collective-permute-start(f32[4,32,128]{2,1,0:T(8,128)S(1)} %shard_map.167.a_ref), channel_id=1, source_target_pairs={{0,8},{4,12},{8,0},{12,4},{16,24},{20,28},{24,16},{28,20},{1,9},{5... | collective-permute-start | bytes 196616 | tf_op jit(solution)/shard_map/ppermute | solution.py:429
  67.8 2.2 %collective-permute-start.18 = (f32[4,32,128]{2,1,0:T(8,128)S(1)}, f32[4,32,128]{2,1,0:T(8,128)S(1)}, u32[]{:S(2)}, u32[]{:S(2)}) collective-permute-start(f32[4,32,128]{2,1,0:T(8,128)S(1)} %shard_map.167.a_ref), channel_id=1, source_target_pairs={{0,16},{4,20},{8,24},{12,28},{16,0},{20,4},{24,8},{28,12},{1,17},{... | collective-permute-start | bytes 196616 | tf_op jit(solution)/shard_map/ppermute | solution.py:429
  70.0 0.7 collective-permute-start.19
  70.9 3.4 %collective-permute-done.18.c_ref = f32[4,32,128]{2,1,0:T(8,128)S(1)} collective-permute-done((f32[4,32,128]{2,1,0:T(8,128)S(1)}, f32[4,32,128]{2,1,0:T(8,128)S(1)}, u32[]{:S(2)}, u32[]{:S(2)}) %collective-permute-start.18) | collective-permute-done | bytes 65568 | tf_op jit(solution)/shard_map/ppermute | solution.py:429
  74.4 1.7 %collective-permute-done.19.d_ref = f32[4,32,128]{2,1,0:T(8,128)S(1)} collective-permute-done((f32[4,32,128]{2,1,0:T(8,128)S(1)}, f32[4,32,128]{2,1,0:T(8,128)S(1)}, u32[]{:S(2)}, u32[]{:S(2)}) %collective-permute-start.19) | collective-permute-done | bytes 65568 | tf_op jit(solution)/shard_map/ppermute | solution.py:429
  76.1 0.8 collective-permute-start.20
  76.8 0.8 collective-permute-start.21
  77.6 2.0 %collective-permute-start.22 = (f32[4,32,128]{2,1,0:T(8,128)S(1)}, f32[4,32,128]{2,1,0:T(8,128)S(1)}, u32[]{:S(2)}, u32[]{:S(2)}) collective-permute-start(f32[4,32,128]{2,1,0:T(8,128)S(1)} %shard_map.168.refs_0_), channel_id=1, source_target_pairs={{0,6},{1,7},{2,4},{3,5},{4,2},{5,3},{6,0},{7,1},{8,14},{9,15},{10,... | collective-permute-start | bytes 196616 | tf_op jit(solution)/shard_map/ppermute | solution.py:551
  79.6 0.8 collective-permute-done.20.refs_1_
  80.4 0.7 collective-permute-done.21.refs_2_
  81.1 1.7 %collective-permute-done.22.refs_3_ = f32[4,32,128]{2,1,0:T(8,128)S(1)} collective-permute-done((f32[4,32,128]{2,1,0:T(8,128)S(1)}, f32[4,32,128]{2,1,0:T(8,128)S(1)}, u32[]{:S(2)}, u32[]{:S(2)}) %collective-permute-start.22) | collective-permute-done | bytes 65568 | tf_op jit(solution)/shard_map/ppermute | solution.py:551
  82.9 1.5 %collective-permute-done.23.theirs_ref = f32[512,128]{1,0:T(8,128)S(1)} collective-permute-done((f32[512,128]{1,0:T(8,128)S(1)}, f32[512,128]{1,0:T(8,128)S(1)}, u32[]{:S(2)}, u32[]{:S(2)}) %collective-permute-start.23) | collective-permute-done | bytes 262176 | tf_op jit(solution)/shard_map/ppermute | solution.py:426
  84.4 1.2 %shard_map.170 = (f32[1024,128]{1,0:T(8,128)}, f32[1024,128]{1,0:T(8,128)}) custom-call(f32[512,128]{1,0:T(8,128)S(1)} %bitcast.10, f32[512,128]{1,0:T(8,128)S(1)} %collective-permute-done.23.theirs_ref, f32[1024,128]{1,0:T(8,128)S(1)} %copy-done, f32[1024,128]{1,0:T(8,128)S(1)} %copy-done.1), custom_call_target="tpu_custom_call" | custom-call | tf_op jit(solution)/shard_map/pallas_call | solution.py:59
  85.6 1.1 %shard_map.173 = (f32[256,128]{1,0:T(8,128)}, f32[256,128]{1,0:T(8,128)}) custom-call(f32[8,72,128]{2,1,0:T(8,128)S(1)} %all-to-all-done.r_0_, f32[256,128]{1,0:T(8,128)S(1)} %copy-done.2, f32[256,128]{1,0:T(8,128)S(1)} %copy-done.3), custom_call_target="tpu_custom_call" | custom-call | tf_op jit(solution)/shard_map/pallas_call | solution.py:59
  (32 shorter events, 1.0 us)
Async XLA Ops:
  1.7 11.0 %collective-permute-start.1 = (bf16[1328,128]{1,0:T(8,128)(2,1)S(1)}, bf16[1328,128]{1,0:T(8,128)(2,1)S(1)}, u32[]{:S(2)}, u32[]{:S(2)}) collective-permute-start(bf16[1328,128]{1,0:T(8,128)(2,1)S(1)} %shard_map.158.r_0_), channel_id=1, source_target_pairs={{0,2},{1,3},{2,0},{3,1},{4,6},{5,7},{6,4},{7,5},{8,10},{9,11},{10,... | collective-permute-start | bytes 1019912 | tf_op jit(solution)/shard_map/ppermute | solution.py:426
  4.7 32.5 %collective-permute-start = (bf16[1328,128]{1,0:T(8,128)(2,1)S(1)}, bf16[1328,128]{1,0:T(8,128)(2,1)S(1)}, u32[]{:S(2)}, u32[]{:S(2)}) collective-permute-start(bf16[1328,128]{1,0:T(8,128)(2,1)S(1)} %shard_map.158.r_0_), channel_id=1, source_target_pairs={{0,1},{1,0},{2,3},{3,2},{4,5},{5,4},{6,7},{7,6},{8,9},{9,8},{10,11... | collective-permute-start | bytes 1019912 | tf_op jit(solution)/shard_map/ppermute | solution.py:426
  12.7 25.5 %collective-permute-start.2 = (bf16[1328,128]{1,0:T(8,128)(2,1)S(1)}, bf16[1328,128]{1,0:T(8,128)(2,1)S(1)}, u32[]{:S(2)}, u32[]{:S(2)}) collective-permute-start(bf16[1328,128]{1,0:T(8,128)(2,1)S(1)} %collective-permute-done.1.r_0_.r_2_), channel_id=1, source_target_pairs={{0,1},{1,0},{2,3},{3,2},{4,5},{5,4},{6,7},{7,6},{8,9},{9,8},{10,11... | collective-permute-start | bytes 1019912 | tf_op jit(solution)/shard_map/ppermute | solution.py:426
  13.6 4.6 %collective-permute-start.4 = (bf16[256,128]{1,0:T(8,128)(2,1)S(1)}, bf16[256,128]{1,0:T(8,128)(2,1)S(1)}, u32[]{:S(2)}, u32[]{:S(2)}) collective-permute-start(bf16[256,128]{1,0:T(8,128)(2,1)S(1)} %shard_map.161.refs_0_), channel_id=1, source_target_pairs={{0,8},{4,12},{8,0},{12,4},{16,24},{20,28},{24,16},{28,20},{1,9},{5... | collective-permute-start | bytes 196616 | tf_op jit(solution)/shard_map/ppermute | solution.py:429
  15.4 7.0 %collective-permute-start.6 = (bf16[256,128]{1,0:T(8,128)(2,1)S(1)}, bf16[256,128]{1,0:T(8,128)(2,1)S(1)}, u32[]{:S(2)}, u32[]{:S(2)}) collective-permute-start(bf16[256,128]{1,0:T(8,128)(2,1)S(1)} %shard_map.161.refs_0_), channel_id=1, source_target_pairs={{0,16},{4,20},{8,24},{12,28},{16,0},{20,4},{24,8},{28,12},{1,17},{... | collective-permute-start | bytes 196616 | tf_op jit(solution)/shard_map/ppermute | solution.py:429
  18.0 6.1 %collective-permute-start.8 = (bf16[256,128]{1,0:T(8,128)(2,1)S(1)}, bf16[256,128]{1,0:T(8,128)(2,1)S(1)}, u32[]{:S(2)}, u32[]{:S(2)}) collective-permute-start(bf16[256,128]{1,0:T(8,128)(2,1)S(1)} %shard_map.161.refs_0_), channel_id=1, source_target_pairs={{0,24},{4,28},{8,16},{12,20},{16,8},{20,12},{24,0},{28,4},{1,25},{... | collective-permute-start | bytes 196616 | tf_op jit(solution)/shard_map/ppermute | solution.py:429
  18.2 7.4 %collective-permute-start.3 = (bf16[256,128]{1,0:T(8,128)(2,1)S(1)}, bf16[256,128]{1,0:T(8,128)(2,1)S(1)}, u32[]{:S(2)}, u32[]{:S(2)}) collective-permute-start(bf16[256,128]{1,0:T(8,128)(2,1)S(1)} %shard_map.161.refs_0_), channel_id=1, source_target_pairs={{0,4},{4,0},{8,12},{12,8},{16,20},{20,16},{24,28},{28,24},{1,5},{5... | collective-permute-start | bytes 196616 | tf_op jit(solution)/shard_map/ppermute | solution.py:429
  22.4 5.1 %collective-permute-start.5 = (bf16[256,128]{1,0:T(8,128)(2,1)S(1)}, bf16[256,128]{1,0:T(8,128)(2,1)S(1)}, u32[]{:S(2)}, u32[]{:S(2)}) collective-permute-start(bf16[256,128]{1,0:T(8,128)(2,1)S(1)} %collective-permute-done.4.refs_2_), channel_id=1, source_target_pairs={{0,4},{4,0},{8,12},{12,8},{16,20},{20,16},{24,28},{28,24},{1,5},{5... | collective-permute-start | bytes 196616 | tf_op jit(solution)/shard_map/ppermute | solution.py:429
  24.1 4.3 %collective-permute-start.7 = (bf16[256,128]{1,0:T(8,128)(2,1)S(1)}, bf16[256,128]{1,0:T(8,128)(2,1)S(1)}, u32[]{:S(2)}, u32[]{:S(2)}) collective-permute-start(bf16[256,128]{1,0:T(8,128)(2,1)S(1)} %collective-permute-done.6.refs_4_), channel_id=1, source_target_pairs={{0,4},{4,0},{8,12},{12,8},{16,20},{20,16},{24,28},{28,24},{1,5},{5... | collective-permute-start | bytes 196616 | tf_op jit(solution)/shard_map/ppermute | solution.py:429
  25.6 4.3 %collective-permute-start.9 = (bf16[256,128]{1,0:T(8,128)(2,1)S(1)}, bf16[256,128]{1,0:T(8,128)(2,1)S(1)}, u32[]{:S(2)}, u32[]{:S(2)}) collective-permute-start(bf16[256,128]{1,0:T(8,128)(2,1)S(1)} %collective-permute-done.8.refs_6_), channel_id=1, source_target_pairs={{0,4},{4,0},{8,12},{12,8},{16,20},{20,16},{24,28},{28,24},{1,5},{5... | collective-permute-start | bytes 196616 | tf_op jit(solution)/shard_map/ppermute | solution.py:429
  30.3 4.3 %collective-permute-start.11 = (bf16[256,128]{1,0:T(8,128)(2,1)S(1)}, bf16[256,128]{1,0:T(8,128)(2,1)S(1)}, u32[]{:S(2)}, u32[]{:S(2)}) collective-permute-start(bf16[256,128]{1,0:T(8,128)(2,1)S(1)} %shard_map.162.r_2_), channel_id=1, source_target_pairs={{0,2},{1,3},{2,0},{3,1},{4,6},{5,7},{6,4},{7,5},{8,10},{9,11},{10,... | collective-permute-start | bytes 196616 | tf_op jit(solution)/shard_map/ppermute | solution.py:426
  31.9 9.3 %collective-permute-start.10 = (bf16[256,128]{1,0:T(8,128)(2,1)S(1)}, bf16[256,128]{1,0:T(8,128)(2,1)S(1)}, u32[]{:S(2)}, u32[]{:S(2)}) collective-permute-start(bf16[256,128]{1,0:T(8,128)(2,1)S(1)} %shard_map.162.r_2_), channel_id=1, source_target_pairs={{0,1},{1,0},{2,3},{3,2},{4,5},{5,4},{6,7},{7,6},{8,9},{9,8},{10,11... | collective-permute-start | bytes 196616 | tf_op jit(solution)/shard_map/ppermute | solution.py:426
  34.6 6.6 %collective-permute-start.12 = (bf16[256,128]{1,0:T(8,128)(2,1)S(1)}, bf16[256,128]{1,0:T(8,128)(2,1)S(1)}, u32[]{:S(2)}, u32[]{:S(2)}) collective-permute-start(bf16[256,128]{1,0:T(8,128)(2,1)S(1)} %collective-permute-done.11.r_4_), channel_id=1, source_target_pairs={{0,1},{1,0},{2,3},{3,2},{4,5},{5,4},{6,7},{7,6},{8,9},{9,8},{10,11... | collective-permute-start | bytes 196616 | tf_op jit(solution)/shard_map/ppermute | solution.py:426
  42.7 41.7 %copy-start = (f32[1024,128]{1,0:T(8,128)S(1)}, f32[1024,128]{1,0:T(8,128)}, u32[]{:S(2)}) copy-start(f32[1024,128]{1,0:T(8,128)} %table_ref.3) | copy-start | bytes 1572868
  42.7 41.7 %copy-start.1 = (f32[1024,128]{1,0:T(8,128)S(1)}, f32[1024,128]{1,0:T(8,128)}, u32[]{:S(2)}) copy-start(f32[1024,128]{1,0:T(8,128)} %accum_ref.1) | copy-start | bytes 1572868
  43.5 42.1 %copy-start.2 = (f32[256,128]{1,0:T(8,128)S(1)}, f32[256,128]{1,0:T(8,128)}, u32[]{:S(2)}) copy-start(f32[256,128]{1,0:T(8,128)} %r_1_.3) | copy-start | bytes 393220
  43.5 42.1 %copy-start.3 = (f32[256,128]{1,0:T(8,128)S(1)}, f32[256,128]{1,0:T(8,128)}, u32[]{:S(2)}) copy-start(f32[256,128]{1,0:T(8,128)} %r_2_.3) | copy-start | bytes 393220
  43.5 1.7 %collective-permute-start.24 = (f32[2,256,128]{2,1,0:T(8,128)S(1)}, f32[2,256,128]{2,1,0:T(8,128)S(1)}, u32[]{:S(2)}, u32[]{:S(2)}) collective-permute-start(f32[2,256,128]{2,1,0:T(8,128)S(1)} %get-tuple-element.53), channel_id=1, source_target_pairs={{0,1},{1,0},{2,3},{3,2},{4,5},{5,4},{6,7},{7,6},{8,9},{9,8},{10,11... | collective-permute-start | bytes 786440 | tf_op jit(solution)/shard_map/ppermute | solution.py:426
  44.1 13.2 %collective-permute-start.13 = (f32[512,128]{1,0:T(8,128)S(1)}, f32[512,128]{1,0:T(8,128)S(1)}, u32[]{:S(2)}, u32[]{:S(2)}) collective-permute-start(f32[512,128]{1,0:T(8,128)S(1)} %get-tuple-element.45), channel_id=1, source_target_pairs={{0,1},{1,0},{2,3},{3,2},{4,5},{5,4},{6,7},{7,6},{8,9},{9,8},{10,11... | collective-permute-start | bytes 786440 | tf_op jit(solution)/shard_map/ppermute | solution.py:426
  45.3 5.8 %collective-permute-start.25 = (f32[256,128]{1,0:T(8,128)S(1)}, f32[256,128]{1,0:T(8,128)S(1)}, u32[]{:S(2)}, u32[]{:S(2)}) collective-permute-start(f32[256,128]{1,0:T(8,128)S(1)} %get-tuple-element.55), channel_id=1, source_target_pairs={{0,2},{1,3},{2,0},{3,1},{4,6},{5,7},{6,4},{7,5},{8,10},{9,11},{10,... | collective-permute-start | bytes 393224 | tf_op jit(solution)/shard_map/ppermute | solution.py:426
  52.1 33.5 %all-to-all-start = ((f32[8,72,128]{2,1,0:T(8,128)}), f32[8,72,128]{2,1,0:T(8,128)S(1)}, u32[]{:S(2)}, u32[]{:S(2)}) async-start(f32[8,72,128]{2,1,0:T(8,128)} %shard_map.172), calls=%async_computation | async-start | bytes 589824 | tf_op jit(solution)/shard_map/all_to_all | solution.py:589
  57.3 4.4 %collective-permute-start.14 = (f32[4,32,128]{2,1,0:T(8,128)S(1)}, f32[4,32,128]{2,1,0:T(8,128)S(1)}, u32[]{:S(2)}, u32[]{:S(2)}) collective-permute-start(f32[4,32,128]{2,1,0:T(8,128)S(1)} %get-tuple-element.47), channel_id=1, source_target_pairs={{0,2},{1,3},{2,0},{3,1},{4,6},{5,7},{6,4},{7,5},{8,10},{9,11},{10,... | collective-permute-start | bytes 196616 | tf_op jit(solution)/shard_map/ppermute | solution.py:551
  58.9 5.9 %collective-permute-start.15 = (f32[4,32,128]{2,1,0:T(8,128)S(1)}, f32[4,32,128]{2,1,0:T(8,128)S(1)}, u32[]{:S(2)}, u32[]{:S(2)}) collective-permute-start(f32[4,32,128]{2,1,0:T(8,128)S(1)} %get-tuple-element.48), channel_id=1, source_target_pairs={{0,4},{1,5},{2,6},{3,7},{4,0},{5,1},{6,2},{7,3},{8,12},{9,13},{10,... | collective-permute-start | bytes 196616 | tf_op jit(solution)/shard_map/ppermute | solution.py:551
  60.9 5.3 %collective-permute-start.16 = (f32[4,32,128]{2,1,0:T(8,128)S(1)}, f32[4,32,128]{2,1,0:T(8,128)S(1)}, u32[]{:S(2)}, u32[]{:S(2)}) collective-permute-start(f32[4,32,128]{2,1,0:T(8,128)S(1)} %get-tuple-element.49), channel_id=1, source_target_pairs={{0,6},{1,7},{2,4},{3,5},{4,2},{5,3},{6,0},{7,1},{8,14},{9,15},{10,... | collective-permute-start | bytes 196616 | tf_op jit(solution)/shard_map/ppermute | solution.py:551
  66.2 4.8 %collective-permute-start.17 = (f32[4,32,128]{2,1,0:T(8,128)S(1)}, f32[4,32,128]{2,1,0:T(8,128)S(1)}, u32[]{:S(2)}, u32[]{:S(2)}) collective-permute-start(f32[4,32,128]{2,1,0:T(8,128)S(1)} %shard_map.167.a_ref), channel_id=1, source_target_pairs={{0,8},{4,12},{8,0},{12,4},{16,24},{20,28},{24,16},{28,20},{1,9},{5... | collective-permute-start | bytes 196616 | tf_op jit(solution)/shard_map/ppermute | solution.py:429
  67.8 6.6 %collective-permute-start.18 = (f32[4,32,128]{2,1,0:T(8,128)S(1)}, f32[4,32,128]{2,1,0:T(8,128)S(1)}, u32[]{:S(2)}, u32[]{:S(2)}) collective-permute-start(f32[4,32,128]{2,1,0:T(8,128)S(1)} %shard_map.167.a_ref), channel_id=1, source_target_pairs={{0,16},{4,20},{8,24},{12,28},{16,0},{20,4},{24,8},{28,12},{1,17},{... | collective-permute-start | bytes 196616 | tf_op jit(solution)/shard_map/ppermute | solution.py:429
  70.0 6.1 %collective-permute-start.19 = (f32[4,32,128]{2,1,0:T(8,128)S(1)}, f32[4,32,128]{2,1,0:T(8,128)S(1)}, u32[]{:S(2)}, u32[]{:S(2)}) collective-permute-start(f32[4,32,128]{2,1,0:T(8,128)S(1)} %shard_map.167.a_ref), channel_id=1, source_target_pairs={{0,24},{4,28},{8,16},{12,20},{16,8},{20,12},{24,0},{28,4},{1,25},{... | collective-permute-start | bytes 196616 | tf_op jit(solution)/shard_map/ppermute | solution.py:429
  76.1 4.3 %collective-permute-start.20 = (f32[4,32,128]{2,1,0:T(8,128)S(1)}, f32[4,32,128]{2,1,0:T(8,128)S(1)}, u32[]{:S(2)}, u32[]{:S(2)}) collective-permute-start(f32[4,32,128]{2,1,0:T(8,128)S(1)} %shard_map.168.refs_0_), channel_id=1, source_target_pairs={{0,2},{1,3},{2,0},{3,1},{4,6},{5,7},{6,4},{7,5},{8,10},{9,11},{10,... | collective-permute-start | bytes 196616 | tf_op jit(solution)/shard_map/ppermute | solution.py:551
  76.8 4.3 %collective-permute-start.21 = (f32[4,32,128]{2,1,0:T(8,128)S(1)}, f32[4,32,128]{2,1,0:T(8,128)S(1)}, u32[]{:S(2)}, u32[]{:S(2)}) collective-permute-start(f32[4,32,128]{2,1,0:T(8,128)S(1)} %shard_map.168.refs_0_), channel_id=1, source_target_pairs={{0,4},{1,5},{2,6},{3,7},{4,0},{5,1},{6,2},{7,3},{8,12},{9,13},{10,... | collective-permute-start | bytes 196616 | tf_op jit(solution)/shard_map/ppermute | solution.py:551
  77.6 5.2 %collective-permute-start.22 = (f32[4,32,128]{2,1,0:T(8,128)S(1)}, f32[4,32,128]{2,1,0:T(8,128)S(1)}, u32[]{:S(2)}, u32[]{:S(2)}) collective-permute-start(f32[4,32,128]{2,1,0:T(8,128)S(1)} %shard_map.168.refs_0_), channel_id=1, source_target_pairs={{0,6},{1,7},{2,4},{3,5},{4,2},{5,3},{6,0},{7,1},{8,14},{9,15},{10,... | collective-permute-start | bytes 196616 | tf_op jit(solution)/shard_map/ppermute | solution.py:551
  82.8 1.6 %collective-permute-start.23 = (f32[512,128]{1,0:T(8,128)S(1)}, f32[512,128]{1,0:T(8,128)S(1)}, u32[]{:S(2)}, u32[]{:S(2)}) collective-permute-start(f32[512,128]{1,0:T(8,128)S(1)} %bitcast.9), channel_id=1, source_target_pairs={{0,1},{1,0},{2,3},{3,2},{4,5},{5,4},{6,7},{7,6},{8,9},{9,8},{10,11... | collective-permute-start | bytes 786440 | tf_op jit(solution)/shard_map/ppermute | solution.py:426

commit v3 on v2

--- a/solution.py
+++ b/solution.py
@@ -49,9 +49,10 @@
 
 
 VM = pl.BlockSpec(memory_space=pltpu.VMEM)
-
-
-def call(body, outs, ins, scratch=(), late=()):
+ANY = pl.BlockSpec(memory_space=pl.ANY)
+
+
+def call(body, outs, ins, scratch=(), late=(), raw=()):
     avals = [
         pltpu.VMEM(shape, dtype) if stay else jax.ShapeDtypeStruct(shape, dtype)
         for shape, dtype, stay in outs
@@ -59,13 +60,15 @@
     return pl.pallas_call(
         body,
         out_shape=avals,
-        in_specs=[VM] * len(ins),
+        in_specs=[ANY if i in raw else VM for i in range(len(ins))],
         out_specs=[VM] * len(outs),
         scratch_shapes=scratch,
         compiler_params=pltpu.CompilerParams(vmem_limit_bytes=16 * 1024 * 1024),
     )(
         *[
-            pltpu.with_memory_space_constraint(x, pltpu.HBM if i in late else pltpu.VMEM)
+            pltpu.with_memory_space_constraint(
+                x, pltpu.HBM if i in late or i in raw else pltpu.VMEM
+            )
             for i, x in enumerate(ins)
         ]
     )
@@ -75,31 +78,38 @@
     return jnp.broadcast_to(row, (8, row.shape[1])).T[:, 0:1]
 
 
-def cast_kernel(table_ref, out_ref):
-    out_ref[...] = table_ref[...].astype(BF16)
-
-
-def spread_kernel(table_ref, out_ref):
+def cast_kernel(count, *refs):
+    sources, outs = refs[:count], refs[count : 2 * count]
+    table_ref, sems = refs[2 * count :]
+    copies = [
+        pltpu.make_async_copy(src, outs[i] if i else table_ref, sems.at[i])
+        for i, src in enumerate(sources)
+    ]
+    for copy in copies:
+        copy.start()
+    copies[0].wait()
     table = table_ref[...].astype(BF16)
-    for o in range(out_ref.shape[0]):
-        out_ref[o] = table
-
-
-def pack_rows(d_in, out_width, hidden, emb, item_rows):
-    starts = [0, d_in, d_in + out_width // emb * hidden]
+    if len(outs[0].shape) == 2:
+        outs[0][...] = table
+    else:
+        for o in range(outs[0].shape[0]):
+            outs[0][o] = table
+    for copy in copies[1:]:
+        copy.wait()
+
+
+def pack_rows(out_width, hidden, emb, item_rows):
+    starts = [0, out_width // emb * hidden]
     starts.append(starts[-1] + -(-item_rows // 16) * 16)
     starts.append(starts[-1] + 16)
     return starts + [starts[-1] + 16]
 
 
-def prep_kernel(at, w_ref, v_ref, items_ref, sizes_ref, bias_ref, out_ref):
+def prep_kernel(at, v_ref, items_ref, sizes_ref, bias_ref, out_ref):
     hidden, width = v_ref.shape
     emb = out_ref.shape[1]
-    out_ref[at[0] : at[1], :] = w_ref[...]
     for j in range(width // emb):
-        out_ref[at[1] + j * hidden : at[1] + (j + 1) * hidden, :] = v_ref[
-            :, j * emb : (j + 1) * emb
-        ]
+        out_ref[j * hidden : (j + 1) * hidden, :] = v_ref[:, j * emb : (j + 1) * emb]
 
     def padded(x, rows):
         if x.shape[0] == rows:
@@ -107,16 +117,29 @@
         return jnp.concatenate([x, jnp.zeros((rows - x.shape[0], emb), F32)], axis=0)
 
     items = items_ref[...].astype(F32)
-    out_ref[at[2] : at[3], :] = padded(items, at[3] - at[2]).astype(BF16)
-    out_ref[at[3] : at[4], :] = padded(sizes_ref[...].astype(F32), 16).astype(BF16)
+    out_ref[at[1] : at[2], :] = padded(items, at[2] - at[1]).astype(BF16)
+    out_ref[at[2] : at[3], :] = padded(sizes_ref[...].astype(F32), 16).astype(BF16)
     bias = bias_ref[...]
     hi = bias.astype(BF16).astype(F32)
     mid = (bias - hi).astype(BF16).astype(F32)
     low = bias - hi - mid
-    out_ref[at[4] : at[5], :] = padded(jnp.concatenate([hi, mid, low], axis=0), 16).astype(BF16)
-
-
-def place_kernel(mp_count, slots, map_ref, ids_ref, pos_ref):
+    out_ref[at[3] : at[4], :] = padded(jnp.concatenate([hi, mid, low], axis=0), 16).astype(BF16)
+
+
+def place_kernel(
+    mp_count, slots, share, map_ref, ids_ref, hot_hbm, hot_ids_hbm, weight_hbm, grads_hbm,
+    pos_ref, row_ref, hot_ref, hot_ids_ref, weight_ref, grads_ref, sems,
+):
+    my = lax.axis_index("mp")
+    mine = grads_hbm.at[pl.ds(pl.multiple_of(my * share, share), share), :]
+    copies = [
+        pltpu.make_async_copy(hot_hbm, hot_ref, sems.at[0]),
+        pltpu.make_async_copy(hot_ids_hbm, hot_ids_ref, sems.at[1]),
+        pltpu.make_async_copy(weight_hbm, weight_ref, sems.at[2]),
+        pltpu.make_async_copy(mine, grads_ref, sems.at[3]),
+    ]
+    for copy in copies:
+        copy.start()
     touch = ids_ref.shape[1]
     map_rows, lanes = map_ref.shape
     ids_col = column(ids_ref[...])
@@ -128,7 +151,11 @@
     in_lane = iota((touch, lanes), 1) == ids_col % lanes
     stored = jnp.sum(jnp.where(in_lane, picked, 0.0), axis=1, keepdims=True).astype(I32)
     stored = jnp.broadcast_to(stored, (touch, lanes))
-    pos_ref[...] = stored // (mp_count * slots) * slots + stored % slots
+    pos = stored // (mp_count * slots) * slots + stored % slots
+    pos_ref[...] = pos
+    row_ref[...] = pos.T[:8, :]
+    for copy in copies:
+        copy.wait()
 
 
 def count_kernel(
@@ -143,7 +170,7 @@
     upto = (iota((lanes, lanes), 0) <= iota((lanes, lanes), 1)).astype(F32).astype(BF16)
     packs = (p0, p1)
     for k, pack in enumerate(packs):
-        sizes = pack[at[3] : at[4], :]
+        sizes = pack[at[2] : at[3], :]
         ends = dot(sizes, upto)[:count_rows]
         sizes = sizes.astype(F32)[:count_rows]
         totals = jnp.broadcast_to(jnp.sum(sizes, axis=1, keepdims=True), ends.shape)
@@ -152,7 +179,7 @@
             ends = ends + jnp.where(row > r, totals[r : r + 1, :], 0.0)
         ends_ref[k] = ends
         starts_ref[k] = ends - sizes
-        items_ref[k] = pack[at[2] : at[3], :].astype(F32)[:item_rows]
+        items_ref[k] = pack[at[1] : at[2], :].astype(F32)[:item_rows]
 
     def rows_of(ref, k):
         return jnp.concatenate([ref[k, pl.ds(my * per + j, 1), :] for j in range(per)], axis=1)
@@ -191,47 +218,56 @@
 
 
 def pre_kernel(
-    share, at, hidden, p0, p1, p2, p3, grads_ref, rows_ref, wt_ref, tail_ref, pre_ref, back_ref
+    share, at, hidden, w0, w1, w2, w3, p0, p1, p2, p3, grads_ref, rows_ref,
+    wt_ref, tail_ref, pre_ref, back_ref,
 ):
-    my = lax.axis_index("mp")
     emb = p0.shape[1]
     hot_cols = rows_ref.shape[0]
-    grads = grads_ref[pl.ds(pl.multiple_of(my * share, share), share), :]
+    grads = grads_ref[...]
     rows = rows_ref[...]
-    for k, p in enumerate((p0, p1, p2, p3)):
+    for k, (w, p) in enumerate(zip((w0, w1, w2, w3), (p0, p1, p2, p3))):
         cols = slice(k * hidden, (k + 1) * hidden)
-        bias = jnp.sum(p[at[4] : at[5], :].astype(F32), axis=0, keepdims=True)
-        pre_ref[:, cols] = dot(rows, p[:hot_cols, :], TN) + bias
+        bias = jnp.sum(p[at[3] : at[4], :].astype(F32), axis=0, keepdims=True)
+        pre_ref[:, cols] = dot(rows, w[:hot_cols, :], TN) + bias
         back = jnp.zeros((share, hidden), F32)
         for j in range(grads.shape[1] // emb):
-            piece = p[at[1] + j * hidden : at[1] + (j + 1) * hidden, :]
+            piece = p[j * hidden : (j + 1) * hidden, :]
             back = back + dot(grads[:, j * emb : (j + 1) * emb], piece, NT)
         back_ref[:, cols] = back
-        tail_ref[:, cols] = p[hot_cols : at[1], :]
-        wt_ref[cols, :] = p[: at[1], :].astype(F32).T.astype(BF16)
+        tail_ref[:, cols] = w[hot_cols:, :]
+        wt_ref[cols, :] = w[...].astype(F32).T.astype(BF16)
 
 
 def fetch_kernel(pos_ref, table_ref, out_ref):
     owners, slots, _ = table_ref.shape
 
     def body(o, acc):
-        return acc + dot(hits(pos_ref, o * slots, slots), table_ref[o])
+        return acc + dot(hits(pos_ref[...], o * slots, slots), table_ref[o])
 
     out_ref[...] = loop(owners, body, jnp.zeros(out_ref.shape, F32)).astype(BF16)
 
 
-def fetch_near_kernel(pos_ref, *refs):
-    out_ref = refs[-1]
-    slots = refs[0].shape[0]
+def fetch_near_kernel(pos_ref, row_ref, *refs):
+    tables, (mine_ref, give_ref) = refs[:-2], refs[-2:]
+    touch, lanes = pos_ref.shape
+    slots = tables[0].shape[0]
     my = lax.axis_index("dp")
-    acc = jnp.zeros(out_ref.shape, F32)
-    for k, table in enumerate(refs[:-1]):
-        acc = acc + dot(hits(pos_ref, (my ^ k) * slots, slots), table[...])
-    out_ref[...] = acc.astype(BF16)
-
-
-def hits(pos_ref, first, slots):
-    rel = pos_ref[...] - first
+    theirs = jnp.broadcast_to(row_ref[...].T[:, 0:1], (touch, lanes))
+    both = jnp.concatenate([pos_ref[...], theirs], axis=0)
+    acc = jnp.zeros((2 * touch, mine_ref.shape[1]), F32)
+    for k, table in enumerate(tables):
+        acc = acc + dot(hits(both, (my ^ (2 * k)) * slots, slots), table[...])
+    mine_ref[...] = acc[:touch].astype(BF16)
+    give_ref[...] = acc[touch:].astype(BF16)
+
+
+def join_kernel(mine_ref, near_ref, far_ref, cross_ref, out_ref):
+    out_ref[0] = (mine_ref[...].astype(F32) + near_ref[...].astype(F32)).astype(BF16)
+    out_ref[1] = (far_ref[...].astype(F32) + cross_ref[...].astype(F32)).astype(BF16)
+
+
+def hits(pos, first, slots):
+    rel = pos - first
     lane = iota(rel.shape, 1)
     lanes = rel.shape[1]
     return jnp.concatenate(
@@ -239,9 +275,7 @@
     )
 
 
-def onehot_kernel(
-    share, fields, slots, cap, ids_ref, pos_ref, hot_ref, out_ref, q_ref, srow_ref, rows_ref
-):
+def onehot_kernel(share, fields, ids_ref, hot_ref, out_ref, rows_ref):
     my = lax.axis_index("mp")
     emb = hot_ref.shape[1]
     hot = hot_ref[...].T.astype(BF16)
@@ -251,6 +285,9 @@
         hit = (sub == mine).astype(F32).astype(BF16)
         out_ref[:, f * share : (f + 1) * share] = hit
         rows_ref[f * emb : (f + 1) * emb, :] = dot(hot, hit).astype(BF16)
+
+
+def bucket_kernel(slots, cap, pos_ref, q_ref, srow_ref):
     pos = pos_ref[...]
     touch, lanes = pos.shape
     row = pos.T[0:1, :]
@@ -272,16 +309,17 @@
 
 
 def main_kernel(
-    fields, cnta_ref, cntb_ref, f0, f1, f2, f3, pre_ref, back_ref, tail_ref, wt_ref, oht_ref,
+    fields, cnta_ref, cntb_ref, mine_ref, core_ref, pre_ref, back_ref, tail_ref, wt_ref, oht_ref,
     ig_ref, bag_ref, send_ref,
 ):
-    touch, emb = f0.shape
+    _, touch, emb = mine_ref.shape
     share = cnta_ref.shape[0]
     core = lax.axis_index("mp") % 2
     pooled = jnp.zeros((share, emb), F32)
-    for k, f in enumerate((f0, f1, f2, f3)):
+    for k in range(4):
         cnt = (cnta_ref, cntb_ref)[k // 2]
-        pooled = pooled + dot(cnt[:, k % 2 * touch : (k % 2 + 1) * touch], f[...])
+        rows = (mine_ref, core_ref)[k % 2][k // 2]
+        pooled = pooled + dot(cnt[:, k % 2 * touch : (k % 2 + 1) * touch], rows)
     pre = pre_ref[...] + dot(pooled.astype(BF16), tail_ref[...])
     sig = jax.nn.sigmoid(pre)
     hidden = (back_ref[...] * sig * (1.0 + pre * (1.0 - sig))).astype(BF16)
@@ -428,45 +466,65 @@
     def far_swap(x, mask):
         return lax.ppermute(x, "dp", [(i, i ^ mask) for i in range(dp_count)])
 
+    def near_swap(x, k):
+        mask = k // 2 * mp_count + k % 2 * 2
+        return lax.ppermute(
+            x, both, [(i, i ^ mask) for i in range(dp_count * mp_count)]
+        )
+
     near = dp_count == 8 and mp_count == 4
 
+    small = [
+        owner_map.reshape(-1, emb),
+        touched.reshape(1, touch),
+        weight_out,
+        cold_items.reshape(item_rows, emb),
+        bag_counts.reshape(count_rows, emb),
+        bias_in.reshape(1, hidden),
+    ]
+    own, *small = call(
+        lambda *r: cast_kernel(1 + len(small), *r),
+        [((slots, emb) if near else (dp_count, slots, emb), BF16, near)]
+        + [(x.shape, x.dtype, True) for x in small],
+        [cold_table, *small],
+        raw=range(1 + len(small)),
+        scratch=[
+            pltpu.VMEM((slots, emb), F32),
+            pltpu.SemaphoreType.DMA((1 + len(small),)),
+        ],
+    )
+    map_rows, touched_row, *small = small
     if near:
-        (own,) = call(cast_kernel, [((slots, emb), BF16, True)], [cold_table], late=(0,))
-        tables = [own] + [None] * 7
-        for k in (4, 6, 2):
-            tables[k] = far_swap(own, k)
-        for k in (0, 4, 6, 2):
-            tables[k + 1] = far_swap(tables[k], 1)
+        tables = [own]
+        for k in (2, 4, 6):
+            tables.append(far_swap(own, k))
     else:
-        (mine,) = call(
-            spread_kernel, [((dp_count, slots, emb), BF16, False)], [cold_table], late=(0,)
-        )
-        tables = [lax.all_to_all(mine, "dp", split_axis=0, concat_axis=0, tiled=True)]
-
-    at = pack_rows(d_in, weight_out.shape[1], hidden, emb, item_rows)
-    (pack,) = call(
-        lambda *r: prep_kernel(at, *r),
-        [((at[-1], emb), BF16, True)],
-        [
-            weight_in,
-            weight_out,
-            cold_items.reshape(item_rows, emb),
-            bag_counts.reshape(count_rows, emb),
-            bias_in.reshape(1, hidden),
-        ],
-        late=range(5),
-    )
+        tables = lax.all_to_all(own, "dp", split_axis=0, concat_axis=0, tiled=True)
+
+    w_far = swap(weight_in, 2)
+    w_near = swap(weight_in, 1)
+    weights = [weight_in, w_near, w_far, swap(w_far, 1)]
+    at = pack_rows(weight_out.shape[1], hidden, emb, item_rows)
+    (pack,) = call(lambda *r: prep_kernel(at, *r), [((at[-1], emb), BF16, True)], small)
     pack_far = swap(pack, 2)
     pack_near = swap(pack, 1)
-    pack_cross = swap(pack_far, 1)
-    packs = [pack, pack_near, pack_far, pack_cross]
-
-    (pos,) = call(
-        lambda *r: place_kernel(mp_count, slots, *r),
-        [((touch, emb), I32, True)],
-        [owner_map.reshape(-1, emb), touched.reshape(1, touch)],
-        late=range(2),
-    )
+    packs = [pack, pack_near, pack_far, swap(pack_far, 1)]
+
+    pos, pos_row, hot_near, ids_near, weight_near, grads_near = call(
+        lambda *r: place_kernel(mp_count, slots, share, *r),
+        [
+            ((touch, emb), I32, True),
+            ((8, touch), I32, True),
+            (hot_table.shape, F32, True),
+            ((fields, samples), I32, True),
+            (weight_in.shape, BF16, True),
+            ((share, grad_out.shape[1]), BF16, True),
+        ],
+        [map_rows, touched_row, hot_table, hot_ids.T, weight_in, grad_out],
+        raw=range(2, 6),
+        scratch=[pltpu.SemaphoreType.DMA((4,))],
+    )
+    weights[0] = weight_near
 
     def count(pair):
         return call(
@@ -484,16 +542,10 @@
     cnta, cntta = count(packs[:2])
     cntb, cnttb = count(packs[2:])
 
-    oht, q_mat, slot_rows, rows = call(
-        lambda *r: onehot_kernel(share, fields, slots, cap, *r),
-        [
-            ((hot_rows, fields * share), BF16, True),
-            ((dp_count * cap, touch), BF16, True),
-            ((dp_count * 8, emb), F32, True),
-            ((fields * emb, share), BF16, True),
-        ],
-        [hot_ids.T, pos, hot_table],
-        late=(0, 2),
+    oht, rows = call(
+        lambda *r: onehot_kernel(share, fields, *r),
+        [((hot_rows, fields * share), BF16, True), ((fields * emb, share), BF16, True)],
+        [ids_near, hot_near],
     )
 
     wt, tail, pre, back = call(
@@ -504,18 +556,24 @@
             ((share, all_hidden), F32, True),
             ((share, all_hidden), F32, True),
         ],
-        [*packs, grad_out, rows],
-        late=(4,),
-    )
-
-    (fetched,) = call(
-        fetch_near_kernel if near else fetch_kernel,
-        [((touch, emb), BF16, True)],
-        [pos, *tables],
-        late=() if near else (1,),
-    )
-    far = swap(fetched, 2)
-    around = [fetched, swap(fetched, 1), far, swap(far, 1)]
+        [*weights, *packs, grads_near, rows],
+    )
+
+    if near:
+        other_row = far_swap(pos_row, 1)
+        mine, give = call(
+            fetch_near_kernel, [((touch, emb), BF16, True)] * 2, [pos, other_row, *tables]
+        )
+        from_near = near_swap(give, 2)
+        from_far = near_swap(mine, 1)
+        from_cross = near_swap(give, 3)
+        (fetched,) = call(
+            join_kernel, [((2, touch, emb), BF16, True)], [mine, from_near, from_far, from_cross]
+        )
+    else:
+        (mine,) = call(fetch_kernel, [((touch, emb), BF16, True)], [pos, tables], late=(1,))
+        fetched = jnp.stack([mine, swap(mine, 2)])
+    fetched_core = swap(fetched, 1)
 
     half_rows = hot_rows // 2
     ig, bag, hot_send = call(
@@ -525,7 +583,7 @@
             ((share, 2 * emb), BF16, True),
             ((half_rows, emb), F32, True),
         ],
-        [cnta, cntb, *around, pre, back, tail, wt, oht],
+        [cnta, cntb, fetched, fetched_core, pre, back, tail, wt, oht],
     )
     hot_got = swap(hot_send, 1)
     hot_keep, touch_send, touch_keep = call(
@@ -544,12 +602,6 @@
     def exchange(x):
         return lax.all_to_all(
             x, both, split_axis=0, concat_axis=0, tiled=True, axis_index_groups=rank_groups
-        )
-
-    def near_swap(x, k):
-        mask = k // 2 * mp_count + k % 2 * 2
-        return lax.ppermute(
-            x, both, [(i, i ^ mask) for i in range(dp_count * mp_count)]
         )
 
     if near:
@@ -578,6 +630,11 @@
         final_kernel, [(hot_table.shape, F32, False)] * 2, [half, other, hot_table, hot_accum]
     )
 
+    q_mat, slot_rows = call(
+        lambda *r: bucket_kernel(slots, cap, *r),
+        [((dp_count * cap, touch), BF16, True), ((dp_count * 8, emb), F32, True)],
+        [pos],
+    )
     touch_got = swap(touch_send, 1)
     mine, give = call(pair_kernel, [((touch, emb), F32, True)] * 2, [touch_keep, touch_got])
     got = swap(give, 2)

time: 87.1 us -> 74.2 us (0.85)
  waiting for transfers between devices: 36.7 us -> 27.1 us
  Pallas kernels: 15.9 us -> 13.2 us
    ppermute x10 -> x11, waiting for transfers between devices: 17.6 us -> 7.34 us  [swap(): return lax.ppermute(x, 'mp', [(i, i ^ mask) for i in range(mp_count)])]
    ppermute x10 -> x7, starting transfers between devices: 14.1 us -> 10.5 us  [far_swap(): return lax.ppermute(x, 'dp', [(i, i ^ mask) for i in range(dp_count)])]
    ppermute x6 -> x9, starting transfers between devices: 7.12 us -> 10.7 us  [near_swap(): lax.ppermute(x, both, [(i, i ^ mask) for i in range(dp_count * mp_count)])]
    ppermute x6 -> x9, waiting for transfers between devices: 8.41 us -> 11.8 us  [near_swap(): lax.ppermute(x, both, [(i, i ^ mask) for i in range(dp_count * mp_count)])]
    pallas_call x18 -> x20, Pallas kernels: 15.9 us -> 13.2 us  [call(): pl.pallas_call(body, out_shape=avals, in_specs=[ANY if i in raw else VM f...]
    ppermute x10 -> x7, waiting for transfers between devices: 10.6 us -> 7.97 us  [far_swap(): return lax.ppermute(x, 'dp', [(i, i ^ mask) for i in range(dp_count)])]
    ppermute x10 -> x11, starting transfers between devices: 6.88 us -> 6.12 us  [swap(): return lax.ppermute(x, 'mp', [(i, i ^ mask) for i in range(mp_count)])]
  transfers between devices with their start and end apart: 27 -> 28, of which waited for: 19 -> 17; matrix products, arithmetic and copies ran while one was open for 0% -> 0% of each run, Pallas kernels for 13% -> 13%
where the time goes in v3:
time: 74.2 us; the launch traced here: 73.9 us
  starting transfers between devices  32.8 us (44%)
  waiting for transfers between devices  27.1 us (37%)
  Pallas kernels  13.2 us (18%)
  between operations  0.85 us (1%)
    pallas_call x20, Pallas kernels, call(): pl.pallas_call(body, out_shape=avals, in_specs=[ANY if i in raw else VM f...  13.2 us
    ppermute x9, waiting for transfers between devices, near_swap(): lax.ppermute(x, both, [(i, i ^ mask) for i in range(dp_count * mp_count)])  11.8 us
    ppermute x9, starting transfers between devices, near_swap(): lax.ppermute(x, both, [(i, i ^ mask) for i in range(dp_count * mp_count)])  10.7 us
    ppermute x7, starting transfers between devices, far_swap(): return lax.ppermute(x, 'dp', [(i, i ^ mask) for i in range(dp_count)])  10.5 us
    ppermute x7, waiting for transfers between devices, far_swap(): return lax.ppermute(x, 'dp', [(i, i ^ mask) for i in range(dp_count)])  7.97 us
    ppermute x11, waiting for transfers between devices, swap(): return lax.ppermute(x, 'mp', [(i, i ^ mask) for i in range(mp_count)])  7.34 us
    ppermute x11, starting transfers between devices, swap(): return lax.ppermute(x, 'mp', [(i, i ^ mask) for i in range(mp_count)])  6.12 us
    all_to_all x1, starting transfers between devices, per_device(): lax.all_to_all(outgoing, 'dp', split_axis=0, concat_axis=0, tiled=True)  5.5 us
  transfers between devices with their start and end apart: 28, of which 17 were waited for; matrix products, arithmetic and copies ran while one was open for 0% of the time, Pallas kernels for 13%

profile of v3, /device:TPU:0, one launch (start us, length us, event | category | flops | bytes accessed | tf_op | source)
XLA Modules:
  0.0 73.9 jit_solution(11734725362700882667)
XLA Ops:
  0.6 3.0 %collective-permute-start.12 = (bf16[1024,128]{1,0:T(8,128)(2,1)}, bf16[1024,128]{1,0:T(8,128)(2,1)S(1)}, u32[]{:S(2)}, u32[]{:S(2)}) collective-permute-start(bf16[1024,128]{1,0:T(8,128)(2,1)} %r_4_.1), channel_id=1, source_target_pairs={{0,2},{1,3},{2,0},{3,1},{4,6},{5,7},{6,4},{7,5},{8,10},{9,11},{10,... | collective-permute-start | bytes 786440 | tf_op jit(solution)/shard_map/ppermute | solution.py:464
  3.7 1.0 %shard_map.156 = (bf16[256,128]{1,0:T(8,128)(2,1)S(1)}, s32[64,128]{1,0:T(8,128)S(1)}, s32[1,256]{1,0:T(1,128)S(1)}, bf16[128,256]{1,0:T(8,128)(2,1)S(1)}, s32[1...) custom-call(f32[256,128]{1,0:T(8,128)} %r_1_.1, s32[64,128]{1,0:T(8,128)} %bitcast.14, ...), custom_call_target="tpu_custom_call" | custom-call | tf_op jit(solution)/shard_map/pallas_call | solution.py:60
  4.7 1.6 %collective-permute-start.4 = (bf16[256,128]{1,0:T(8,128)(2,1)S(1)}, bf16[256,128]{1,0:T(8,128)(2,1)S(1)}, u32[]{:S(2)}, u32[]{:S(2)}) collective-permute-start(bf16[256,128]{1,0:T(8,128)(2,1)S(1)} %get-tuple-element.60.refs_0_), channel_id=1, source_target_pairs={{0,8},{4,12},{8,0},{12,4},{16,24},{20,28},{24,16},{28,20},{1,9},{5... | collective-permute-start | bytes 196616 | tf_op jit(solution)/shard_map/ppermute | solution.py:467
  6.3 2.6 %collective-permute-start.5 = (bf16[256,128]{1,0:T(8,128)(2,1)S(1)}, bf16[256,128]{1,0:T(8,128)(2,1)S(1)}, u32[]{:S(2)}, u32[]{:S(2)}) collective-permute-start(bf16[256,128]{1,0:T(8,128)(2,1)S(1)} %get-tuple-element.60.refs_0_), channel_id=1, source_target_pairs={{0,16},{4,20},{8,24},{12,28},{16,0},{20,4},{24,8},{28,12},{1,17},{... | collective-permute-start | bytes 196616 | tf_op jit(solution)/shard_map/ppermute | solution.py:467
  9.1 1.3 %shard_map.157 = (s32[256,128]{1,0:T(8,128)S(1)}, s32[8,256]{1,0:T(8,128)S(1)}, f32[1024,128]{1,0:T(8,128)S(1)}, s32[7,1024]{1,0:T(8,128)S(1)}, bf16[1024,128]{1...) custom-call(s32[64,128]{1,0:T(8,128)S(1)} %get-tuple-element.47.r_0_, s32[1,256]{1,0:T(1,128)S(1)} %get-tuple-element.48.r_1_, ...), custom_call_target="tpu_custom_call" | custom-call | tf_op jit(solution)/shard_map/pallas_call | solution.py:60
  10.4 1.6 %collective-permute-start.3 = (s32[8,256]{1,0:T(8,128)S(1)}, s32[8,256]{1,0:T(8,128)S(1)}, u32[]{:S(2)}, u32[]{:S(2)}) collective-permute-start(s32[8,256]{1,0:T(8,128)S(1)} %get-tuple-element.59), channel_id=1, source_target_pairs={{0,4},{4,0},{8,12},{12,8},{16,20},{20,16},{24,28},{28,24},{1,5},{5... | collective-permute-start | bytes 24584 | tf_op jit(solution)/shard_map/ppermute | solution.py:467
  12.0 2.1 %collective-permute-done.3.row_ref = s32[8,256]{1,0:T(8,128)S(1)} collective-permute-done((s32[8,256]{1,0:T(8,128)S(1)}, s32[8,256]{1,0:T(8,128)S(1)}, u32[]{:S(2)}, u32[]{:S(2)}) %collective-permute-start.3) | collective-permute-done | bytes 8224 | tf_op jit(solution)/shard_map/ppermute | solution.py:467
  15.0 0.6 shard_map.162
  15.6 1.6 %collective-permute-start.7 = (bf16[256,128]{1,0:T(8,128)(2,1)S(1)}, bf16[256,128]{1,0:T(8,128)(2,1)S(1)}, u32[]{:S(2)}, u32[]{:S(2)}) collective-permute-start(bf16[256,128]{1,0:T(8,128)(2,1)S(1)} %get-tuple-element.62), channel_id=1, source_target_pairs={{0,4},{1,5},{2,6},{3,7},{4,0},{5,1},{6,2},{7,3},{8,12},{9,13},{10,... | collective-permute-start | bytes 196616 | tf_op jit(solution)/shard_map/ppermute | solution.py:471
  17.2 0.5 collective-permute-start.8
  17.7 1.4 %collective-permute-start.9 = (bf16[256,128]{1,0:T(8,128)(2,1)S(1)}, bf16[256,128]{1,0:T(8,128)(2,1)S(1)}, u32[]{:S(2)}, u32[]{:S(2)}) collective-permute-start(bf16[256,128]{1,0:T(8,128)(2,1)S(1)} %get-tuple-element.62), channel_id=1, source_target_pairs={{0,6},{1,7},{2,4},{3,5},{4,2},{5,3},{6,0},{7,1},{8,14},{9,15},{10,... | collective-permute-start | bytes 196616 | tf_op jit(solution)/shard_map/ppermute | solution.py:471
  19.2 0.8 %collective-permute-done.7.near_ref = bf16[256,128]{1,0:T(8,128)(2,1)S(1)} collective-permute-done((bf16[256,128]{1,0:T(8,128)(2,1)S(1)}, bf16[256,128]{1,0:T(8,128)(2,1)S(1)}, u32[]{:S(2)}, u32[]{:S(2)}) %collective-permute-start.7) | collective-permute-done | bytes 65568 | tf_op jit(solution)/shard_map/ppermute | solution.py:471
  19.9 0.5 collective-permute-start.1
  20.5 1.4 %collective-permute-done.8.far_ref = bf16[256,128]{1,0:T(8,128)(2,1)S(1)} collective-permute-done((bf16[256,128]{1,0:T(8,128)(2,1)S(1)}, bf16[256,128]{1,0:T(8,128)(2,1)S(1)}, u32[]{:S(2)}, u32[]{:S(2)}) %collective-permute-start.8) | collective-permute-done | bytes 65568 | tf_op jit(solution)/shard_map/ppermute | solution.py:471
  21.8 1.7 %collective-permute-done.9.cross_ref = bf16[256,128]{1,0:T(8,128)(2,1)S(1)} collective-permute-done((bf16[256,128]{1,0:T(8,128)(2,1)S(1)}, bf16[256,128]{1,0:T(8,128)(2,1)S(1)}, u32[]{:S(2)}, u32[]{:S(2)}) %collective-permute-start.9) | collective-permute-done | bytes 65568 | tf_op jit(solution)/shard_map/ppermute | solution.py:471
  24.3 1.2 %shard_map.158 = (bf16[1024,1792]{1,0:T(8,128)(2,1)S(1)}, bf16[896,256]{1,0:T(8,128)(2,1)S(1)}) custom-call(s32[7,1024]{1,0:T(8,128)S(1)} %get-tuple-element.49.r_0_, f32[1024,128]{1,0:T(8,128)S(1)} %get-tuple-element.50.r_1_), custom_call_target="tpu_custom_call" | custom-call | tf_op jit(solution)/shard_map/pallas_call | solution.py:60
  25.5 1.0 %shard_map.160 = (bf16[256,512]{1,0:T(8,128)(2,1)S(1)}, bf16[512,256]{1,0:T(8,128)(2,1)S(1)}) custom-call(bf16[304,128]{1,0:T(8,128)(2,1)S(1)} %shard_map.159.r_0_.r_4_, bf16[304,128]{1,0:T(8,128)(2,1)S(1)} %collective-permute-done.r_1_.r_5_), custom_call_target="tpu_custom_call" | custom-call | tf_op jit(solution)/shard_map/pallas_call | solution.py:60
  26.6 1.0 %shard_map.161 = (bf16[256,512]{1,0:T(8,128)(2,1)S(1)}, bf16[512,256]{1,0:T(8,128)(2,1)S(1)}) custom-call(bf16[304,128]{1,0:T(8,128)(2,1)S(1)} %collective-permute-done.1.r_0_.r_6_, bf16[304,128]{1,0:T(8,128)(2,1)S(1)} %collective-permute-done.2.r_1_.r_7_), custom_call_target="tpu_custom_call" | custom-call | tf_op jit(solution)/shard_map/pallas_call | solution.py:60
  27.6 0.8 %shard_map.164 = (bf16[512,1024]{1,0:T(8,128)(2,1)S(1)}, bf16[128,512]{1,0:T(8,128)(2,1)S(1)}, f32[256,512]{1,0:T(8,128)S(1)}, f32[256,512]{1,0:T(8,128)S(1)}) custom-call(bf16[1024,128]{1,0:T(8,128)(2,1)S(1)} %get-tuple-element.63.r_0_, bf16[1024,128]{1,0:T(8,128)(2,1)S(1)} %collective-permute-done.11.r_1_, ...), custom_call_target="tpu_custom_call" | custom-call | tf_op jit(solution)/shard_map/pallas_call | solution.py:60
  28.5 1.5 %shard_map.165 = (bf16[1792,256]{1,0:T(8,128)(2,1)S(1)}, bf16[256,256]{1,0:T(8,128)(2,1)S(1)}, f32[512,128]{1,0:T(8,128)S(1)}) custom-call(bf16[256,512]{1,0:T(8,128)(2,1)S(1)} %get-tuple-element.56.r_0_, bf16[256,512]{1,0:T(8,128)(2,1)S(1)} %get-tuple-element.57.r_1_, bf16[2,256,128]{2,1,0:T(8,128)(2,1)S(1)} %shard_map.163.r_2_, ...), custom_call_target="tpu_custom_call" | custom-call | tf_op jit(solution)/shard_map/pallas_call | solution.py:60
  30.0 0.8 %shard_map.166 = (f32[512,128]{1,0:T(8,128)S(1)}, f32[2,256,128]{2,1,0:T(8,128)S(1)}, f32[2,256,128]{2,1,0:T(8,128)S(1)}) custom-call(bf16[1024,1792]{1,0:T(8,128)(2,1)S(1)} %get-tuple-element.51.r_8_.oht_ref, bf16[1792,256]{1,0:T(8,128)(2,1)S(1)} %get-tuple-element.70.ig_ref, bf16[256,256]{1,0:T(8,128)(2,1)S(1)} %get-tuple-element.71.bag_ref, ...), custom_call_target="tpu_custom_call" | custom-call | tf_op jit(solution)/shard_map/pallas_call | solution.py:60
  30.8 0.6 collective-permute-start.25
  31.4 1.1 %collective-permute-done.25.got_ref = f32[2,256,128]{2,1,0:T(8,128)S(1)} collective-permute-done((f32[2,256,128]{2,1,0:T(8,128)S(1)}, f32[2,256,128]{2,1,0:T(8,128)S(1)}, u32[]{:S(2)}, u32[]{:S(2)}) %collective-permute-start.25) | collective-permute-done | bytes 262176 | tf_op jit(solution)/shard_map/ppermute | solution.py:464
  32.6 0.7 %collective-permute-start.26 = (f32[256,128]{1,0:T(8,128)S(1)}, f32[256,128]{1,0:T(8,128)S(1)}, u32[]{:S(2)}, u32[]{:S(2)}) collective-permute-start(f32[256,128]{1,0:T(8,128)S(1)} %get-tuple-element.85), channel_id=1, source_target_pairs={{0,2},{1,3},{2,0},{3,1},{4,6},{5,7},{6,4},{7,5},{8,10},{9,11},{10,... | collective-permute-start | bytes 393224 | tf_op jit(solution)/shard_map/ppermute | solution.py:464
  33.3 0.5 shard_map.173
  33.9 4.5 %collective-permute-done.26.r_1_ = f32[256,128]{1,0:T(8,128)S(1)} collective-permute-done((f32[256,128]{1,0:T(8,128)S(1)}, f32[256,128]{1,0:T(8,128)S(1)}, u32[]{:S(2)}, u32[]{:S(2)}) %collective-permute-start.26) | collective-permute-done | bytes 131104 | tf_op jit(solution)/shard_map/ppermute | solution.py:464
  38.4 0.9 %shard_map.174 = f32[8,72,128]{2,1,0:T(8,128)} custom-call(f32[256,128]{1,0:T(8,128)S(1)} %get-tuple-element.84.r_0_, f32[256,128]{1,0:T(8,128)S(1)} %collective-permute-done.26.r_1_, bf16[512,256]{1,0:T(8,128)(2,1)S(1)} %get-tuple-element.86.r_2_, f32[64,128]{1,0:T(8,128)S(1)} %get-tuple-element.87.r_3_), custom_call_target="tpu_custom_call" | custom-call | tf_op jit(solution)/shard_map/pallas_call | solution.py:60
  39.4 5.5 %all-to-all-start = ((f32[8,72,128]{2,1,0:T(8,128)}), f32[8,72,128]{2,1,0:T(8,128)S(1)}, u32[]{:S(2)}, u32[]{:S(2)}) async-start(f32[8,72,128]{2,1,0:T(8,128)} %shard_map.174), calls=%async_computation | async-start | bytes 589824 | tf_op jit(solution)/shard_map/all_to_all | solution.py:646
  44.9 0.6 collective-permute-start.15
  45.5 2.0 %collective-permute-start.16 = (f32[4,32,128]{2,1,0:T(8,128)S(1)}, f32[4,32,128]{2,1,0:T(8,128)S(1)}, u32[]{:S(2)}, u32[]{:S(2)}) collective-permute-start(f32[4,32,128]{2,1,0:T(8,128)S(1)} %get-tuple-element.78), channel_id=1, source_target_pairs={{0,4},{1,5},{2,6},{3,7},{4,0},{5,1},{6,2},{7,3},{8,12},{9,13},{10,... | collective-permute-start | bytes 196616 | tf_op jit(solution)/shard_map/ppermute | solution.py:471
  47.5 0.9 %collective-permute-start.17 = (f32[4,32,128]{2,1,0:T(8,128)S(1)}, f32[4,32,128]{2,1,0:T(8,128)S(1)}, u32[]{:S(2)}, u32[]{:S(2)}) collective-permute-start(f32[4,32,128]{2,1,0:T(8,128)S(1)} %get-tuple-element.79), channel_id=1, source_target_pairs={{0,6},{1,7},{2,4},{3,5},{4,2},{5,3},{6,0},{7,1},{8,14},{9,15},{10,... | collective-permute-start | bytes 196616 | tf_op jit(solution)/shard_map/ppermute | solution.py:471
  48.5 1.2 %collective-permute-done.15.b_ref = f32[4,32,128]{2,1,0:T(8,128)S(1)} collective-permute-done((f32[4,32,128]{2,1,0:T(8,128)S(1)}, f32[4,32,128]{2,1,0:T(8,128)S(1)}, u32[]{:S(2)}, u32[]{:S(2)}) %collective-permute-start.15) | collective-permute-done | bytes 65568 | tf_op jit(solution)/shard_map/ppermute | solution.py:471
  49.7 2.1 %collective-permute-done.16.c_ref = f32[4,32,128]{2,1,0:T(8,128)S(1)} collective-permute-done((f32[4,32,128]{2,1,0:T(8,128)S(1)}, f32[4,32,128]{2,1,0:T(8,128)S(1)}, u32[]{:S(2)}, u32[]{:S(2)}) %collective-permute-start.16) | collective-permute-done | bytes 65568 | tf_op jit(solution)/shard_map/ppermute | solution.py:471
  51.8 1.1 %collective-permute-done.17.d_ref = f32[4,32,128]{2,1,0:T(8,128)S(1)} collective-permute-done((f32[4,32,128]{2,1,0:T(8,128)S(1)}, f32[4,32,128]{2,1,0:T(8,128)S(1)}, u32[]{:S(2)}, u32[]{:S(2)}) %collective-permute-start.17) | collective-permute-done | bytes 65568 | tf_op jit(solution)/shard_map/ppermute | solution.py:471
  52.9 1.7 %collective-permute-start.18 = (f32[4,32,128]{2,1,0:T(8,128)S(1)}, f32[4,32,128]{2,1,0:T(8,128)S(1)}, u32[]{:S(2)}, u32[]{:S(2)}) collective-permute-start(f32[4,32,128]{2,1,0:T(8,128)S(1)} %shard_map.168.a_ref), channel_id=1, source_target_pairs={{0,8},{4,12},{8,0},{12,4},{16,24},{20,28},{24,16},{28,20},{1,9},{5... | collective-permute-start | bytes 196616 | tf_op jit(solution)/shard_map/ppermute | solution.py:467
  54.6 2.2 %collective-permute-start.19 = (f32[4,32,128]{2,1,0:T(8,128)S(1)}, f32[4,32,128]{2,1,0:T(8,128)S(1)}, u32[]{:S(2)}, u32[]{:S(2)}) collective-permute-start(f32[4,32,128]{2,1,0:T(8,128)S(1)} %shard_map.168.a_ref), channel_id=1, source_target_pairs={{0,16},{4,20},{8,24},{12,28},{16,0},{20,4},{24,8},{28,12},{1,17},{... | collective-permute-start | bytes 196616 | tf_op jit(solution)/shard_map/ppermute | solution.py:467
  56.8 0.6 collective-permute-start.20
  57.4 3.8 %collective-permute-done.19.c_ref = f32[4,32,128]{2,1,0:T(8,128)S(1)} collective-permute-done((f32[4,32,128]{2,1,0:T(8,128)S(1)}, f32[4,32,128]{2,1,0:T(8,128)S(1)}, u32[]{:S(2)}, u32[]{:S(2)}) %collective-permute-start.19) | collective-permute-done | bytes 65568 | tf_op jit(solution)/shard_map/ppermute | solution.py:467
  61.2 1.7 %collective-permute-done.20.d_ref = f32[4,32,128]{2,1,0:T(8,128)S(1)} collective-permute-done((f32[4,32,128]{2,1,0:T(8,128)S(1)}, f32[4,32,128]{2,1,0:T(8,128)S(1)}, u32[]{:S(2)}, u32[]{:S(2)}) %collective-permute-start.20) | collective-permute-done | bytes 65568 | tf_op jit(solution)/shard_map/ppermute | solution.py:467
  62.9 1.4 %collective-permute-start.21 = (f32[4,32,128]{2,1,0:T(8,128)S(1)}, f32[4,32,128]{2,1,0:T(8,128)S(1)}, u32[]{:S(2)}, u32[]{:S(2)}) collective-permute-start(f32[4,32,128]{2,1,0:T(8,128)S(1)} %shard_map.169.refs_0_), channel_id=1, source_target_pairs={{0,2},{1,3},{2,0},{3,1},{4,6},{5,7},{6,4},{7,5},{8,10},{9,11},{10,... | collective-permute-start | bytes 196616 | tf_op jit(solution)/shard_map/ppermute | solution.py:471
  64.2 0.6 collective-permute-start.22
  64.8 1.6 %collective-permute-start.23 = (f32[4,32,128]{2,1,0:T(8,128)S(1)}, f32[4,32,128]{2,1,0:T(8,128)S(1)}, u32[]{:S(2)}, u32[]{:S(2)}) collective-permute-start(f32[4,32,128]{2,1,0:T(8,128)S(1)} %shard_map.169.refs_0_), channel_id=1, source_target_pairs={{0,6},{1,7},{2,4},{3,5},{4,2},{5,3},{6,0},{7,1},{8,14},{9,15},{10,... | collective-permute-start | bytes 196616 | tf_op jit(solution)/shard_map/ppermute | solution.py:471
  66.4 0.8 %collective-permute-done.21.refs_1_ = f32[4,32,128]{2,1,0:T(8,128)S(1)} collective-permute-done((f32[4,32,128]{2,1,0:T(8,128)S(1)}, f32[4,32,128]{2,1,0:T(8,128)S(1)}, u32[]{:S(2)}, u32[]{:S(2)}) %collective-permute-start.21) | collective-permute-done | bytes 65568 | tf_op jit(solution)/shard_map/ppermute | solution.py:471
  67.2 1.3 %collective-permute-done.22.refs_2_ = f32[4,32,128]{2,1,0:T(8,128)S(1)} collective-permute-done((f32[4,32,128]{2,1,0:T(8,128)S(1)}, f32[4,32,128]{2,1,0:T(8,128)S(1)}, u32[]{:S(2)}, u32[]{:S(2)}) %collective-permute-start.22) | collective-permute-done | bytes 65568 | tf_op jit(solution)/shard_map/ppermute | solution.py:471
  68.5 1.5 %collective-permute-done.23.refs_3_ = f32[4,32,128]{2,1,0:T(8,128)S(1)} collective-permute-done((f32[4,32,128]{2,1,0:T(8,128)S(1)}, f32[4,32,128]{2,1,0:T(8,128)S(1)}, u32[]{:S(2)}, u32[]{:S(2)}) %collective-permute-start.23) | collective-permute-done | bytes 65568 | tf_op jit(solution)/shard_map/ppermute | solution.py:471
  70.1 1.5 %collective-permute-done.24.theirs_ref = f32[512,128]{1,0:T(8,128)S(1)} collective-permute-done((f32[512,128]{1,0:T(8,128)S(1)}, f32[512,128]{1,0:T(8,128)S(1)}, u32[]{:S(2)}, u32[]{:S(2)}) %collective-permute-start.24) | collective-permute-done | bytes 262176 | tf_op jit(solution)/shard_map/ppermute | solution.py:464
  71.6 1.2 %shard_map.171 = (f32[1024,128]{1,0:T(8,128)}, f32[1024,128]{1,0:T(8,128)}) custom-call(f32[512,128]{1,0:T(8,128)S(1)} %bitcast.10, f32[512,128]{1,0:T(8,128)S(1)} %collective-permute-done.24.theirs_ref, f32[1024,128]{1,0:T(8,128)S(1)} %copy-done, f32[1024,128]{1,0:T(8,128)S(1)} %copy-done.1), custom_call_target="tpu_custom_call" | custom-call | tf_op jit(solution)/shard_map/pallas_call | solution.py:60
  72.8 1.1 %shard_map.175 = (f32[256,128]{1,0:T(8,128)}, f32[256,128]{1,0:T(8,128)}) custom-call(f32[8,72,128]{2,1,0:T(8,128)S(1)} %all-to-all-done.r_0_, f32[256,128]{1,0:T(8,128)S(1)} %copy-done.2, f32[256,128]{1,0:T(8,128)S(1)} %copy-done.3), custom_call_target="tpu_custom_call" | custom-call | tf_op jit(solution)/shard_map/pallas_call | solution.py:60
  (36 shorter events, 2.2 us)
Async XLA Ops:
  0.6 13.5 %collective-permute-start.12 = (bf16[1024,128]{1,0:T(8,128)(2,1)}, bf16[1024,128]{1,0:T(8,128)(2,1)S(1)}, u32[]{:S(2)}, u32[]{:S(2)}) collective-permute-start(bf16[1024,128]{1,0:T(8,128)(2,1)} %r_4_.1), channel_id=1, source_target_pairs={{0,2},{1,3},{2,0},{3,1},{4,6},{5,7},{6,4},{7,5},{8,10},{9,11},{10,... | collective-permute-start | bytes 786440 | tf_op jit(solution)/shard_map/ppermute | solution.py:464
  4.7 9.9 %collective-permute-start.4 = (bf16[256,128]{1,0:T(8,128)(2,1)S(1)}, bf16[256,128]{1,0:T(8,128)(2,1)S(1)}, u32[]{:S(2)}, u32[]{:S(2)}) collective-permute-start(bf16[256,128]{1,0:T(8,128)(2,1)S(1)} %get-tuple-element.60.refs_0_), channel_id=1, source_target_pairs={{0,8},{4,12},{8,0},{12,4},{16,24},{20,28},{24,16},{28,20},{1,9},{5... | collective-permute-start | bytes 196616 | tf_op jit(solution)/shard_map/ppermute | solution.py:467
  6.3 8.3 %collective-permute-start.5 = (bf16[256,128]{1,0:T(8,128)(2,1)S(1)}, bf16[256,128]{1,0:T(8,128)(2,1)S(1)}, u32[]{:S(2)}, u32[]{:S(2)}) collective-permute-start(bf16[256,128]{1,0:T(8,128)(2,1)S(1)} %get-tuple-element.60.refs_0_), channel_id=1, source_target_pairs={{0,16},{4,20},{8,24},{12,28},{16,0},{20,4},{24,8},{28,12},{1,17},{... | collective-permute-start | bytes 196616 | tf_op jit(solution)/shard_map/ppermute | solution.py:467
  8.9 6.1 %collective-permute-start.6 = (bf16[256,128]{1,0:T(8,128)(2,1)S(1)}, bf16[256,128]{1,0:T(8,128)(2,1)S(1)}, u32[]{:S(2)}, u32[]{:S(2)}) collective-permute-start(bf16[256,128]{1,0:T(8,128)(2,1)S(1)} %get-tuple-element.60.refs_0_), channel_id=1, source_target_pairs={{0,24},{4,28},{8,16},{12,20},{16,8},{20,12},{24,0},{28,4},{1,25},{... | collective-permute-start | bytes 196616 | tf_op jit(solution)/shard_map/ppermute | solution.py:467
  10.4 3.7 %collective-permute-start.3 = (s32[8,256]{1,0:T(8,128)S(1)}, s32[8,256]{1,0:T(8,128)S(1)}, u32[]{:S(2)}, u32[]{:S(2)}) collective-permute-start(s32[8,256]{1,0:T(8,128)S(1)} %get-tuple-element.59), channel_id=1, source_target_pairs={{0,4},{4,0},{8,12},{12,8},{16,20},{20,16},{24,28},{28,24},{1,5},{5... | collective-permute-start | bytes 24584 | tf_op jit(solution)/shard_map/ppermute | solution.py:467
  14.1 13.5 %collective-permute-start.11 = (bf16[1024,128]{1,0:T(8,128)(2,1)}, bf16[1024,128]{1,0:T(8,128)(2,1)S(1)}, u32[]{:S(2)}, u32[]{:S(2)}) collective-permute-start(bf16[1024,128]{1,0:T(8,128)(2,1)} %r_4_.1), channel_id=1, source_target_pairs={{0,1},{1,0},{2,3},{3,2},{4,5},{5,4},{6,7},{7,6},{8,9},{9,8},{10,11... | collective-permute-start | bytes 786440 | tf_op jit(solution)/shard_map/ppermute | solution.py:464
  14.1 13.5 %collective-permute-start.13 = (bf16[1024,128]{1,0:T(8,128)(2,1)S(1)}, bf16[1024,128]{1,0:T(8,128)(2,1)S(1)}, u32[]{:S(2)}, u32[]{:S(2)}) collective-permute-start(bf16[1024,128]{1,0:T(8,128)(2,1)S(1)} %collective-permute-done.12.r_2_), channel_id=1, source_target_pairs={{0,1},{1,0},{2,3},{3,2},{4,5},{5,4},{6,7},{7,6},{8,9},{9,8},{10,11... | collective-permute-start | bytes 786440 | tf_op jit(solution)/shard_map/ppermute | solution.py:464
  15.6 4.3 %collective-permute-start.7 = (bf16[256,128]{1,0:T(8,128)(2,1)S(1)}, bf16[256,128]{1,0:T(8,128)(2,1)S(1)}, u32[]{:S(2)}, u32[]{:S(2)}) collective-permute-start(bf16[256,128]{1,0:T(8,128)(2,1)S(1)} %get-tuple-element.62), channel_id=1, source_target_pairs={{0,4},{1,5},{2,6},{3,7},{4,0},{5,1},{6,2},{7,3},{8,12},{9,13},{10,... | collective-permute-start | bytes 196616 | tf_op jit(solution)/shard_map/ppermute | solution.py:471
  17.2 4.7 %collective-permute-start.8 = (bf16[256,128]{1,0:T(8,128)(2,1)S(1)}, bf16[256,128]{1,0:T(8,128)(2,1)S(1)}, u32[]{:S(2)}, u32[]{:S(2)}) collective-permute-start(bf16[256,128]{1,0:T(8,128)(2,1)S(1)} %get-tuple-element.61.mine_ref), channel_id=1, source_target_pairs={{0,2},{1,3},{2,0},{3,1},{4,6},{5,7},{6,4},{7,5},{8,10},{9,11},{10,... | collective-permute-start | bytes 196616 | tf_op jit(solution)/shard_map/ppermute | solution.py:471
  17.7 5.8 %collective-permute-start.9 = (bf16[256,128]{1,0:T(8,128)(2,1)S(1)}, bf16[256,128]{1,0:T(8,128)(2,1)S(1)}, u32[]{:S(2)}, u32[]{:S(2)}) collective-permute-start(bf16[256,128]{1,0:T(8,128)(2,1)S(1)} %get-tuple-element.62), channel_id=1, source_target_pairs={{0,6},{1,7},{2,4},{3,5},{4,2},{5,3},{6,0},{7,1},{8,14},{9,15},{10,... | collective-permute-start | bytes 196616 | tf_op jit(solution)/shard_map/ppermute | solution.py:471
  19.9 4.4 %collective-permute-start.1 = (bf16[304,128]{1,0:T(8,128)(2,1)S(1)}, bf16[304,128]{1,0:T(8,128)(2,1)S(1)}, u32[]{:S(2)}, u32[]{:S(2)}) collective-permute-start(bf16[304,128]{1,0:T(8,128)(2,1)S(1)} %shard_map.159.r_0_.r_4_), channel_id=1, source_target_pairs={{0,2},{1,3},{2,0},{3,1},{4,6},{5,7},{6,4},{7,5},{8,10},{9,11},{10,... | collective-permute-start | bytes 233480 | tf_op jit(solution)/shard_map/ppermute | solution.py:464
  23.6 4.9 %collective-permute-start.10 = (bf16[2,256,128]{2,1,0:T(8,128)(2,1)S(1)}, bf16[2,256,128]{2,1,0:T(8,128)(2,1)S(1)}, u32[]{:S(2)}, u32[]{:S(2)}) collective-permute-start(bf16[2,256,128]{2,1,0:T(8,128)(2,1)S(1)} %shard_map.163.r_2_), channel_id=1, source_target_pairs={{0,1},{1,0},{2,3},{3,2},{4,5},{5,4},{6,7},{7,6},{8,9},{9,8},{10,11... | collective-permute-start | bytes 393224 | tf_op jit(solution)/shard_map/ppermute | solution.py:464
  23.6 1.9 %collective-permute-start = (bf16[304,128]{1,0:T(8,128)(2,1)S(1)}, bf16[304,128]{1,0:T(8,128)(2,1)S(1)}, u32[]{:S(2)}, u32[]{:S(2)}) collective-permute-start(bf16[304,128]{1,0:T(8,128)(2,1)S(1)} %shard_map.159.r_0_.r_4_), channel_id=1, source_target_pairs={{0,1},{1,0},{2,3},{3,2},{4,5},{5,4},{6,7},{7,6},{8,9},{9,8},{10,11... | collective-permute-start | bytes 233480 | tf_op jit(solution)/shard_map/ppermute | solution.py:464
  24.3 2.2 %collective-permute-start.2 = (bf16[304,128]{1,0:T(8,128)(2,1)S(1)}, bf16[304,128]{1,0:T(8,128)(2,1)S(1)}, u32[]{:S(2)}, u32[]{:S(2)}) collective-permute-start(bf16[304,128]{1,0:T(8,128)(2,1)S(1)} %collective-permute-done.1.r_0_.r_6_), channel_id=1, source_target_pairs={{0,1},{1,0},{2,3},{3,2},{4,5},{5,4},{6,7},{7,6},{8,9},{9,8},{10,11... | collective-permute-start | bytes 233480 | tf_op jit(solution)/shard_map/ppermute | solution.py:464
  30.0 41.6 %copy-start = (f32[1024,128]{1,0:T(8,128)S(1)}, f32[1024,128]{1,0:T(8,128)}, u32[]{:S(2)}) copy-start(f32[1024,128]{1,0:T(8,128)} %table_ref.1) | copy-start | bytes 1572868
  30.0 41.6 %copy-start.1 = (f32[1024,128]{1,0:T(8,128)S(1)}, f32[1024,128]{1,0:T(8,128)}, u32[]{:S(2)}) copy-start(f32[1024,128]{1,0:T(8,128)} %accum_ref.1) | copy-start | bytes 1572868
  30.8 42.0 %copy-start.2 = (f32[256,128]{1,0:T(8,128)S(1)}, f32[256,128]{1,0:T(8,128)}, u32[]{:S(2)}) copy-start(f32[256,128]{1,0:T(8,128)} %r_1_.1) | copy-start | bytes 393220
  30.8 42.0 %copy-start.3 = (f32[256,128]{1,0:T(8,128)S(1)}, f32[256,128]{1,0:T(8,128)}, u32[]{:S(2)}) copy-start(f32[256,128]{1,0:T(8,128)} %r_2_.3) | copy-start | bytes 393220
  30.8 1.7 %collective-permute-start.25 = (f32[2,256,128]{2,1,0:T(8,128)S(1)}, f32[2,256,128]{2,1,0:T(8,128)S(1)}, u32[]{:S(2)}, u32[]{:S(2)}) collective-permute-start(f32[2,256,128]{2,1,0:T(8,128)S(1)} %get-tuple-element.83), channel_id=1, source_target_pairs={{0,1},{1,0},{2,3},{3,2},{4,5},{5,4},{6,7},{7,6},{8,9},{9,8},{10,11... | collective-permute-start | bytes 786440 | tf_op jit(solution)/shard_map/ppermute | solution.py:464
  31.4 13.5 %collective-permute-start.14 = (f32[512,128]{1,0:T(8,128)S(1)}, f32[512,128]{1,0:T(8,128)S(1)}, u32[]{:S(2)}, u32[]{:S(2)}) collective-permute-start(f32[512,128]{1,0:T(8,128)S(1)} %get-tuple-element.75), channel_id=1, source_target_pairs={{0,1},{1,0},{2,3},{3,2},{4,5},{5,4},{6,7},{7,6},{8,9},{9,8},{10,11... | collective-permute-start | bytes 786440 | tf_op jit(solution)/shard_map/ppermute | solution.py:464
  32.6 5.8 %collective-permute-start.26 = (f32[256,128]{1,0:T(8,128)S(1)}, f32[256,128]{1,0:T(8,128)S(1)}, u32[]{:S(2)}, u32[]{:S(2)}) collective-permute-start(f32[256,128]{1,0:T(8,128)S(1)} %get-tuple-element.85), channel_id=1, source_target_pairs={{0,2},{1,3},{2,0},{3,1},{4,6},{5,7},{6,4},{7,5},{8,10},{9,11},{10,... | collective-permute-start | bytes 393224 | tf_op jit(solution)/shard_map/ppermute | solution.py:464
  39.4 33.4 %all-to-all-start = ((f32[8,72,128]{2,1,0:T(8,128)}), f32[8,72,128]{2,1,0:T(8,128)S(1)}, u32[]{:S(2)}, u32[]{:S(2)}) async-start(f32[8,72,128]{2,1,0:T(8,128)} %shard_map.174), calls=%async_computation | async-start | bytes 589824 | tf_op jit(solution)/shard_map/all_to_all | solution.py:646
  44.9 4.7 %collective-permute-start.15 = (f32[4,32,128]{2,1,0:T(8,128)S(1)}, f32[4,32,128]{2,1,0:T(8,128)S(1)}, u32[]{:S(2)}, u32[]{:S(2)}) collective-permute-start(f32[4,32,128]{2,1,0:T(8,128)S(1)} %get-tuple-element.77), channel_id=1, source_target_pairs={{0,2},{1,3},{2,0},{3,1},{4,6},{5,7},{6,4},{7,5},{8,10},{9,11},{10,... | collective-permute-start | bytes 196616 | tf_op jit(solution)/shard_map/ppermute | solution.py:471
  45.5 6.3 %collective-permute-start.16 = (f32[4,32,128]{2,1,0:T(8,128)S(1)}, f32[4,32,128]{2,1,0:T(8,128)S(1)}, u32[]{:S(2)}, u32[]{:S(2)}) collective-permute-start(f32[4,32,128]{2,1,0:T(8,128)S(1)} %get-tuple-element.78), channel_id=1, source_target_pairs={{0,4},{1,5},{2,6},{3,7},{4,0},{5,1},{6,2},{7,3},{8,12},{9,13},{10,... | collective-permute-start | bytes 196616 | tf_op jit(solution)/shard_map/ppermute | solution.py:471
  47.5 5.4 %collective-permute-start.17 = (f32[4,32,128]{2,1,0:T(8,128)S(1)}, f32[4,32,128]{2,1,0:T(8,128)S(1)}, u32[]{:S(2)}, u32[]{:S(2)}) collective-permute-start(f32[4,32,128]{2,1,0:T(8,128)S(1)} %get-tuple-element.79), channel_id=1, source_target_pairs={{0,6},{1,7},{2,4},{3,5},{4,2},{5,3},{6,0},{7,1},{8,14},{9,15},{10,... | collective-permute-start | bytes 196616 | tf_op jit(solution)/shard_map/ppermute | solution.py:471
  52.9 4.5 %collective-permute-start.18 = (f32[4,32,128]{2,1,0:T(8,128)S(1)}, f32[4,32,128]{2,1,0:T(8,128)S(1)}, u32[]{:S(2)}, u32[]{:S(2)}) collective-permute-start(f32[4,32,128]{2,1,0:T(8,128)S(1)} %shard_map.168.a_ref), channel_id=1, source_target_pairs={{0,8},{4,12},{8,0},{12,4},{16,24},{20,28},{24,16},{28,20},{1,9},{5... | collective-permute-start | bytes 196616 | tf_op jit(solution)/shard_map/ppermute | solution.py:467
  54.6 6.6 %collective-permute-start.19 = (f32[4,32,128]{2,1,0:T(8,128)S(1)}, f32[4,32,128]{2,1,0:T(8,128)S(1)}, u32[]{:S(2)}, u32[]{:S(2)}) collective-permute-start(f32[4,32,128]{2,1,0:T(8,128)S(1)} %shard_map.168.a_ref), channel_id=1, source_target_pairs={{0,16},{4,20},{8,24},{12,28},{16,0},{20,4},{24,8},{28,12},{1,17},{... | collective-permute-start | bytes 196616 | tf_op jit(solution)/shard_map/ppermute | solution.py:467
  56.8 6.1 %collective-permute-start.20 = (f32[4,32,128]{2,1,0:T(8,128)S(1)}, f32[4,32,128]{2,1,0:T(8,128)S(1)}, u32[]{:S(2)}, u32[]{:S(2)}) collective-permute-start(f32[4,32,128]{2,1,0:T(8,128)S(1)} %shard_map.168.a_ref), channel_id=1, source_target_pairs={{0,24},{4,28},{8,16},{12,20},{16,8},{20,12},{24,0},{28,4},{1,25},{... | collective-permute-start | bytes 196616 | tf_op jit(solution)/shard_map/ppermute | solution.py:467
  62.9 4.3 %collective-permute-start.21 = (f32[4,32,128]{2,1,0:T(8,128)S(1)}, f32[4,32,128]{2,1,0:T(8,128)S(1)}, u32[]{:S(2)}, u32[]{:S(2)}) collective-permute-start(f32[4,32,128]{2,1,0:T(8,128)S(1)} %shard_map.169.refs_0_), channel_id=1, source_target_pairs={{0,2},{1,3},{2,0},{3,1},{4,6},{5,7},{6,4},{7,5},{8,10},{9,11},{10,... | collective-permute-start | bytes 196616 | tf_op jit(solution)/shard_map/ppermute | solution.py:471
  64.2 4.3 %collective-permute-start.22 = (f32[4,32,128]{2,1,0:T(8,128)S(1)}, f32[4,32,128]{2,1,0:T(8,128)S(1)}, u32[]{:S(2)}, u32[]{:S(2)}) collective-permute-start(f32[4,32,128]{2,1,0:T(8,128)S(1)} %shard_map.169.refs_0_), channel_id=1, source_target_pairs={{0,4},{1,5},{2,6},{3,7},{4,0},{5,1},{6,2},{7,3},{8,12},{9,13},{10,... | collective-permute-start | bytes 196616 | tf_op jit(solution)/shard_map/ppermute | solution.py:471
  64.8 5.2 %collective-permute-start.23 = (f32[4,32,128]{2,1,0:T(8,128)S(1)}, f32[4,32,128]{2,1,0:T(8,128)S(1)}, u32[]{:S(2)}, u32[]{:S(2)}) collective-permute-start(f32[4,32,128]{2,1,0:T(8,128)S(1)} %shard_map.169.refs_0_), channel_id=1, source_target_pairs={{0,6},{1,7},{2,4},{3,5},{4,2},{5,3},{6,0},{7,1},{8,14},{9,15},{10,... | collective-permute-start | bytes 196616 | tf_op jit(solution)/shard_map/ppermute | solution.py:471
  70.0 1.6 %collective-permute-start.24 = (f32[512,128]{1,0:T(8,128)S(1)}, f32[512,128]{1,0:T(8,128)S(1)}, u32[]{:S(2)}, u32[]{:S(2)}) collective-permute-start(f32[512,128]{1,0:T(8,128)S(1)} %bitcast.9), channel_id=1, source_target_pairs={{0,1},{1,0},{2,3},{3,2},{4,5},{5,4},{6,7},{7,6},{8,9},{9,8},{10,11... | collective-permute-start | bytes 786440 | tf_op jit(solution)/shard_map/ppermute | solution.py:464

commit v4 on v3

--- a/solution.py
+++ b/solution.py
@@ -468,9 +468,7 @@
 
     def near_swap(x, k):
         mask = k // 2 * mp_count + k % 2 * 2
-        return lax.ppermute(
-            x, both, [(i, i ^ mask) for i in range(dp_count * mp_count)]
-        )
+        return lax.ppermute(x, both, [(i, i ^ mask) for i in range(dp_count * mp_count)])
 
     near = dp_count == 8 and mp_count == 4
 
@@ -615,7 +613,9 @@
         )
         pieces = [near_swap(x, k) if k else x for k, x in enumerate(pieces)]
         (part,) = call(sum_kernel, [(line, F32, True)], pieces)
-        pieces = [far_swap(part, 2 * k) if k else part for k in range(4)]
+        pieces = [part]
+        for k in (1, 2, 3):
+            pieces.append(far_swap(part, 2 * k))
         (part,) = call(sum_kernel, [(line, F32, True)], pieces)
         pieces = [near_swap(part, k) if k else part for k in range(4)]
         (half,) = call(order_near_kernel, [(shape, F32, True)], pieces)

time: 74.2 us -> 74.2 us (level)
  no operation moved by 1% of the time
where the time goes in v4:
time: 74.2 us; the launch traced here: 73.9 us
  starting transfers between devices  32.8 us (44%)
  waiting for transfers between devices  27.1 us (37%)
  Pallas kernels  13.2 us (18%)
  between operations  0.85 us (1%)
    pallas_call x20, Pallas kernels, call(): pl.pallas_call(body, out_shape=avals, in_specs=[ANY if i in raw else VM f...  13.2 us
    ppermute x9, waiting for transfers between devices, near_swap(): lax.ppermute(x, both, [(i, i ^ mask) for i in range(dp_count * mp_count)])  11.8 us
    ppermute x9, starting transfers between devices, near_swap(): lax.ppermute(x, both, [(i, i ^ mask) for i in range(dp_count * mp_count)])  10.7 us
    ppermute x7, starting transfers between devices, far_swap(): return lax.ppermute(x, 'dp', [(i, i ^ mask) for i in range(dp_count)])  10.5 us
    ppermute x7, waiting for transfers between devices, far_swap(): return lax.ppermute(x, 'dp', [(i, i ^ mask) for i in range(dp_count)])  7.97 us
    ppermute x11, waiting for transfers between devices, swap(): return lax.ppermute(x, 'mp', [(i, i ^ mask) for i in range(mp_count)])  7.34 us
    ppermute x11, starting transfers between devices, swap(): return lax.ppermute(x, 'mp', [(i, i ^ mask) for i in range(mp_count)])  6.12 us
    all_to_all x1, starting transfers between devices, per_device(): lax.all_to_all(outgoing, 'dp', split_axis=0, concat_axis=0, tiled=True)  5.5 us
  transfers between devices with their start and end apart: 28, of which 17 were waited for; matrix products, arithmetic and copies ran while one was open for 0% of the time, Pallas kernels for 13%

profile of v4, /device:TPU:0, one launch (start us, length us, event | category | flops | bytes accessed | tf_op | source)
XLA Modules:
  0.0 73.9 jit_solution(11734725362700882667)
XLA Ops:
  0.6 3.0 %collective-permute-start.12 = (bf16[1024,128]{1,0:T(8,128)(2,1)}, bf16[1024,128]{1,0:T(8,128)(2,1)S(1)}, u32[]{:S(2)}, u32[]{:S(2)}) collective-permute-start(bf16[1024,128]{1,0:T(8,128)(2,1)} %r_4_.1), channel_id=1, source_target_pairs={{0,2},{1,3},{2,0},{3,1},{4,6},{5,7},{6,4},{7,5},{8,10},{9,11},{10,... | collective-permute-start | bytes 786440 | tf_op jit(solution)/shard_map/ppermute | solution.py:464
  3.7 1.0 %shard_map.156 = (bf16[256,128]{1,0:T(8,128)(2,1)S(1)}, s32[64,128]{1,0:T(8,128)S(1)}, s32[1,256]{1,0:T(1,128)S(1)}, bf16[128,256]{1,0:T(8,128)(2,1)S(1)}, s32[1...) custom-call(f32[256,128]{1,0:T(8,128)} %r_1_.1, s32[64,128]{1,0:T(8,128)} %bitcast.14, ...), custom_call_target="tpu_custom_call" | custom-call | tf_op jit(solution)/shard_map/pallas_call | solution.py:60
  4.7 1.6 %collective-permute-start.4 = (bf16[256,128]{1,0:T(8,128)(2,1)S(1)}, bf16[256,128]{1,0:T(8,128)(2,1)S(1)}, u32[]{:S(2)}, u32[]{:S(2)}) collective-permute-start(bf16[256,128]{1,0:T(8,128)(2,1)S(1)} %get-tuple-element.60.refs_0_), channel_id=1, source_target_pairs={{0,8},{4,12},{8,0},{12,4},{16,24},{20,28},{24,16},{28,20},{1,9},{5... | collective-permute-start | bytes 196616 | tf_op jit(solution)/shard_map/ppermute | solution.py:467
  6.3 2.6 %collective-permute-start.5 = (bf16[256,128]{1,0:T(8,128)(2,1)S(1)}, bf16[256,128]{1,0:T(8,128)(2,1)S(1)}, u32[]{:S(2)}, u32[]{:S(2)}) collective-permute-start(bf16[256,128]{1,0:T(8,128)(2,1)S(1)} %get-tuple-element.60.refs_0_), channel_id=1, source_target_pairs={{0,16},{4,20},{8,24},{12,28},{16,0},{20,4},{24,8},{28,12},{1,17},{... | collective-permute-start | bytes 196616 | tf_op jit(solution)/shard_map/ppermute | solution.py:467
  9.1 1.3 %shard_map.157 = (s32[256,128]{1,0:T(8,128)S(1)}, s32[8,256]{1,0:T(8,128)S(1)}, f32[1024,128]{1,0:T(8,128)S(1)}, s32[7,1024]{1,0:T(8,128)S(1)}, bf16[1024,128]{1...) custom-call(s32[64,128]{1,0:T(8,128)S(1)} %get-tuple-element.47.r_0_, s32[1,256]{1,0:T(1,128)S(1)} %get-tuple-element.48.r_1_, ...), custom_call_target="tpu_custom_call" | custom-call | tf_op jit(solution)/shard_map/pallas_call | solution.py:60
  10.4 1.6 %collective-permute-start.3 = (s32[8,256]{1,0:T(8,128)S(1)}, s32[8,256]{1,0:T(8,128)S(1)}, u32[]{:S(2)}, u32[]{:S(2)}) collective-permute-start(s32[8,256]{1,0:T(8,128)S(1)} %get-tuple-element.59), channel_id=1, source_target_pairs={{0,4},{4,0},{8,12},{12,8},{16,20},{20,16},{24,28},{28,24},{1,5},{5... | collective-permute-start | bytes 24584 | tf_op jit(solution)/shard_map/ppermute | solution.py:467
  12.0 2.1 %collective-permute-done.3.row_ref = s32[8,256]{1,0:T(8,128)S(1)} collective-permute-done((s32[8,256]{1,0:T(8,128)S(1)}, s32[8,256]{1,0:T(8,128)S(1)}, u32[]{:S(2)}, u32[]{:S(2)}) %collective-permute-start.3) | collective-permute-done | bytes 8224 | tf_op jit(solution)/shard_map/ppermute | solution.py:467
  15.0 0.6 shard_map.162
  15.6 1.6 %collective-permute-start.7 = (bf16[256,128]{1,0:T(8,128)(2,1)S(1)}, bf16[256,128]{1,0:T(8,128)(2,1)S(1)}, u32[]{:S(2)}, u32[]{:S(2)}) collective-permute-start(bf16[256,128]{1,0:T(8,128)(2,1)S(1)} %get-tuple-element.62), channel_id=1, source_target_pairs={{0,4},{1,5},{2,6},{3,7},{4,0},{5,1},{6,2},{7,3},{8,12},{9,13},{10,... | collective-permute-start | bytes 196616 | tf_op jit(solution)/shard_map/ppermute | solution.py:471
  17.2 0.5 collective-permute-start.8
  17.7 1.4 %collective-permute-start.9 = (bf16[256,128]{1,0:T(8,128)(2,1)S(1)}, bf16[256,128]{1,0:T(8,128)(2,1)S(1)}, u32[]{:S(2)}, u32[]{:S(2)}) collective-permute-start(bf16[256,128]{1,0:T(8,128)(2,1)S(1)} %get-tuple-element.62), channel_id=1, source_target_pairs={{0,6},{1,7},{2,4},{3,5},{4,2},{5,3},{6,0},{7,1},{8,14},{9,15},{10,... | collective-permute-start | bytes 196616 | tf_op jit(solution)/shard_map/ppermute | solution.py:471
  19.2 0.8 %collective-permute-done.7.near_ref = bf16[256,128]{1,0:T(8,128)(2,1)S(1)} collective-permute-done((bf16[256,128]{1,0:T(8,128)(2,1)S(1)}, bf16[256,128]{1,0:T(8,128)(2,1)S(1)}, u32[]{:S(2)}, u32[]{:S(2)}) %collective-permute-start.7) | collective-permute-done | bytes 65568 | tf_op jit(solution)/shard_map/ppermute | solution.py:471
  19.9 0.5 collective-permute-start.1
  20.5 1.4 %collective-permute-done.8.far_ref = bf16[256,128]{1,0:T(8,128)(2,1)S(1)} collective-permute-done((bf16[256,128]{1,0:T(8,128)(2,1)S(1)}, bf16[256,128]{1,0:T(8,128)(2,1)S(1)}, u32[]{:S(2)}, u32[]{:S(2)}) %collective-permute-start.8) | collective-permute-done | bytes 65568 | tf_op jit(solution)/shard_map/ppermute | solution.py:471
  21.8 1.7 %collective-permute-done.9.cross_ref = bf16[256,128]{1,0:T(8,128)(2,1)S(1)} collective-permute-done((bf16[256,128]{1,0:T(8,128)(2,1)S(1)}, bf16[256,128]{1,0:T(8,128)(2,1)S(1)}, u32[]{:S(2)}, u32[]{:S(2)}) %collective-permute-start.9) | collective-permute-done | bytes 65568 | tf_op jit(solution)/shard_map/ppermute | solution.py:471
  24.3 1.2 %shard_map.158 = (bf16[1024,1792]{1,0:T(8,128)(2,1)S(1)}, bf16[896,256]{1,0:T(8,128)(2,1)S(1)}) custom-call(s32[7,1024]{1,0:T(8,128)S(1)} %get-tuple-element.49.r_0_, f32[1024,128]{1,0:T(8,128)S(1)} %get-tuple-element.50.r_1_), custom_call_target="tpu_custom_call" | custom-call | tf_op jit(solution)/shard_map/pallas_call | solution.py:60
  25.5 1.0 %shard_map.160 = (bf16[256,512]{1,0:T(8,128)(2,1)S(1)}, bf16[512,256]{1,0:T(8,128)(2,1)S(1)}) custom-call(bf16[304,128]{1,0:T(8,128)(2,1)S(1)} %shard_map.159.r_0_.r_4_, bf16[304,128]{1,0:T(8,128)(2,1)S(1)} %collective-permute-done.r_1_.r_5_), custom_call_target="tpu_custom_call" | custom-call | tf_op jit(solution)/shard_map/pallas_call | solution.py:60
  26.6 1.0 %shard_map.161 = (bf16[256,512]{1,0:T(8,128)(2,1)S(1)}, bf16[512,256]{1,0:T(8,128)(2,1)S(1)}) custom-call(bf16[304,128]{1,0:T(8,128)(2,1)S(1)} %collective-permute-done.1.r_0_.r_6_, bf16[304,128]{1,0:T(8,128)(2,1)S(1)} %collective-permute-done.2.r_1_.r_7_), custom_call_target="tpu_custom_call" | custom-call | tf_op jit(solution)/shard_map/pallas_call | solution.py:60
  27.6 0.8 %shard_map.164 = (bf16[512,1024]{1,0:T(8,128)(2,1)S(1)}, bf16[128,512]{1,0:T(8,128)(2,1)S(1)}, f32[256,512]{1,0:T(8,128)S(1)}, f32[256,512]{1,0:T(8,128)S(1)}) custom-call(bf16[1024,128]{1,0:T(8,128)(2,1)S(1)} %get-tuple-element.63.r_0_, bf16[1024,128]{1,0:T(8,128)(2,1)S(1)} %collective-permute-done.11.r_1_, ...), custom_call_target="tpu_custom_call" | custom-call | tf_op jit(solution)/shard_map/pallas_call | solution.py:60
  28.5 1.5 %shard_map.165 = (bf16[1792,256]{1,0:T(8,128)(2,1)S(1)}, bf16[256,256]{1,0:T(8,128)(2,1)S(1)}, f32[512,128]{1,0:T(8,128)S(1)}) custom-call(bf16[256,512]{1,0:T(8,128)(2,1)S(1)} %get-tuple-element.56.r_0_, bf16[256,512]{1,0:T(8,128)(2,1)S(1)} %get-tuple-element.57.r_1_, bf16[2,256,128]{2,1,0:T(8,128)(2,1)S(1)} %shard_map.163.r_2_, ...), custom_call_target="tpu_custom_call" | custom-call | tf_op jit(solution)/shard_map/pallas_call | solution.py:60
  30.0 0.8 %shard_map.166 = (f32[512,128]{1,0:T(8,128)S(1)}, f32[2,256,128]{2,1,0:T(8,128)S(1)}, f32[2,256,128]{2,1,0:T(8,128)S(1)}) custom-call(bf16[1024,1792]{1,0:T(8,128)(2,1)S(1)} %get-tuple-element.51.r_8_.oht_ref, bf16[1792,256]{1,0:T(8,128)(2,1)S(1)} %get-tuple-element.70.ig_ref, bf16[256,256]{1,0:T(8,128)(2,1)S(1)} %get-tuple-element.71.bag_ref, ...), custom_call_target="tpu_custom_call" | custom-call | tf_op jit(solution)/shard_map/pallas_call | solution.py:60
  30.8 0.6 collective-permute-start.25
  31.4 1.1 %collective-permute-done.25.got_ref = f32[2,256,128]{2,1,0:T(8,128)S(1)} collective-permute-done((f32[2,256,128]{2,1,0:T(8,128)S(1)}, f32[2,256,128]{2,1,0:T(8,128)S(1)}, u32[]{:S(2)}, u32[]{:S(2)}) %collective-permute-start.25) | collective-permute-done | bytes 262176 | tf_op jit(solution)/shard_map/ppermute | solution.py:464
  32.6 0.7 %collective-permute-start.26 = (f32[256,128]{1,0:T(8,128)S(1)}, f32[256,128]{1,0:T(8,128)S(1)}, u32[]{:S(2)}, u32[]{:S(2)}) collective-permute-start(f32[256,128]{1,0:T(8,128)S(1)} %get-tuple-element.85), channel_id=1, source_target_pairs={{0,2},{1,3},{2,0},{3,1},{4,6},{5,7},{6,4},{7,5},{8,10},{9,11},{10,... | collective-permute-start | bytes 393224 | tf_op jit(solution)/shard_map/ppermute | solution.py:464
  33.3 0.5 shard_map.173
  33.9 4.5 %collective-permute-done.26.r_1_ = f32[256,128]{1,0:T(8,128)S(1)} collective-permute-done((f32[256,128]{1,0:T(8,128)S(1)}, f32[256,128]{1,0:T(8,128)S(1)}, u32[]{:S(2)}, u32[]{:S(2)}) %collective-permute-start.26) | collective-permute-done | bytes 131104 | tf_op jit(solution)/shard_map/ppermute | solution.py:464
  38.4 0.9 %shard_map.174 = f32[8,72,128]{2,1,0:T(8,128)} custom-call(f32[256,128]{1,0:T(8,128)S(1)} %get-tuple-element.84.r_0_, f32[256,128]{1,0:T(8,128)S(1)} %collective-permute-done.26.r_1_, bf16[512,256]{1,0:T(8,128)(2,1)S(1)} %get-tuple-element.86.r_2_, f32[64,128]{1,0:T(8,128)S(1)} %get-tuple-element.87.r_3_), custom_call_target="tpu_custom_call" | custom-call | tf_op jit(solution)/shard_map/pallas_call | solution.py:60
  39.4 5.5 %all-to-all-start = ((f32[8,72,128]{2,1,0:T(8,128)}), f32[8,72,128]{2,1,0:T(8,128)S(1)}, u32[]{:S(2)}, u32[]{:S(2)}) async-start(f32[8,72,128]{2,1,0:T(8,128)} %shard_map.174), calls=%async_computation | async-start | bytes 589824 | tf_op jit(solution)/shard_map/all_to_all | solution.py:646
  44.9 0.6 collective-permute-start.15
  45.5 2.0 %collective-permute-start.16 = (f32[4,32,128]{2,1,0:T(8,128)S(1)}, f32[4,32,128]{2,1,0:T(8,128)S(1)}, u32[]{:S(2)}, u32[]{:S(2)}) collective-permute-start(f32[4,32,128]{2,1,0:T(8,128)S(1)} %get-tuple-element.78), channel_id=1, source_target_pairs={{0,4},{1,5},{2,6},{3,7},{4,0},{5,1},{6,2},{7,3},{8,12},{9,13},{10,... | collective-permute-start | bytes 196616 | tf_op jit(solution)/shard_map/ppermute | solution.py:471
  47.5 0.9 %collective-permute-start.17 = (f32[4,32,128]{2,1,0:T(8,128)S(1)}, f32[4,32,128]{2,1,0:T(8,128)S(1)}, u32[]{:S(2)}, u32[]{:S(2)}) collective-permute-start(f32[4,32,128]{2,1,0:T(8,128)S(1)} %get-tuple-element.79), channel_id=1, source_target_pairs={{0,6},{1,7},{2,4},{3,5},{4,2},{5,3},{6,0},{7,1},{8,14},{9,15},{10,... | collective-permute-start | bytes 196616 | tf_op jit(solution)/shard_map/ppermute | solution.py:471
  48.5 1.2 %collective-permute-done.15.b_ref = f32[4,32,128]{2,1,0:T(8,128)S(1)} collective-permute-done((f32[4,32,128]{2,1,0:T(8,128)S(1)}, f32[4,32,128]{2,1,0:T(8,128)S(1)}, u32[]{:S(2)}, u32[]{:S(2)}) %collective-permute-start.15) | collective-permute-done | bytes 65568 | tf_op jit(solution)/shard_map/ppermute | solution.py:471
  49.7 2.1 %collective-permute-done.16.c_ref = f32[4,32,128]{2,1,0:T(8,128)S(1)} collective-permute-done((f32[4,32,128]{2,1,0:T(8,128)S(1)}, f32[4,32,128]{2,1,0:T(8,128)S(1)}, u32[]{:S(2)}, u32[]{:S(2)}) %collective-permute-start.16) | collective-permute-done | bytes 65568 | tf_op jit(solution)/shard_map/ppermute | solution.py:471
  51.8 1.1 %collective-permute-done.17.d_ref = f32[4,32,128]{2,1,0:T(8,128)S(1)} collective-permute-done((f32[4,32,128]{2,1,0:T(8,128)S(1)}, f32[4,32,128]{2,1,0:T(8,128)S(1)}, u32[]{:S(2)}, u32[]{:S(2)}) %collective-permute-start.17) | collective-permute-done | bytes 65568 | tf_op jit(solution)/shard_map/ppermute | solution.py:471
  52.9 1.7 %collective-permute-start.18 = (f32[4,32,128]{2,1,0:T(8,128)S(1)}, f32[4,32,128]{2,1,0:T(8,128)S(1)}, u32[]{:S(2)}, u32[]{:S(2)}) collective-permute-start(f32[4,32,128]{2,1,0:T(8,128)S(1)} %shard_map.168.a_ref), channel_id=1, source_target_pairs={{0,8},{4,12},{8,0},{12,4},{16,24},{20,28},{24,16},{28,20},{1,9},{5... | collective-permute-start | bytes 196616 | tf_op jit(solution)/shard_map/ppermute | solution.py:467
  54.6 2.2 %collective-permute-start.19 = (f32[4,32,128]{2,1,0:T(8,128)S(1)}, f32[4,32,128]{2,1,0:T(8,128)S(1)}, u32[]{:S(2)}, u32[]{:S(2)}) collective-permute-start(f32[4,32,128]{2,1,0:T(8,128)S(1)} %shard_map.168.a_ref), channel_id=1, source_target_pairs={{0,16},{4,20},{8,24},{12,28},{16,0},{20,4},{24,8},{28,12},{1,17},{... | collective-permute-start | bytes 196616 | tf_op jit(solution)/shard_map/ppermute | solution.py:467
  56.8 0.6 collective-permute-start.20
  57.4 3.8 %collective-permute-done.19.c_ref = f32[4,32,128]{2,1,0:T(8,128)S(1)} collective-permute-done((f32[4,32,128]{2,1,0:T(8,128)S(1)}, f32[4,32,128]{2,1,0:T(8,128)S(1)}, u32[]{:S(2)}, u32[]{:S(2)}) %collective-permute-start.19) | collective-permute-done | bytes 65568 | tf_op jit(solution)/shard_map/ppermute | solution.py:467
  61.2 1.7 %collective-permute-done.20.d_ref = f32[4,32,128]{2,1,0:T(8,128)S(1)} collective-permute-done((f32[4,32,128]{2,1,0:T(8,128)S(1)}, f32[4,32,128]{2,1,0:T(8,128)S(1)}, u32[]{:S(2)}, u32[]{:S(2)}) %collective-permute-start.20) | collective-permute-done | bytes 65568 | tf_op jit(solution)/shard_map/ppermute | solution.py:467
  62.9 1.4 %collective-permute-start.21 = (f32[4,32,128]{2,1,0:T(8,128)S(1)}, f32[4,32,128]{2,1,0:T(8,128)S(1)}, u32[]{:S(2)}, u32[]{:S(2)}) collective-permute-start(f32[4,32,128]{2,1,0:T(8,128)S(1)} %shard_map.169.refs_0_), channel_id=1, source_target_pairs={{0,2},{1,3},{2,0},{3,1},{4,6},{5,7},{6,4},{7,5},{8,10},{9,11},{10,... | collective-permute-start | bytes 196616 | tf_op jit(solution)/shard_map/ppermute | solution.py:471
  64.2 0.6 collective-permute-start.22
  64.8 1.6 %collective-permute-start.23 = (f32[4,32,128]{2,1,0:T(8,128)S(1)}, f32[4,32,128]{2,1,0:T(8,128)S(1)}, u32[]{:S(2)}, u32[]{:S(2)}) collective-permute-start(f32[4,32,128]{2,1,0:T(8,128)S(1)} %shard_map.169.refs_0_), channel_id=1, source_target_pairs={{0,6},{1,7},{2,4},{3,5},{4,2},{5,3},{6,0},{7,1},{8,14},{9,15},{10,... | collective-permute-start | bytes 196616 | tf_op jit(solution)/shard_map/ppermute | solution.py:471
  66.4 0.8 %collective-permute-done.21.refs_1_ = f32[4,32,128]{2,1,0:T(8,128)S(1)} collective-permute-done((f32[4,32,128]{2,1,0:T(8,128)S(1)}, f32[4,32,128]{2,1,0:T(8,128)S(1)}, u32[]{:S(2)}, u32[]{:S(2)}) %collective-permute-start.21) | collective-permute-done | bytes 65568 | tf_op jit(solution)/shard_map/ppermute | solution.py:471
  67.2 1.3 %collective-permute-done.22.refs_2_ = f32[4,32,128]{2,1,0:T(8,128)S(1)} collective-permute-done((f32[4,32,128]{2,1,0:T(8,128)S(1)}, f32[4,32,128]{2,1,0:T(8,128)S(1)}, u32[]{:S(2)}, u32[]{:S(2)}) %collective-permute-start.22) | collective-permute-done | bytes 65568 | tf_op jit(solution)/shard_map/ppermute | solution.py:471
  68.5 1.5 %collective-permute-done.23.refs_3_ = f32[4,32,128]{2,1,0:T(8,128)S(1)} collective-permute-done((f32[4,32,128]{2,1,0:T(8,128)S(1)}, f32[4,32,128]{2,1,0:T(8,128)S(1)}, u32[]{:S(2)}, u32[]{:S(2)}) %collective-permute-start.23) | collective-permute-done | bytes 65568 | tf_op jit(solution)/shard_map/ppermute | solution.py:471
  70.1 1.5 %collective-permute-done.24.theirs_ref = f32[512,128]{1,0:T(8,128)S(1)} collective-permute-done((f32[512,128]{1,0:T(8,128)S(1)}, f32[512,128]{1,0:T(8,128)S(1)}, u32[]{:S(2)}, u32[]{:S(2)}) %collective-permute-start.24) | collective-permute-done | bytes 262176 | tf_op jit(solution)/shard_map/ppermute | solution.py:464
  71.6 1.2 %shard_map.171 = (f32[1024,128]{1,0:T(8,128)}, f32[1024,128]{1,0:T(8,128)}) custom-call(f32[512,128]{1,0:T(8,128)S(1)} %bitcast.10, f32[512,128]{1,0:T(8,128)S(1)} %collective-permute-done.24.theirs_ref, f32[1024,128]{1,0:T(8,128)S(1)} %copy-done, f32[1024,128]{1,0:T(8,128)S(1)} %copy-done.1), custom_call_target="tpu_custom_call" | custom-call | tf_op jit(solution)/shard_map/pallas_call | solution.py:60
  72.8 1.1 %shard_map.175 = (f32[256,128]{1,0:T(8,128)}, f32[256,128]{1,0:T(8,128)}) custom-call(f32[8,72,128]{2,1,0:T(8,128)S(1)} %all-to-all-done.r_0_, f32[256,128]{1,0:T(8,128)S(1)} %copy-done.2, f32[256,128]{1,0:T(8,128)S(1)} %copy-done.3), custom_call_target="tpu_custom_call" | custom-call | tf_op jit(solution)/shard_map/pallas_call | solution.py:60
  (36 shorter events, 2.2 us)
Async XLA Ops:
  0.6 13.5 %collective-permute-start.12 = (bf16[1024,128]{1,0:T(8,128)(2,1)}, bf16[1024,128]{1,0:T(8,128)(2,1)S(1)}, u32[]{:S(2)}, u32[]{:S(2)}) collective-permute-start(bf16[1024,128]{1,0:T(8,128)(2,1)} %r_4_.1), channel_id=1, source_target_pairs={{0,2},{1,3},{2,0},{3,1},{4,6},{5,7},{6,4},{7,5},{8,10},{9,11},{10,... | collective-permute-start | bytes 786440 | tf_op jit(solution)/shard_map/ppermute | solution.py:464
  4.7 9.9 %collective-permute-start.4 = (bf16[256,128]{1,0:T(8,128)(2,1)S(1)}, bf16[256,128]{1,0:T(8,128)(2,1)S(1)}, u32[]{:S(2)}, u32[]{:S(2)}) collective-permute-start(bf16[256,128]{1,0:T(8,128)(2,1)S(1)} %get-tuple-element.60.refs_0_), channel_id=1, source_target_pairs={{0,8},{4,12},{8,0},{12,4},{16,24},{20,28},{24,16},{28,20},{1,9},{5... | collective-permute-start | bytes 196616 | tf_op jit(solution)/shard_map/ppermute | solution.py:467
  6.3 8.3 %collective-permute-start.5 = (bf16[256,128]{1,0:T(8,128)(2,1)S(1)}, bf16[256,128]{1,0:T(8,128)(2,1)S(1)}, u32[]{:S(2)}, u32[]{:S(2)}) collective-permute-start(bf16[256,128]{1,0:T(8,128)(2,1)S(1)} %get-tuple-element.60.refs_0_), channel_id=1, source_target_pairs={{0,16},{4,20},{8,24},{12,28},{16,0},{20,4},{24,8},{28,12},{1,17},{... | collective-permute-start | bytes 196616 | tf_op jit(solution)/shard_map/ppermute | solution.py:467
  8.9 6.1 %collective-permute-start.6 = (bf16[256,128]{1,0:T(8,128)(2,1)S(1)}, bf16[256,128]{1,0:T(8,128)(2,1)S(1)}, u32[]{:S(2)}, u32[]{:S(2)}) collective-permute-start(bf16[256,128]{1,0:T(8,128)(2,1)S(1)} %get-tuple-element.60.refs_0_), channel_id=1, source_target_pairs={{0,24},{4,28},{8,16},{12,20},{16,8},{20,12},{24,0},{28,4},{1,25},{... | collective-permute-start | bytes 196616 | tf_op jit(solution)/shard_map/ppermute | solution.py:467
  10.4 3.7 %collective-permute-start.3 = (s32[8,256]{1,0:T(8,128)S(1)}, s32[8,256]{1,0:T(8,128)S(1)}, u32[]{:S(2)}, u32[]{:S(2)}) collective-permute-start(s32[8,256]{1,0:T(8,128)S(1)} %get-tuple-element.59), channel_id=1, source_target_pairs={{0,4},{4,0},{8,12},{12,8},{16,20},{20,16},{24,28},{28,24},{1,5},{5... | collective-permute-start | bytes 24584 | tf_op jit(solution)/shard_map/ppermute | solution.py:467
  14.1 13.5 %collective-permute-start.11 = (bf16[1024,128]{1,0:T(8,128)(2,1)}, bf16[1024,128]{1,0:T(8,128)(2,1)S(1)}, u32[]{:S(2)}, u32[]{:S(2)}) collective-permute-start(bf16[1024,128]{1,0:T(8,128)(2,1)} %r_4_.1), channel_id=1, source_target_pairs={{0,1},{1,0},{2,3},{3,2},{4,5},{5,4},{6,7},{7,6},{8,9},{9,8},{10,11... | collective-permute-start | bytes 786440 | tf_op jit(solution)/shard_map/ppermute | solution.py:464
  14.1 13.5 %collective-permute-start.13 = (bf16[1024,128]{1,0:T(8,128)(2,1)S(1)}, bf16[1024,128]{1,0:T(8,128)(2,1)S(1)}, u32[]{:S(2)}, u32[]{:S(2)}) collective-permute-start(bf16[1024,128]{1,0:T(8,128)(2,1)S(1)} %collective-permute-done.12.r_2_), channel_id=1, source_target_pairs={{0,1},{1,0},{2,3},{3,2},{4,5},{5,4},{6,7},{7,6},{8,9},{9,8},{10,11... | collective-permute-start | bytes 786440 | tf_op jit(solution)/shard_map/ppermute | solution.py:464
  15.6 4.3 %collective-permute-start.7 = (bf16[256,128]{1,0:T(8,128)(2,1)S(1)}, bf16[256,128]{1,0:T(8,128)(2,1)S(1)}, u32[]{:S(2)}, u32[]{:S(2)}) collective-permute-start(bf16[256,128]{1,0:T(8,128)(2,1)S(1)} %get-tuple-element.62), channel_id=1, source_target_pairs={{0,4},{1,5},{2,6},{3,7},{4,0},{5,1},{6,2},{7,3},{8,12},{9,13},{10,... | collective-permute-start | bytes 196616 | tf_op jit(solution)/shard_map/ppermute | solution.py:471
  17.2 4.7 %collective-permute-start.8 = (bf16[256,128]{1,0:T(8,128)(2,1)S(1)}, bf16[256,128]{1,0:T(8,128)(2,1)S(1)}, u32[]{:S(2)}, u32[]{:S(2)}) collective-permute-start(bf16[256,128]{1,0:T(8,128)(2,1)S(1)} %get-tuple-element.61.mine_ref), channel_id=1, source_target_pairs={{0,2},{1,3},{2,0},{3,1},{4,6},{5,7},{6,4},{7,5},{8,10},{9,11},{10,... | collective-permute-start | bytes 196616 | tf_op jit(solution)/shard_map/ppermute | solution.py:471
  17.7 5.8 %collective-permute-start.9 = (bf16[256,128]{1,0:T(8,128)(2,1)S(1)}, bf16[256,128]{1,0:T(8,128)(2,1)S(1)}, u32[]{:S(2)}, u32[]{:S(2)}) collective-permute-start(bf16[256,128]{1,0:T(8,128)(2,1)S(1)} %get-tuple-element.62), channel_id=1, source_target_pairs={{0,6},{1,7},{2,4},{3,5},{4,2},{5,3},{6,0},{7,1},{8,14},{9,15},{10,... | collective-permute-start | bytes 196616 | tf_op jit(solution)/shard_map/ppermute | solution.py:471
  19.9 4.4 %collective-permute-start.1 = (bf16[304,128]{1,0:T(8,128)(2,1)S(1)}, bf16[304,128]{1,0:T(8,128)(2,1)S(1)}, u32[]{:S(2)}, u32[]{:S(2)}) collective-permute-start(bf16[304,128]{1,0:T(8,128)(2,1)S(1)} %shard_map.159.r_0_.r_4_), channel_id=1, source_target_pairs={{0,2},{1,3},{2,0},{3,1},{4,6},{5,7},{6,4},{7,5},{8,10},{9,11},{10,... | collective-permute-start | bytes 233480 | tf_op jit(solution)/shard_map/ppermute | solution.py:464
  23.6 4.9 %collective-permute-start.10 = (bf16[2,256,128]{2,1,0:T(8,128)(2,1)S(1)}, bf16[2,256,128]{2,1,0:T(8,128)(2,1)S(1)}, u32[]{:S(2)}, u32[]{:S(2)}) collective-permute-start(bf16[2,256,128]{2,1,0:T(8,128)(2,1)S(1)} %shard_map.163.r_2_), channel_id=1, source_target_pairs={{0,1},{1,0},{2,3},{3,2},{4,5},{5,4},{6,7},{7,6},{8,9},{9,8},{10,11... | collective-permute-start | bytes 393224 | tf_op jit(solution)/shard_map/ppermute | solution.py:464
  23.6 1.9 %collective-permute-start = (bf16[304,128]{1,0:T(8,128)(2,1)S(1)}, bf16[304,128]{1,0:T(8,128)(2,1)S(1)}, u32[]{:S(2)}, u32[]{:S(2)}) collective-permute-start(bf16[304,128]{1,0:T(8,128)(2,1)S(1)} %shard_map.159.r_0_.r_4_), channel_id=1, source_target_pairs={{0,1},{1,0},{2,3},{3,2},{4,5},{5,4},{6,7},{7,6},{8,9},{9,8},{10,11... | collective-permute-start | bytes 233480 | tf_op jit(solution)/shard_map/ppermute | solution.py:464
  24.3 2.2 %collective-permute-start.2 = (bf16[304,128]{1,0:T(8,128)(2,1)S(1)}, bf16[304,128]{1,0:T(8,128)(2,1)S(1)}, u32[]{:S(2)}, u32[]{:S(2)}) collective-permute-start(bf16[304,128]{1,0:T(8,128)(2,1)S(1)} %collective-permute-done.1.r_0_.r_6_), channel_id=1, source_target_pairs={{0,1},{1,0},{2,3},{3,2},{4,5},{5,4},{6,7},{7,6},{8,9},{9,8},{10,11... | collective-permute-start | bytes 233480 | tf_op jit(solution)/shard_map/ppermute | solution.py:464
  30.0 41.6 %copy-start = (f32[1024,128]{1,0:T(8,128)S(1)}, f32[1024,128]{1,0:T(8,128)}, u32[]{:S(2)}) copy-start(f32[1024,128]{1,0:T(8,128)} %table_ref.1) | copy-start | bytes 1572868
  30.0 41.6 %copy-start.1 = (f32[1024,128]{1,0:T(8,128)S(1)}, f32[1024,128]{1,0:T(8,128)}, u32[]{:S(2)}) copy-start(f32[1024,128]{1,0:T(8,128)} %accum_ref.1) | copy-start | bytes 1572868
  30.8 42.0 %copy-start.2 = (f32[256,128]{1,0:T(8,128)S(1)}, f32[256,128]{1,0:T(8,128)}, u32[]{:S(2)}) copy-start(f32[256,128]{1,0:T(8,128)} %r_1_.1) | copy-start | bytes 393220
  30.8 42.0 %copy-start.3 = (f32[256,128]{1,0:T(8,128)S(1)}, f32[256,128]{1,0:T(8,128)}, u32[]{:S(2)}) copy-start(f32[256,128]{1,0:T(8,128)} %r_2_.3) | copy-start | bytes 393220
  30.8 1.7 %collective-permute-start.25 = (f32[2,256,128]{2,1,0:T(8,128)S(1)}, f32[2,256,128]{2,1,0:T(8,128)S(1)}, u32[]{:S(2)}, u32[]{:S(2)}) collective-permute-start(f32[2,256,128]{2,1,0:T(8,128)S(1)} %get-tuple-element.83), channel_id=1, source_target_pairs={{0,1},{1,0},{2,3},{3,2},{4,5},{5,4},{6,7},{7,6},{8,9},{9,8},{10,11... | collective-permute-start | bytes 786440 | tf_op jit(solution)/shard_map/ppermute | solution.py:464
  31.4 13.5 %collective-permute-start.14 = (f32[512,128]{1,0:T(8,128)S(1)}, f32[512,128]{1,0:T(8,128)S(1)}, u32[]{:S(2)}, u32[]{:S(2)}) collective-permute-start(f32[512,128]{1,0:T(8,128)S(1)} %get-tuple-element.75), channel_id=1, source_target_pairs={{0,1},{1,0},{2,3},{3,2},{4,5},{5,4},{6,7},{7,6},{8,9},{9,8},{10,11... | collective-permute-start | bytes 786440 | tf_op jit(solution)/shard_map/ppermute | solution.py:464
  32.6 5.8 %collective-permute-start.26 = (f32[256,128]{1,0:T(8,128)S(1)}, f32[256,128]{1,0:T(8,128)S(1)}, u32[]{:S(2)}, u32[]{:S(2)}) collective-permute-start(f32[256,128]{1,0:T(8,128)S(1)} %get-tuple-element.85), channel_id=1, source_target_pairs={{0,2},{1,3},{2,0},{3,1},{4,6},{5,7},{6,4},{7,5},{8,10},{9,11},{10,... | collective-permute-start | bytes 393224 | tf_op jit(solution)/shard_map/ppermute | solution.py:464
  39.4 33.4 %all-to-all-start = ((f32[8,72,128]{2,1,0:T(8,128)}), f32[8,72,128]{2,1,0:T(8,128)S(1)}, u32[]{:S(2)}, u32[]{:S(2)}) async-start(f32[8,72,128]{2,1,0:T(8,128)} %shard_map.174), calls=%async_computation | async-start | bytes 589824 | tf_op jit(solution)/shard_map/all_to_all | solution.py:646
  44.9 4.7 %collective-permute-start.15 = (f32[4,32,128]{2,1,0:T(8,128)S(1)}, f32[4,32,128]{2,1,0:T(8,128)S(1)}, u32[]{:S(2)}, u32[]{:S(2)}) collective-permute-start(f32[4,32,128]{2,1,0:T(8,128)S(1)} %get-tuple-element.77), channel_id=1, source_target_pairs={{0,2},{1,3},{2,0},{3,1},{4,6},{5,7},{6,4},{7,5},{8,10},{9,11},{10,... | collective-permute-start | bytes 196616 | tf_op jit(solution)/shard_map/ppermute | solution.py:471
  45.5 6.3 %collective-permute-start.16 = (f32[4,32,128]{2,1,0:T(8,128)S(1)}, f32[4,32,128]{2,1,0:T(8,128)S(1)}, u32[]{:S(2)}, u32[]{:S(2)}) collective-permute-start(f32[4,32,128]{2,1,0:T(8,128)S(1)} %get-tuple-element.78), channel_id=1, source_target_pairs={{0,4},{1,5},{2,6},{3,7},{4,0},{5,1},{6,2},{7,3},{8,12},{9,13},{10,... | collective-permute-start | bytes 196616 | tf_op jit(solution)/shard_map/ppermute | solution.py:471
  47.5 5.4 %collective-permute-start.17 = (f32[4,32,128]{2,1,0:T(8,128)S(1)}, f32[4,32,128]{2,1,0:T(8,128)S(1)}, u32[]{:S(2)}, u32[]{:S(2)}) collective-permute-start(f32[4,32,128]{2,1,0:T(8,128)S(1)} %get-tuple-element.79), channel_id=1, source_target_pairs={{0,6},{1,7},{2,4},{3,5},{4,2},{5,3},{6,0},{7,1},{8,14},{9,15},{10,... | collective-permute-start | bytes 196616 | tf_op jit(solution)/shard_map/ppermute | solution.py:471
  52.9 4.5 %collective-permute-start.18 = (f32[4,32,128]{2,1,0:T(8,128)S(1)}, f32[4,32,128]{2,1,0:T(8,128)S(1)}, u32[]{:S(2)}, u32[]{:S(2)}) collective-permute-start(f32[4,32,128]{2,1,0:T(8,128)S(1)} %shard_map.168.a_ref), channel_id=1, source_target_pairs={{0,8},{4,12},{8,0},{12,4},{16,24},{20,28},{24,16},{28,20},{1,9},{5... | collective-permute-start | bytes 196616 | tf_op jit(solution)/shard_map/ppermute | solution.py:467
  54.6 6.6 %collective-permute-start.19 = (f32[4,32,128]{2,1,0:T(8,128)S(1)}, f32[4,32,128]{2,1,0:T(8,128)S(1)}, u32[]{:S(2)}, u32[]{:S(2)}) collective-permute-start(f32[4,32,128]{2,1,0:T(8,128)S(1)} %shard_map.168.a_ref), channel_id=1, source_target_pairs={{0,16},{4,20},{8,24},{12,28},{16,0},{20,4},{24,8},{28,12},{1,17},{... | collective-permute-start | bytes 196616 | tf_op jit(solution)/shard_map/ppermute | solution.py:467
  56.8 6.1 %collective-permute-start.20 = (f32[4,32,128]{2,1,0:T(8,128)S(1)}, f32[4,32,128]{2,1,0:T(8,128)S(1)}, u32[]{:S(2)}, u32[]{:S(2)}) collective-permute-start(f32[4,32,128]{2,1,0:T(8,128)S(1)} %shard_map.168.a_ref), channel_id=1, source_target_pairs={{0,24},{4,28},{8,16},{12,20},{16,8},{20,12},{24,0},{28,4},{1,25},{... | collective-permute-start | bytes 196616 | tf_op jit(solution)/shard_map/ppermute | solution.py:467
  62.9 4.3 %collective-permute-start.21 = (f32[4,32,128]{2,1,0:T(8,128)S(1)}, f32[4,32,128]{2,1,0:T(8,128)S(1)}, u32[]{:S(2)}, u32[]{:S(2)}) collective-permute-start(f32[4,32,128]{2,1,0:T(8,128)S(1)} %shard_map.169.refs_0_), channel_id=1, source_target_pairs={{0,2},{1,3},{2,0},{3,1},{4,6},{5,7},{6,4},{7,5},{8,10},{9,11},{10,... | collective-permute-start | bytes 196616 | tf_op jit(solution)/shard_map/ppermute | solution.py:471
  64.2 4.3 %collective-permute-start.22 = (f32[4,32,128]{2,1,0:T(8,128)S(1)}, f32[4,32,128]{2,1,0:T(8,128)S(1)}, u32[]{:S(2)}, u32[]{:S(2)}) collective-permute-start(f32[4,32,128]{2,1,0:T(8,128)S(1)} %shard_map.169.refs_0_), channel_id=1, source_target_pairs={{0,4},{1,5},{2,6},{3,7},{4,0},{5,1},{6,2},{7,3},{8,12},{9,13},{10,... | collective-permute-start | bytes 196616 | tf_op jit(solution)/shard_map/ppermute | solution.py:471
  64.8 5.2 %collective-permute-start.23 = (f32[4,32,128]{2,1,0:T(8,128)S(1)}, f32[4,32,128]{2,1,0:T(8,128)S(1)}, u32[]{:S(2)}, u32[]{:S(2)}) collective-permute-start(f32[4,32,128]{2,1,0:T(8,128)S(1)} %shard_map.169.refs_0_), channel_id=1, source_target_pairs={{0,6},{1,7},{2,4},{3,5},{4,2},{5,3},{6,0},{7,1},{8,14},{9,15},{10,... | collective-permute-start | bytes 196616 | tf_op jit(solution)/shard_map/ppermute | solution.py:471
  70.0 1.6 %collective-permute-start.24 = (f32[512,128]{1,0:T(8,128)S(1)}, f32[512,128]{1,0:T(8,128)S(1)}, u32[]{:S(2)}, u32[]{:S(2)}) collective-permute-start(f32[512,128]{1,0:T(8,128)S(1)} %bitcast.9), channel_id=1, source_target_pairs={{0,1},{1,0},{2,3},{3,2},{4,5},{5,4},{6,7},{7,6},{8,9},{9,8},{10,11... | collective-permute-start | bytes 786440 | tf_op jit(solution)/shard_map/ppermute | solution.py:464

commit v5 on v4

--- a/solution.py
+++ b/solution.py
@@ -126,9 +126,26 @@
     out_ref[at[3] : at[4], :] = padded(jnp.concatenate([hi, mid, low], axis=0), 16).astype(BF16)
 
 
-def place_kernel(
-    mp_count, slots, share, map_ref, ids_ref, hot_hbm, hot_ids_hbm, weight_hbm, grads_hbm,
-    pos_ref, row_ref, hot_ref, hot_ids_ref, weight_ref, grads_ref, sems,
+def place_kernel(mp_count, slots, map_ref, ids_ref, pos_ref, row_ref):
+    touch = ids_ref.shape[1]
+    map_rows, lanes = map_ref.shape
+    ids_col = column(ids_ref[...])
+    in_row = (iota((touch, map_rows), 1) == ids_col // lanes).astype(F32)
+    picked = lax.dot_general(
+        in_row, map_ref[...].astype(F32), (((1,), (0,)), ((), ())),
+        precision=lax.Precision.HIGHEST, preferred_element_type=F32,
+    )
+    in_lane = iota((touch, lanes), 1) == ids_col % lanes
+    stored = jnp.sum(jnp.where(in_lane, picked, 0.0), axis=1, keepdims=True).astype(I32)
+    stored = jnp.broadcast_to(stored, (touch, lanes))
+    pos = stored // (mp_count * slots) * slots + stored % slots
+    pos_ref[...] = pos
+    row_ref[...] = pos.T[:8, :]
+
+
+def load_kernel(
+    share, hot_hbm, hot_ids_hbm, weight_hbm, grads_hbm,
+    hot_ref, hot_ids_ref, weight_ref, grads_ref, sems,
 ):
     my = lax.axis_index("mp")
     mine = grads_hbm.at[pl.ds(pl.multiple_of(my * share, share), share), :]
@@ -140,20 +157,6 @@
     ]
     for copy in copies:
         copy.start()
-    touch = ids_ref.shape[1]
-    map_rows, lanes = map_ref.shape
-    ids_col = column(ids_ref[...])
-    in_row = (iota((touch, map_rows), 1) == ids_col // lanes).astype(F32)
-    picked = lax.dot_general(
-        in_row, map_ref[...].astype(F32), (((1,), (0,)), ((), ())),
-        precision=lax.Precision.HIGHEST, preferred_element_type=F32,
-    )
-    in_lane = iota((touch, lanes), 1) == ids_col % lanes
-    stored = jnp.sum(jnp.where(in_lane, picked, 0.0), axis=1, keepdims=True).astype(I32)
-    stored = jnp.broadcast_to(stored, (touch, lanes))
-    pos = stored // (mp_count * slots) * slots + stored % slots
-    pos_ref[...] = pos
-    row_ref[...] = pos.T[:8, :]
     for copy in copies:
         copy.wait()
 
@@ -508,18 +511,21 @@
     pack_near = swap(pack, 1)
     packs = [pack, pack_near, pack_far, swap(pack_far, 1)]
 
-    pos, pos_row, hot_near, ids_near, weight_near, grads_near = call(
-        lambda *r: place_kernel(mp_count, slots, share, *r),
+    pos, pos_row = call(
+        lambda *r: place_kernel(mp_count, slots, *r),
+        [((touch, emb), I32, True), ((8, touch), I32, True)],
+        [map_rows, touched_row],
+    )
+    hot_near, ids_near, weight_near, grads_near = call(
+        lambda *r: load_kernel(share, *r),
         [
-            ((touch, emb), I32, True),
-            ((8, touch), I32, True),
             (hot_table.shape, F32, True),
             ((fields, samples), I32, True),
             (weight_in.shape, BF16, True),
             ((share, grad_out.shape[1]), BF16, True),
         ],
-        [map_rows, touched_row, hot_table, hot_ids.T, weight_in, grad_out],
-        raw=range(2, 6),
+        [hot_table, hot_ids.T, weight_in, grad_out],
+        raw=range(4),
         scratch=[pltpu.SemaphoreType.DMA((4,))],
     )
     weights[0] = weight_near
@@ -668,7 +674,7 @@
             P(),
             P("dp", None),
             P(None, "mp"),
-            P("mp"),
+            P("mp",),
             P("mp", None),
             P(),
             P(),

time: 74.2 us -> 74.8 us (level)
  starting transfers between devices: 32.8 us -> 30.2 us
  waiting for transfers between devices: 27.1 us -> 29.6 us
    ppermute x11, waiting for transfers between devices: 7.34 us -> 9.32 us  [swap(): return lax.ppermute(x, 'mp', [(i, i ^ mask) for i in range(mp_count)])]
    all_to_all x1, starting transfers between devices: 5.5 us -> 4.16 us  [per_device(): lax.all_to_all(outgoing, 'dp', split_axis=0, concat_axis=0, tiled=True)]
    ppermute x11, starting transfers between devices: 6.12 us -> 4.91 us  [swap(): return lax.ppermute(x, 'mp', [(i, i ^ mask) for i in range(mp_count)])]
    pallas_call x20 -> x21, Pallas kernels: 13.2 us -> 13.8 us  [call(): pl.pallas_call(body, out_shape=avals, in_specs=[ANY if i in raw else VM f...]
  transfers between devices with their start and end apart: 28 -> 28, of which waited for: 17 -> 17; matrix products, arithmetic and copies ran while one was open for 0% -> 0% of each run, Pallas kernels for 13% -> 14%
where the time goes in v5:
time: 74.8 us; the launch traced here: 74.5 us
  starting transfers between devices  30.2 us (40%)
  waiting for transfers between devices  29.6 us (40%)
  Pallas kernels  13.8 us (18%)
  between operations  0.86 us (1%)
    pallas_call x21, Pallas kernels, call(): pl.pallas_call(body, out_shape=avals, in_specs=[ANY if i in raw else VM f...  13.8 us
    ppermute x9, waiting for transfers between devices, near_swap(): lax.ppermute(x, both, [(i, i ^ mask) for i in range(dp_count * mp_count)])  11.7 us
    ppermute x9, starting transfers between devices, near_swap(): lax.ppermute(x, both, [(i, i ^ mask) for i in range(dp_count * mp_count)])  10.7 us
    ppermute x7, starting transfers between devices, far_swap(): return lax.ppermute(x, 'dp', [(i, i ^ mask) for i in range(dp_count)])  10.5 us
    ppermute x11, waiting for transfers between devices, swap(): return lax.ppermute(x, 'mp', [(i, i ^ mask) for i in range(mp_count)])  9.32 us
    ppermute x7, waiting for transfers between devices, far_swap(): return lax.ppermute(x, 'dp', [(i, i ^ mask) for i in range(dp_count)])  8.57 us
    ppermute x11, starting transfers between devices, swap(): return lax.ppermute(x, 'mp', [(i, i ^ mask) for i in range(mp_count)])  4.91 us
    all_to_all x1, starting transfers between devices, per_device(): lax.all_to_all(outgoing, 'dp', split_axis=0, concat_axis=0, tiled=True)  4.16 us
  transfers between devices with their start and end apart: 28, of which 17 were waited for; matrix products, arithmetic and copies ran while one was open for 0% of the time, Pallas kernels for 14%

profile of v5, /device:TPU:0, one launch (start us, length us, event | category | flops | bytes accessed | tf_op | source)
XLA Modules:
  0.0 74.5 jit_solution(9629288538278347842)
XLA Ops:
  0.6 3.0 %collective-permute-start.12 = (bf16[1024,128]{1,0:T(8,128)(2,1)}, bf16[1024,128]{1,0:T(8,128)(2,1)S(1)}, u32[]{:S(2)}, u32[]{:S(2)}) collective-permute-start(bf16[1024,128]{1,0:T(8,128)(2,1)} %r_2_.2), channel_id=1, source_target_pairs={{0,2},{1,3},{2,0},{3,1},{4,6},{5,7},{6,4},{7,5},{8,10},{9,11},{10,... | collective-permute-start | bytes 786440 | tf_op jit(solution)/shard_map/ppermute | solution.py:467
  3.7 1.0 %shard_map.158 = (bf16[256,128]{1,0:T(8,128)(2,1)S(1)}, s32[64,128]{1,0:T(8,128)S(1)}, s32[1,256]{1,0:T(1,128)S(1)}, bf16[128,256]{1,0:T(8,128)(2,1)S(1)}, s32[1...) custom-call(f32[256,128]{1,0:T(8,128)} %r_1_.1, s32[64,128]{1,0:T(8,128)} %bitcast.13, ...), custom_call_target="tpu_custom_call" | custom-call | tf_op jit(solution)/shard_map/pallas_call | solution.py:60
  4.7 1.6 %collective-permute-start.4 = (bf16[256,128]{1,0:T(8,128)(2,1)S(1)}, bf16[256,128]{1,0:T(8,128)(2,1)S(1)}, u32[]{:S(2)}, u32[]{:S(2)}) collective-permute-start(bf16[256,128]{1,0:T(8,128)(2,1)S(1)} %get-tuple-element.60.refs_0_), channel_id=1, source_target_pairs={{0,8},{4,12},{8,0},{12,4},{16,24},{20,28},{24,16},{28,20},{1,9},{5... | collective-permute-start | bytes 196616 | tf_op jit(solution)/shard_map/ppermute | solution.py:470
  6.3 2.6 %collective-permute-start.5 = (bf16[256,128]{1,0:T(8,128)(2,1)S(1)}, bf16[256,128]{1,0:T(8,128)(2,1)S(1)}, u32[]{:S(2)}, u32[]{:S(2)}) collective-permute-start(bf16[256,128]{1,0:T(8,128)(2,1)S(1)} %get-tuple-element.60.refs_0_), channel_id=1, source_target_pairs={{0,16},{4,20},{8,24},{12,28},{16,0},{20,4},{24,8},{28,12},{1,17},{... | collective-permute-start | bytes 196616 | tf_op jit(solution)/shard_map/ppermute | solution.py:470
  9.1 0.7 shard_map.162
  9.8 1.6 %collective-permute-start.3 = (s32[8,256]{1,0:T(8,128)S(1)}, s32[8,256]{1,0:T(8,128)S(1)}, u32[]{:S(2)}, u32[]{:S(2)}) collective-permute-start(s32[8,256]{1,0:T(8,128)S(1)} %get-tuple-element.59), channel_id=1, source_target_pairs={{0,4},{4,0},{8,12},{12,8},{16,20},{20,16},{24,28},{28,24},{1,5},{5... | collective-permute-start | bytes 24584 | tf_op jit(solution)/shard_map/ppermute | solution.py:470
  11.4 2.1 %collective-permute-done.3.row_ref = s32[8,256]{1,0:T(8,128)S(1)} collective-permute-done((s32[8,256]{1,0:T(8,128)S(1)}, s32[8,256]{1,0:T(8,128)S(1)}, u32[]{:S(2)}, u32[]{:S(2)}) %collective-permute-start.3) | collective-permute-done | bytes 8224 | tf_op jit(solution)/shard_map/ppermute | solution.py:470
  14.0 1.0 %collective-permute-done.6.refs_3_ = bf16[256,128]{1,0:T(8,128)(2,1)S(1)} collective-permute-done((bf16[256,128]{1,0:T(8,128)(2,1)S(1)}, bf16[256,128]{1,0:T(8,128)(2,1)S(1)}, u32[]{:S(2)}, u32[]{:S(2)}) %collective-permute-start.6) | collective-permute-done | bytes 65568 | tf_op jit(solution)/shard_map/ppermute | solution.py:470
  15.0 0.6 shard_map.163
  15.6 1.6 %collective-permute-start.7 = (bf16[256,128]{1,0:T(8,128)(2,1)S(1)}, bf16[256,128]{1,0:T(8,128)(2,1)S(1)}, u32[]{:S(2)}, u32[]{:S(2)}) collective-permute-start(bf16[256,128]{1,0:T(8,128)(2,1)S(1)} %get-tuple-element.62), channel_id=1, source_target_pairs={{0,4},{1,5},{2,6},{3,7},{4,0},{5,1},{6,2},{7,3},{8,12},{9,13},{10,... | collective-permute-start | bytes 196616 | tf_op jit(solution)/shard_map/ppermute | solution.py:474
  17.7 1.4 %collective-permute-start.9 = (bf16[256,128]{1,0:T(8,128)(2,1)S(1)}, bf16[256,128]{1,0:T(8,128)(2,1)S(1)}, u32[]{:S(2)}, u32[]{:S(2)}) collective-permute-start(bf16[256,128]{1,0:T(8,128)(2,1)S(1)} %get-tuple-element.62), channel_id=1, source_target_pairs={{0,6},{1,7},{2,4},{3,5},{4,2},{5,3},{6,0},{7,1},{8,14},{9,15},{10,... | collective-permute-start | bytes 196616 | tf_op jit(solution)/shard_map/ppermute | solution.py:474
  19.2 1.5 %collective-permute-done.7.near_ref = bf16[256,128]{1,0:T(8,128)(2,1)S(1)} collective-permute-done((bf16[256,128]{1,0:T(8,128)(2,1)S(1)}, bf16[256,128]{1,0:T(8,128)(2,1)S(1)}, u32[]{:S(2)}, u32[]{:S(2)}) %collective-permute-start.7) | collective-permute-done | bytes 65568 | tf_op jit(solution)/shard_map/ppermute | solution.py:474
  20.6 1.3 %collective-permute-done.8.far_ref = bf16[256,128]{1,0:T(8,128)(2,1)S(1)} collective-permute-done((bf16[256,128]{1,0:T(8,128)(2,1)S(1)}, bf16[256,128]{1,0:T(8,128)(2,1)S(1)}, u32[]{:S(2)}, u32[]{:S(2)}) %collective-permute-start.8) | collective-permute-done | bytes 65568 | tf_op jit(solution)/shard_map/ppermute | solution.py:474
  22.0 1.0 %collective-permute-done.9.cross_ref = bf16[256,128]{1,0:T(8,128)(2,1)S(1)} collective-permute-done((bf16[256,128]{1,0:T(8,128)(2,1)S(1)}, bf16[256,128]{1,0:T(8,128)(2,1)S(1)}, u32[]{:S(2)}, u32[]{:S(2)}) %collective-permute-start.9) | collective-permute-done | bytes 65568 | tf_op jit(solution)/shard_map/ppermute | solution.py:474
  23.5 1.5 %collective-permute-done.1.r_0_.r_6_ = bf16[304,128]{1,0:T(8,128)(2,1)S(1)} collective-permute-done((bf16[304,128]{1,0:T(8,128)(2,1)S(1)}, bf16[304,128]{1,0:T(8,128)(2,1)S(1)}, u32[]{:S(2)}, u32[]{:S(2)}) %collective-permute-start.1) | collective-permute-done | bytes 77856 | tf_op jit(solution)/shard_map/ppermute | solution.py:467
  25.0 1.2 %shard_map.156 = (f32[1024,128]{1,0:T(8,128)S(1)}, s32[7,1024]{1,0:T(8,128)S(1)}, bf16[1024,128]{1,0:T(8,128)(2,1)S(1)}, bf16[256,256]{1,0:T(8,128)(2,1)S(1)}) custom-call(f32[1024,128]{1,0:T(8,128)} %table_ref.1, s32[7,1024]{1,0:T(8,128)} %bitcast.14, bf16[1024,128]{1,0:T(8,128)(2,1)} %r_2_.2, bf16[1024,256]{1,0:T(8,128)(2,1)} %r_3_.2), custom_call_target="tpu_custom_call" | custom-call | tf_op jit(solution)/shard_map/pallas_call | solution.py:60
  26.2 1.2 %shard_map.157 = (bf16[1024,1792]{1,0:T(8,128)(2,1)S(1)}, bf16[896,256]{1,0:T(8,128)(2,1)S(1)}) custom-call(s32[7,1024]{1,0:T(8,128)S(1)} %get-tuple-element.47.r_0_, f32[1024,128]{1,0:T(8,128)S(1)} %get-tuple-element.48.r_1_), custom_call_target="tpu_custom_call" | custom-call | tf_op jit(solution)/shard_map/pallas_call | solution.py:60
  27.4 1.0 %shard_map.160 = (bf16[256,512]{1,0:T(8,128)(2,1)S(1)}, bf16[512,256]{1,0:T(8,128)(2,1)S(1)}) custom-call(bf16[304,128]{1,0:T(8,128)(2,1)S(1)} %shard_map.159.r_0_.r_4_, bf16[304,128]{1,0:T(8,128)(2,1)S(1)} %collective-permute-done.r_1_.r_5_), custom_call_target="tpu_custom_call" | custom-call | tf_op jit(solution)/shard_map/pallas_call | solution.py:60
  28.5 1.0 %shard_map.161 = (bf16[256,512]{1,0:T(8,128)(2,1)S(1)}, bf16[512,256]{1,0:T(8,128)(2,1)S(1)}) custom-call(bf16[304,128]{1,0:T(8,128)(2,1)S(1)} %collective-permute-done.1.r_0_.r_6_, bf16[304,128]{1,0:T(8,128)(2,1)S(1)} %collective-permute-done.2.r_1_.r_7_), custom_call_target="tpu_custom_call" | custom-call | tf_op jit(solution)/shard_map/pallas_call | solution.py:60
  29.5 0.8 %shard_map.165 = (bf16[512,1024]{1,0:T(8,128)(2,1)S(1)}, bf16[128,512]{1,0:T(8,128)(2,1)S(1)}, f32[256,512]{1,0:T(8,128)S(1)}, f32[256,512]{1,0:T(8,128)S(1)}) custom-call(bf16[1024,128]{1,0:T(8,128)(2,1)S(1)} %get-tuple-element.63.r_0_, bf16[1024,128]{1,0:T(8,128)(2,1)S(1)} %collective-permute-done.11.r_1_, ...), custom_call_target="tpu_custom_call" | custom-call | tf_op jit(solution)/shard_map/pallas_call | solution.py:60
  30.4 1.5 %shard_map.166 = (bf16[1792,256]{1,0:T(8,128)(2,1)S(1)}, bf16[256,256]{1,0:T(8,128)(2,1)S(1)}, f32[512,128]{1,0:T(8,128)S(1)}) custom-call(bf16[256,512]{1,0:T(8,128)(2,1)S(1)} %get-tuple-element.54.r_0_, bf16[256,512]{1,0:T(8,128)(2,1)S(1)} %get-tuple-element.55.r_1_, bf16[2,256,128]{2,1,0:T(8,128)(2,1)S(1)} %shard_map.164.r_2_, ...), custom_call_target="tpu_custom_call" | custom-call | tf_op jit(solution)/shard_map/pallas_call | solution.py:60
  31.9 0.8 %shard_map.167 = (f32[512,128]{1,0:T(8,128)S(1)}, f32[2,256,128]{2,1,0:T(8,128)S(1)}, f32[2,256,128]{2,1,0:T(8,128)S(1)}) custom-call(bf16[1024,1792]{1,0:T(8,128)(2,1)S(1)} %get-tuple-element.49.r_8_.oht_ref, bf16[1792,256]{1,0:T(8,128)(2,1)S(1)} %get-tuple-element.70.ig_ref, bf16[256,256]{1,0:T(8,128)(2,1)S(1)} %get-tuple-element.71.bag_ref, ...), custom_call_target="tpu_custom_call" | custom-call | tf_op jit(solution)/shard_map/pallas_call | solution.py:60
  32.7 0.6 collective-permute-start.25
  33.4 1.1 %collective-permute-done.25.got_ref = f32[2,256,128]{2,1,0:T(8,128)S(1)} collective-permute-done((f32[2,256,128]{2,1,0:T(8,128)S(1)}, f32[2,256,128]{2,1,0:T(8,128)S(1)}, u32[]{:S(2)}, u32[]{:S(2)}) %collective-permute-start.25) | collective-permute-done | bytes 262176 | tf_op jit(solution)/shard_map/ppermute | solution.py:467
  34.6 0.5 shard_map.174
  35.1 5.2 %collective-permute-done.26.r_1_ = f32[256,128]{1,0:T(8,128)S(1)} collective-permute-done((f32[256,128]{1,0:T(8,128)S(1)}, f32[256,128]{1,0:T(8,128)S(1)}, u32[]{:S(2)}, u32[]{:S(2)}) %collective-permute-start.26) | collective-permute-done | bytes 131104 | tf_op jit(solution)/shard_map/ppermute | solution.py:467
  40.3 1.0 %shard_map.175 = f32[8,72,128]{2,1,0:T(8,128)} custom-call(f32[256,128]{1,0:T(8,128)S(1)} %get-tuple-element.84.r_0_, f32[256,128]{1,0:T(8,128)S(1)} %collective-permute-done.26.r_1_, bf16[512,256]{1,0:T(8,128)(2,1)S(1)} %get-tuple-element.86.r_2_, f32[64,128]{1,0:T(8,128)S(1)} %get-tuple-element.87.r_3_), custom_call_target="tpu_custom_call" | custom-call | tf_op jit(solution)/shard_map/pallas_call | solution.py:60
  41.3 4.2 %all-to-all-start = ((f32[8,72,128]{2,1,0:T(8,128)}), f32[8,72,128]{2,1,0:T(8,128)S(1)}, u32[]{:S(2)}, u32[]{:S(2)}) async-start(f32[8,72,128]{2,1,0:T(8,128)} %shard_map.175), calls=%async_computation | async-start | bytes 589824 | tf_op jit(solution)/shard_map/all_to_all | solution.py:652
  45.5 0.6 collective-permute-start.15
  46.1 2.0 %collective-permute-start.16 = (f32[4,32,128]{2,1,0:T(8,128)S(1)}, f32[4,32,128]{2,1,0:T(8,128)S(1)}, u32[]{:S(2)}, u32[]{:S(2)}) collective-permute-start(f32[4,32,128]{2,1,0:T(8,128)S(1)} %get-tuple-element.78), channel_id=1, source_target_pairs={{0,4},{1,5},{2,6},{3,7},{4,0},{5,1},{6,2},{7,3},{8,12},{9,13},{10,... | collective-permute-start | bytes 196616 | tf_op jit(solution)/shard_map/ppermute | solution.py:474
  48.1 0.9 %collective-permute-start.17 = (f32[4,32,128]{2,1,0:T(8,128)S(1)}, f32[4,32,128]{2,1,0:T(8,128)S(1)}, u32[]{:S(2)}, u32[]{:S(2)}) collective-permute-start(f32[4,32,128]{2,1,0:T(8,128)S(1)} %get-tuple-element.79), channel_id=1, source_target_pairs={{0,6},{1,7},{2,4},{3,5},{4,2},{5,3},{6,0},{7,1},{8,14},{9,15},{10,... | collective-permute-start | bytes 196616 | tf_op jit(solution)/shard_map/ppermute | solution.py:474
  49.0 1.2 %collective-permute-done.15.b_ref = f32[4,32,128]{2,1,0:T(8,128)S(1)} collective-permute-done((f32[4,32,128]{2,1,0:T(8,128)S(1)}, f32[4,32,128]{2,1,0:T(8,128)S(1)}, u32[]{:S(2)}, u32[]{:S(2)}) %collective-permute-start.15) | collective-permute-done | bytes 65568 | tf_op jit(solution)/shard_map/ppermute | solution.py:474
  50.3 2.1 %collective-permute-done.16.c_ref = f32[4,32,128]{2,1,0:T(8,128)S(1)} collective-permute-done((f32[4,32,128]{2,1,0:T(8,128)S(1)}, f32[4,32,128]{2,1,0:T(8,128)S(1)}, u32[]{:S(2)}, u32[]{:S(2)}) %collective-permute-start.16) | collective-permute-done | bytes 65568 | tf_op jit(solution)/shard_map/ppermute | solution.py:474
  52.4 1.1 %collective-permute-done.17.d_ref = f32[4,32,128]{2,1,0:T(8,128)S(1)} collective-permute-done((f32[4,32,128]{2,1,0:T(8,128)S(1)}, f32[4,32,128]{2,1,0:T(8,128)S(1)}, u32[]{:S(2)}, u32[]{:S(2)}) %collective-permute-start.17) | collective-permute-done | bytes 65568 | tf_op jit(solution)/shard_map/ppermute | solution.py:474
  53.5 1.7 %collective-permute-start.18 = (f32[4,32,128]{2,1,0:T(8,128)S(1)}, f32[4,32,128]{2,1,0:T(8,128)S(1)}, u32[]{:S(2)}, u32[]{:S(2)}) collective-permute-start(f32[4,32,128]{2,1,0:T(8,128)S(1)} %shard_map.169.a_ref), channel_id=1, source_target_pairs={{0,8},{4,12},{8,0},{12,4},{16,24},{20,28},{24,16},{28,20},{1,9},{5... | collective-permute-start | bytes 196616 | tf_op jit(solution)/shard_map/ppermute | solution.py:470
  55.2 2.2 %collective-permute-start.19 = (f32[4,32,128]{2,1,0:T(8,128)S(1)}, f32[4,32,128]{2,1,0:T(8,128)S(1)}, u32[]{:S(2)}, u32[]{:S(2)}) collective-permute-start(f32[4,32,128]{2,1,0:T(8,128)S(1)} %shard_map.169.a_ref), channel_id=1, source_target_pairs={{0,16},{4,20},{8,24},{12,28},{16,0},{20,4},{24,8},{28,12},{1,17},{... | collective-permute-start | bytes 196616 | tf_op jit(solution)/shard_map/ppermute | solution.py:470
  57.4 0.6 collective-permute-start.20
  58.0 3.8 %collective-permute-done.19.c_ref = f32[4,32,128]{2,1,0:T(8,128)S(1)} collective-permute-done((f32[4,32,128]{2,1,0:T(8,128)S(1)}, f32[4,32,128]{2,1,0:T(8,128)S(1)}, u32[]{:S(2)}, u32[]{:S(2)}) %collective-permute-start.19) | collective-permute-done | bytes 65568 | tf_op jit(solution)/shard_map/ppermute | solution.py:470
  61.8 1.7 %collective-permute-done.20.d_ref = f32[4,32,128]{2,1,0:T(8,128)S(1)} collective-permute-done((f32[4,32,128]{2,1,0:T(8,128)S(1)}, f32[4,32,128]{2,1,0:T(8,128)S(1)}, u32[]{:S(2)}, u32[]{:S(2)}) %collective-permute-start.20) | collective-permute-done | bytes 65568 | tf_op jit(solution)/shard_map/ppermute | solution.py:470
  63.4 1.4 %collective-permute-start.21 = (f32[4,32,128]{2,1,0:T(8,128)S(1)}, f32[4,32,128]{2,1,0:T(8,128)S(1)}, u32[]{:S(2)}, u32[]{:S(2)}) collective-permute-start(f32[4,32,128]{2,1,0:T(8,128)S(1)} %shard_map.170.refs_0_), channel_id=1, source_target_pairs={{0,2},{1,3},{2,0},{3,1},{4,6},{5,7},{6,4},{7,5},{8,10},{9,11},{10,... | collective-permute-start | bytes 196616 | tf_op jit(solution)/shard_map/ppermute | solution.py:474
  64.8 0.6 collective-permute-start.22
  65.4 1.6 %collective-permute-start.23 = (f32[4,32,128]{2,1,0:T(8,128)S(1)}, f32[4,32,128]{2,1,0:T(8,128)S(1)}, u32[]{:S(2)}, u32[]{:S(2)}) collective-permute-start(f32[4,32,128]{2,1,0:T(8,128)S(1)} %shard_map.170.refs_0_), channel_id=1, source_target_pairs={{0,6},{1,7},{2,4},{3,5},{4,2},{5,3},{6,0},{7,1},{8,14},{9,15},{10,... | collective-permute-start | bytes 196616 | tf_op jit(solution)/shard_map/ppermute | solution.py:474
  67.0 0.8 %collective-permute-done.21.refs_1_ = f32[4,32,128]{2,1,0:T(8,128)S(1)} collective-permute-done((f32[4,32,128]{2,1,0:T(8,128)S(1)}, f32[4,32,128]{2,1,0:T(8,128)S(1)}, u32[]{:S(2)}, u32[]{:S(2)}) %collective-permute-start.21) | collective-permute-done | bytes 65568 | tf_op jit(solution)/shard_map/ppermute | solution.py:474
  67.8 1.3 %collective-permute-done.22.refs_2_ = f32[4,32,128]{2,1,0:T(8,128)S(1)} collective-permute-done((f32[4,32,128]{2,1,0:T(8,128)S(1)}, f32[4,32,128]{2,1,0:T(8,128)S(1)}, u32[]{:S(2)}, u32[]{:S(2)}) %collective-permute-start.22) | collective-permute-done | bytes 65568 | tf_op jit(solution)/shard_map/ppermute | solution.py:474
  69.1 1.5 %collective-permute-done.23.refs_3_ = f32[4,32,128]{2,1,0:T(8,128)S(1)} collective-permute-done((f32[4,32,128]{2,1,0:T(8,128)S(1)}, f32[4,32,128]{2,1,0:T(8,128)S(1)}, u32[]{:S(2)}, u32[]{:S(2)}) %collective-permute-start.23) | collective-permute-done | bytes 65568 | tf_op jit(solution)/shard_map/ppermute | solution.py:474
  70.7 1.5 %collective-permute-done.24.theirs_ref = f32[512,128]{1,0:T(8,128)S(1)} collective-permute-done((f32[512,128]{1,0:T(8,128)S(1)}, f32[512,128]{1,0:T(8,128)S(1)}, u32[]{:S(2)}, u32[]{:S(2)}) %collective-permute-start.24) | collective-permute-done | bytes 262176 | tf_op jit(solution)/shard_map/ppermute | solution.py:467
  72.2 1.2 %shard_map.172 = (f32[1024,128]{1,0:T(8,128)}, f32[1024,128]{1,0:T(8,128)}) custom-call(f32[512,128]{1,0:T(8,128)S(1)} %bitcast.10, f32[512,128]{1,0:T(8,128)S(1)} %collective-permute-done.24.theirs_ref, f32[1024,128]{1,0:T(8,128)S(1)} %copy-done, f32[1024,128]{1,0:T(8,128)S(1)} %copy-done.1), custom_call_target="tpu_custom_call" | custom-call | tf_op jit(solution)/shard_map/pallas_call | solution.py:60
  73.4 1.1 %shard_map.176 = (f32[256,128]{1,0:T(8,128)}, f32[256,128]{1,0:T(8,128)}) custom-call(f32[8,72,128]{2,1,0:T(8,128)S(1)} %all-to-all-done.r_0_, f32[256,128]{1,0:T(8,128)S(1)} %copy-done.2, f32[256,128]{1,0:T(8,128)S(1)} %copy-done.3), custom_call_target="tpu_custom_call" | custom-call | tf_op jit(solution)/shard_map/pallas_call | solution.py:60
  (37 shorter events, 2.3 us)
Async XLA Ops:
  0.6 12.9 %collective-permute-start.12 = (bf16[1024,128]{1,0:T(8,128)(2,1)}, bf16[1024,128]{1,0:T(8,128)(2,1)S(1)}, u32[]{:S(2)}, u32[]{:S(2)}) collective-permute-start(bf16[1024,128]{1,0:T(8,128)(2,1)} %r_2_.2), channel_id=1, source_target_pairs={{0,2},{1,3},{2,0},{3,1},{4,6},{5,7},{6,4},{7,5},{8,10},{9,11},{10,... | collective-permute-start | bytes 786440 | tf_op jit(solution)/shard_map/ppermute | solution.py:467
  4.7 9.3 %collective-permute-start.4 = (bf16[256,128]{1,0:T(8,128)(2,1)S(1)}, bf16[256,128]{1,0:T(8,128)(2,1)S(1)}, u32[]{:S(2)}, u32[]{:S(2)}) collective-permute-start(bf16[256,128]{1,0:T(8,128)(2,1)S(1)} %get-tuple-element.60.refs_0_), channel_id=1, source_target_pairs={{0,8},{4,12},{8,0},{12,4},{16,24},{20,28},{24,16},{28,20},{1,9},{5... | collective-permute-start | bytes 196616 | tf_op jit(solution)/shard_map/ppermute | solution.py:470
  6.3 7.7 %collective-permute-start.5 = (bf16[256,128]{1,0:T(8,128)(2,1)S(1)}, bf16[256,128]{1,0:T(8,128)(2,1)S(1)}, u32[]{:S(2)}, u32[]{:S(2)}) collective-permute-start(bf16[256,128]{1,0:T(8,128)(2,1)S(1)} %get-tuple-element.60.refs_0_), channel_id=1, source_target_pairs={{0,16},{4,20},{8,24},{12,28},{16,0},{20,4},{24,8},{28,12},{1,17},{... | collective-permute-start | bytes 196616 | tf_op jit(solution)/shard_map/ppermute | solution.py:470
  8.9 6.1 %collective-permute-start.6 = (bf16[256,128]{1,0:T(8,128)(2,1)S(1)}, bf16[256,128]{1,0:T(8,128)(2,1)S(1)}, u32[]{:S(2)}, u32[]{:S(2)}) collective-permute-start(bf16[256,128]{1,0:T(8,128)(2,1)S(1)} %get-tuple-element.60.refs_0_), channel_id=1, source_target_pairs={{0,24},{4,28},{8,16},{12,20},{16,8},{20,12},{24,0},{28,4},{1,25},{... | collective-permute-start | bytes 196616 | tf_op jit(solution)/shard_map/ppermute | solution.py:470
  9.8 3.7 %collective-permute-start.3 = (s32[8,256]{1,0:T(8,128)S(1)}, s32[8,256]{1,0:T(8,128)S(1)}, u32[]{:S(2)}, u32[]{:S(2)}) collective-permute-start(s32[8,256]{1,0:T(8,128)S(1)} %get-tuple-element.59), channel_id=1, source_target_pairs={{0,4},{4,0},{8,12},{12,8},{16,20},{20,16},{24,28},{28,24},{1,5},{5... | collective-permute-start | bytes 24584 | tf_op jit(solution)/shard_map/ppermute | solution.py:470
  13.5 16.0 %collective-permute-start.11 = (bf16[1024,128]{1,0:T(8,128)(2,1)}, bf16[1024,128]{1,0:T(8,128)(2,1)S(1)}, u32[]{:S(2)}, u32[]{:S(2)}) collective-permute-start(bf16[1024,128]{1,0:T(8,128)(2,1)} %r_2_.2), channel_id=1, source_target_pairs={{0,1},{1,0},{2,3},{3,2},{4,5},{5,4},{6,7},{7,6},{8,9},{9,8},{10,11... | collective-permute-start | bytes 786440 | tf_op jit(solution)/shard_map/ppermute | solution.py:467
  13.5 16.0 %collective-permute-start.13 = (bf16[1024,128]{1,0:T(8,128)(2,1)S(1)}, bf16[1024,128]{1,0:T(8,128)(2,1)S(1)}, u32[]{:S(2)}, u32[]{:S(2)}) collective-permute-start(bf16[1024,128]{1,0:T(8,128)(2,1)S(1)} %collective-permute-done.12.r_2_), channel_id=1, source_target_pairs={{0,1},{1,0},{2,3},{3,2},{4,5},{5,4},{6,7},{7,6},{8,9},{9,8},{10,11... | collective-permute-start | bytes 786440 | tf_op jit(solution)/shard_map/ppermute | solution.py:467
  15.6 5.0 %collective-permute-start.7 = (bf16[256,128]{1,0:T(8,128)(2,1)S(1)}, bf16[256,128]{1,0:T(8,128)(2,1)S(1)}, u32[]{:S(2)}, u32[]{:S(2)}) collective-permute-start(bf16[256,128]{1,0:T(8,128)(2,1)S(1)} %get-tuple-element.62), channel_id=1, source_target_pairs={{0,4},{1,5},{2,6},{3,7},{4,0},{5,1},{6,2},{7,3},{8,12},{9,13},{10,... | collective-permute-start | bytes 196616 | tf_op jit(solution)/shard_map/ppermute | solution.py:474
  17.2 4.8 %collective-permute-start.8 = (bf16[256,128]{1,0:T(8,128)(2,1)S(1)}, bf16[256,128]{1,0:T(8,128)(2,1)S(1)}, u32[]{:S(2)}, u32[]{:S(2)}) collective-permute-start(bf16[256,128]{1,0:T(8,128)(2,1)S(1)} %get-tuple-element.61.mine_ref), channel_id=1, source_target_pairs={{0,2},{1,3},{2,0},{3,1},{4,6},{5,7},{6,4},{7,5},{8,10},{9,11},{10,... | collective-permute-start | bytes 196616 | tf_op jit(solution)/shard_map/ppermute | solution.py:474
  17.7 5.2 %collective-permute-start.9 = (bf16[256,128]{1,0:T(8,128)(2,1)S(1)}, bf16[256,128]{1,0:T(8,128)(2,1)S(1)}, u32[]{:S(2)}, u32[]{:S(2)}) collective-permute-start(bf16[256,128]{1,0:T(8,128)(2,1)S(1)} %get-tuple-element.62), channel_id=1, source_target_pairs={{0,6},{1,7},{2,4},{3,5},{4,2},{5,3},{6,0},{7,1},{8,14},{9,15},{10,... | collective-permute-start | bytes 196616 | tf_op jit(solution)/shard_map/ppermute | solution.py:474
  20.6 4.4 %collective-permute-start.1 = (bf16[304,128]{1,0:T(8,128)(2,1)S(1)}, bf16[304,128]{1,0:T(8,128)(2,1)S(1)}, u32[]{:S(2)}, u32[]{:S(2)}) collective-permute-start(bf16[304,128]{1,0:T(8,128)(2,1)S(1)} %shard_map.159.r_0_.r_4_), channel_id=1, source_target_pairs={{0,2},{1,3},{2,0},{3,1},{4,6},{5,7},{6,4},{7,5},{8,10},{9,11},{10,... | collective-permute-start | bytes 233480 | tf_op jit(solution)/shard_map/ppermute | solution.py:467
  23.0 7.4 %collective-permute-start.10 = (bf16[2,256,128]{2,1,0:T(8,128)(2,1)S(1)}, bf16[2,256,128]{2,1,0:T(8,128)(2,1)S(1)}, u32[]{:S(2)}, u32[]{:S(2)}) collective-permute-start(bf16[2,256,128]{2,1,0:T(8,128)(2,1)S(1)} %shard_map.164.r_2_), channel_id=1, source_target_pairs={{0,1},{1,0},{2,3},{3,2},{4,5},{5,4},{6,7},{7,6},{8,9},{9,8},{10,11... | collective-permute-start | bytes 393224 | tf_op jit(solution)/shard_map/ppermute | solution.py:467
  23.0 4.4 %collective-permute-start = (bf16[304,128]{1,0:T(8,128)(2,1)S(1)}, bf16[304,128]{1,0:T(8,128)(2,1)S(1)}, u32[]{:S(2)}, u32[]{:S(2)}) collective-permute-start(bf16[304,128]{1,0:T(8,128)(2,1)S(1)} %shard_map.159.r_0_.r_4_), channel_id=1, source_target_pairs={{0,1},{1,0},{2,3},{3,2},{4,5},{5,4},{6,7},{7,6},{8,9},{9,8},{10,11... | collective-permute-start | bytes 233480 | tf_op jit(solution)/shard_map/ppermute | solution.py:467
  25.0 3.4 %collective-permute-start.2 = (bf16[304,128]{1,0:T(8,128)(2,1)S(1)}, bf16[304,128]{1,0:T(8,128)(2,1)S(1)}, u32[]{:S(2)}, u32[]{:S(2)}) collective-permute-start(bf16[304,128]{1,0:T(8,128)(2,1)S(1)} %collective-permute-done.1.r_0_.r_6_), channel_id=1, source_target_pairs={{0,1},{1,0},{2,3},{3,2},{4,5},{5,4},{6,7},{7,6},{8,9},{9,8},{10,11... | collective-permute-start | bytes 233480 | tf_op jit(solution)/shard_map/ppermute | solution.py:467
  31.9 40.3 %copy-start = (f32[1024,128]{1,0:T(8,128)S(1)}, f32[1024,128]{1,0:T(8,128)}, u32[]{:S(2)}) copy-start(f32[1024,128]{1,0:T(8,128)} %table_ref.1) | copy-start | bytes 1572868
  31.9 40.3 %copy-start.1 = (f32[1024,128]{1,0:T(8,128)S(1)}, f32[1024,128]{1,0:T(8,128)}, u32[]{:S(2)}) copy-start(f32[1024,128]{1,0:T(8,128)} %accum_ref.1) | copy-start | bytes 1572868
  32.7 40.7 %copy-start.2 = (f32[256,128]{1,0:T(8,128)S(1)}, f32[256,128]{1,0:T(8,128)}, u32[]{:S(2)}) copy-start(f32[256,128]{1,0:T(8,128)} %r_1_.1) | copy-start | bytes 393220
  32.7 40.7 %copy-start.3 = (f32[256,128]{1,0:T(8,128)S(1)}, f32[256,128]{1,0:T(8,128)}, u32[]{:S(2)}) copy-start(f32[256,128]{1,0:T(8,128)} %r_2_.3) | copy-start | bytes 393220
  32.7 1.7 %collective-permute-start.25 = (f32[2,256,128]{2,1,0:T(8,128)S(1)}, f32[2,256,128]{2,1,0:T(8,128)S(1)}, u32[]{:S(2)}, u32[]{:S(2)}) collective-permute-start(f32[2,256,128]{2,1,0:T(8,128)S(1)} %get-tuple-element.83), channel_id=1, source_target_pairs={{0,1},{1,0},{2,3},{3,2},{4,5},{5,4},{6,7},{7,6},{8,9},{9,8},{10,11... | collective-permute-start | bytes 786440 | tf_op jit(solution)/shard_map/ppermute | solution.py:467
  33.3 12.2 %collective-permute-start.14 = (f32[512,128]{1,0:T(8,128)S(1)}, f32[512,128]{1,0:T(8,128)S(1)}, u32[]{:S(2)}, u32[]{:S(2)}) collective-permute-start(f32[512,128]{1,0:T(8,128)S(1)} %get-tuple-element.75), channel_id=1, source_target_pairs={{0,1},{1,0},{2,3},{3,2},{4,5},{5,4},{6,7},{7,6},{8,9},{9,8},{10,11... | collective-permute-start | bytes 786440 | tf_op jit(solution)/shard_map/ppermute | solution.py:467
  34.5 5.8 %collective-permute-start.26 = (f32[256,128]{1,0:T(8,128)S(1)}, f32[256,128]{1,0:T(8,128)S(1)}, u32[]{:S(2)}, u32[]{:S(2)}) collective-permute-start(f32[256,128]{1,0:T(8,128)S(1)} %get-tuple-element.85), channel_id=1, source_target_pairs={{0,2},{1,3},{2,0},{3,1},{4,6},{5,7},{6,4},{7,5},{8,10},{9,11},{10,... | collective-permute-start | bytes 393224 | tf_op jit(solution)/shard_map/ppermute | solution.py:467
  41.3 32.1 %all-to-all-start = ((f32[8,72,128]{2,1,0:T(8,128)}), f32[8,72,128]{2,1,0:T(8,128)S(1)}, u32[]{:S(2)}, u32[]{:S(2)}) async-start(f32[8,72,128]{2,1,0:T(8,128)} %shard_map.175), calls=%async_computation | async-start | bytes 589824 | tf_op jit(solution)/shard_map/all_to_all | solution.py:652
  45.5 4.8 %collective-permute-start.15 = (f32[4,32,128]{2,1,0:T(8,128)S(1)}, f32[4,32,128]{2,1,0:T(8,128)S(1)}, u32[]{:S(2)}, u32[]{:S(2)}) collective-permute-start(f32[4,32,128]{2,1,0:T(8,128)S(1)} %get-tuple-element.77), channel_id=1, source_target_pairs={{0,2},{1,3},{2,0},{3,1},{4,6},{5,7},{6,4},{7,5},{8,10},{9,11},{10,... | collective-permute-start | bytes 196616 | tf_op jit(solution)/shard_map/ppermute | solution.py:474
  46.1 6.2 %collective-permute-start.16 = (f32[4,32,128]{2,1,0:T(8,128)S(1)}, f32[4,32,128]{2,1,0:T(8,128)S(1)}, u32[]{:S(2)}, u32[]{:S(2)}) collective-permute-start(f32[4,32,128]{2,1,0:T(8,128)S(1)} %get-tuple-element.78), channel_id=1, source_target_pairs={{0,4},{1,5},{2,6},{3,7},{4,0},{5,1},{6,2},{7,3},{8,12},{9,13},{10,... | collective-permute-start | bytes 196616 | tf_op jit(solution)/shard_map/ppermute | solution.py:474
  48.1 5.4 %collective-permute-start.17 = (f32[4,32,128]{2,1,0:T(8,128)S(1)}, f32[4,32,128]{2,1,0:T(8,128)S(1)}, u32[]{:S(2)}, u32[]{:S(2)}) collective-permute-start(f32[4,32,128]{2,1,0:T(8,128)S(1)} %get-tuple-element.79), channel_id=1, source_target_pairs={{0,6},{1,7},{2,4},{3,5},{4,2},{5,3},{6,0},{7,1},{8,14},{9,15},{10,... | collective-permute-start | bytes 196616 | tf_op jit(solution)/shard_map/ppermute | solution.py:474
  53.5 4.5 %collective-permute-start.18 = (f32[4,32,128]{2,1,0:T(8,128)S(1)}, f32[4,32,128]{2,1,0:T(8,128)S(1)}, u32[]{:S(2)}, u32[]{:S(2)}) collective-permute-start(f32[4,32,128]{2,1,0:T(8,128)S(1)} %shard_map.169.a_ref), channel_id=1, source_target_pairs={{0,8},{4,12},{8,0},{12,4},{16,24},{20,28},{24,16},{28,20},{1,9},{5... | collective-permute-start | bytes 196616 | tf_op jit(solution)/shard_map/ppermute | solution.py:470
  55.2 6.6 %collective-permute-start.19 = (f32[4,32,128]{2,1,0:T(8,128)S(1)}, f32[4,32,128]{2,1,0:T(8,128)S(1)}, u32[]{:S(2)}, u32[]{:S(2)}) collective-permute-start(f32[4,32,128]{2,1,0:T(8,128)S(1)} %shard_map.169.a_ref), channel_id=1, source_target_pairs={{0,16},{4,20},{8,24},{12,28},{16,0},{20,4},{24,8},{28,12},{1,17},{... | collective-permute-start | bytes 196616 | tf_op jit(solution)/shard_map/ppermute | solution.py:470
  57.4 6.1 %collective-permute-start.20 = (f32[4,32,128]{2,1,0:T(8,128)S(1)}, f32[4,32,128]{2,1,0:T(8,128)S(1)}, u32[]{:S(2)}, u32[]{:S(2)}) collective-permute-start(f32[4,32,128]{2,1,0:T(8,128)S(1)} %shard_map.169.a_ref), channel_id=1, source_target_pairs={{0,24},{4,28},{8,16},{12,20},{16,8},{20,12},{24,0},{28,4},{1,25},{... | collective-permute-start | bytes 196616 | tf_op jit(solution)/shard_map/ppermute | solution.py:470
  63.4 4.3 %collective-permute-start.21 = (f32[4,32,128]{2,1,0:T(8,128)S(1)}, f32[4,32,128]{2,1,0:T(8,128)S(1)}, u32[]{:S(2)}, u32[]{:S(2)}) collective-permute-start(f32[4,32,128]{2,1,0:T(8,128)S(1)} %shard_map.170.refs_0_), channel_id=1, source_target_pairs={{0,2},{1,3},{2,0},{3,1},{4,6},{5,7},{6,4},{7,5},{8,10},{9,11},{10,... | collective-permute-start | bytes 196616 | tf_op jit(solution)/shard_map/ppermute | solution.py:474
  64.8 4.3 %collective-permute-start.22 = (f32[4,32,128]{2,1,0:T(8,128)S(1)}, f32[4,32,128]{2,1,0:T(8,128)S(1)}, u32[]{:S(2)}, u32[]{:S(2)}) collective-permute-start(f32[4,32,128]{2,1,0:T(8,128)S(1)} %shard_map.170.refs_0_), channel_id=1, source_target_pairs={{0,4},{1,5},{2,6},{3,7},{4,0},{5,1},{6,2},{7,3},{8,12},{9,13},{10,... | collective-permute-start | bytes 196616 | tf_op jit(solution)/shard_map/ppermute | solution.py:474
  65.4 5.2 %collective-permute-start.23 = (f32[4,32,128]{2,1,0:T(8,128)S(1)}, f32[4,32,128]{2,1,0:T(8,128)S(1)}, u32[]{:S(2)}, u32[]{:S(2)}) collective-permute-start(f32[4,32,128]{2,1,0:T(8,128)S(1)} %shard_map.170.refs_0_), channel_id=1, source_target_pairs={{0,6},{1,7},{2,4},{3,5},{4,2},{5,3},{6,0},{7,1},{8,14},{9,15},{10,... | collective-permute-start | bytes 196616 | tf_op jit(solution)/shard_map/ppermute | solution.py:474
  70.6 1.6 %collective-permute-start.24 = (f32[512,128]{1,0:T(8,128)S(1)}, f32[512,128]{1,0:T(8,128)S(1)}, u32[]{:S(2)}, u32[]{:S(2)}) collective-permute-start(f32[512,128]{1,0:T(8,128)S(1)} %bitcast.9), channel_id=1, source_target_pairs={{0,1},{1,0},{2,3},{3,2},{4,5},{5,4},{6,7},{7,6},{8,9},{9,8},{10,11... | collective-permute-start | bytes 786440 | tf_op jit(solution)/shard_map/ppermute | solution.py:467

commit v6 on v5

--- a/solution.py
+++ b/solution.py
@@ -52,7 +52,7 @@
 ANY = pl.BlockSpec(memory_space=pl.ANY)
 
 
-def call(body, outs, ins, scratch=(), late=(), raw=()):
+def call(body, outs, ins, scratch=(), late=(), raw=(), sent=False):
     avals = [
         pltpu.VMEM(shape, dtype) if stay else jax.ShapeDtypeStruct(shape, dtype)
         for shape, dtype, stay in outs
@@ -61,7 +61,7 @@
         body,
         out_shape=avals,
         in_specs=[ANY if i in raw else VM for i in range(len(ins))],
-        out_specs=[VM] * len(outs),
+        out_specs=[ANY if sent else VM] * len(outs),
         scratch_shapes=scratch,
         compiler_params=pltpu.CompilerParams(vmem_limit_bytes=16 * 1024 * 1024),
     )(
@@ -425,12 +425,25 @@
     new_ref[...], acc_ref[...] = adagrad(table_ref[...], accum_ref[...], grad)
 
 
-def final_kernel(mine_ref, theirs_ref, table_ref, accum_ref, new_ref, acc_ref):
+def final_kernel(mine_ref, theirs_ref, table_ref, accum_ref, new_hbm, acc_hbm, new_ref, acc_ref, sems):
     half = mine_ref.shape[0]
+    parts = sems.shape[1] // 2
+    rows = half // parts
     core = lax.axis_index("mp") % 2
-    for ref, c in ((mine_ref, core), (theirs_ref, 1 - core)):
-        at = pl.ds(pl.multiple_of(c * half, half), half)
-        new_ref[at, :], acc_ref[at, :] = adagrad(table_ref[at, :], accum_ref[at, :], ref[...])
+    copies = []
+    for i, (ref, c) in enumerate(((mine_ref, core), (theirs_ref, 1 - core))):
+        for j in range(parts):
+            at = pl.ds(pl.multiple_of(c * half + j * rows, rows), rows)
+            new_ref[at, :], acc_ref[at, :] = adagrad(
+                table_ref[at, :], accum_ref[at, :], ref[j * rows : (j + 1) * rows, :]
+            )
+            k = i * parts + j
+            copies.append(pltpu.make_async_copy(new_ref.at[at, :], new_hbm.at[at, :], sems.at[0, k]))
+            copies.append(pltpu.make_async_copy(acc_ref.at[at, :], acc_hbm.at[at, :], sems.at[1, k]))
+            copies[-2].start()
+            copies[-1].start()
+    for copy in copies:
+        copy.wait()
 
 
 def per_device(
@@ -633,7 +646,15 @@
         half = exchange(shard).reshape(half_rows, emb)
     other = swap(half, 1)
     hot_updated, hot_accum_new = call(
-        final_kernel, [(hot_table.shape, F32, False)] * 2, [half, other, hot_table, hot_accum]
+        final_kernel,
+        [(hot_table.shape, F32, False)] * 2,
+        [half, other, hot_table, hot_accum],
+        scratch=[
+            pltpu.VMEM(hot_table.shape, F32),
+            pltpu.VMEM(hot_table.shape, F32),
+            pltpu.SemaphoreType.DMA((2, 4)),
+        ],
+        sent=True,
     )
 
     q_mat, slot_rows = call(

time: 74.8 us -> 74.7 us (level)
  no operation moved by 1% of the time
where the time goes in v6:
time: 74.7 us; the launch traced here: 74.4 us
  starting transfers between devices  30.2 us (40%)
  waiting for transfers between devices  29.6 us (40%)
  Pallas kernels  13.7 us (18%)
  between operations  0.88 us (1%)
    pallas_call x21, Pallas kernels, call(): pl.pallas_call(body, out_shape=avals, in_specs=[ANY if i in raw else VM f...  13.7 us
    ppermute x9, waiting for transfers between devices, near_swap(): lax.ppermute(x, both, [(i, i ^ mask) for i in range(dp_count * mp_count)])  11.7 us
    ppermute x9, starting transfers between devices, near_swap(): lax.ppermute(x, both, [(i, i ^ mask) for i in range(dp_count * mp_count)])  10.7 us
    ppermute x7, starting transfers between devices, far_swap(): return lax.ppermute(x, 'dp', [(i, i ^ mask) for i in range(dp_count)])  10.5 us
    ppermute x11, waiting for transfers between devices, swap(): return lax.ppermute(x, 'mp', [(i, i ^ mask) for i in range(mp_count)])  9.32 us
    ppermute x7, waiting for transfers between devices, far_swap(): return lax.ppermute(x, 'dp', [(i, i ^ mask) for i in range(dp_count)])  8.57 us
    ppermute x11, starting transfers between devices, swap(): return lax.ppermute(x, 'mp', [(i, i ^ mask) for i in range(mp_count)])  4.91 us
    all_to_all x1, starting transfers between devices, per_device(): lax.all_to_all(outgoing, 'dp', split_axis=0, concat_axis=0, tiled=True)  4.16 us
  transfers between devices with their start and end apart: 28, of which 17 were waited for; matrix products, arithmetic and copies ran while one was open for 0% of the time, Pallas kernels for 14%

profile of v6, /device:TPU:0, one launch (start us, length us, event | category | flops | bytes accessed | tf_op | source)
XLA Modules:
  0.0 74.4 jit_solution(11017836545623531725)
XLA Ops:
  0.6 3.0 %collective-permute-start.12 = (bf16[1024,128]{1,0:T(8,128)(2,1)}, bf16[1024,128]{1,0:T(8,128)(2,1)S(1)}, u32[]{:S(2)}, u32[]{:S(2)}) collective-permute-start(bf16[1024,128]{1,0:T(8,128)(2,1)} %r_2_.2), channel_id=1, source_target_pairs={{0,2},{1,3},{2,0},{3,1},{4,6},{5,7},{6,4},{7,5},{8,10},{9,11},{10,... | collective-permute-start | bytes 786440 | tf_op jit(solution)/shard_map/ppermute | solution.py:480
  3.7 1.0 %shard_map.158 = (bf16[256,128]{1,0:T(8,128)(2,1)S(1)}, s32[64,128]{1,0:T(8,128)S(1)}, s32[1,256]{1,0:T(1,128)S(1)}, bf16[128,256]{1,0:T(8,128)(2,1)S(1)}, s32[1...) custom-call(f32[256,128]{1,0:T(8,128)} %r_1_.1, s32[64,128]{1,0:T(8,128)} %bitcast.13, ...), custom_call_target="tpu_custom_call" | custom-call | tf_op jit(solution)/shard_map/pallas_call | solution.py:60
  4.7 1.6 %collective-permute-start.4 = (bf16[256,128]{1,0:T(8,128)(2,1)S(1)}, bf16[256,128]{1,0:T(8,128)(2,1)S(1)}, u32[]{:S(2)}, u32[]{:S(2)}) collective-permute-start(bf16[256,128]{1,0:T(8,128)(2,1)S(1)} %get-tuple-element.60.refs_0_), channel_id=1, source_target_pairs={{0,8},{4,12},{8,0},{12,4},{16,24},{20,28},{24,16},{28,20},{1,9},{5... | collective-permute-start | bytes 196616 | tf_op jit(solution)/shard_map/ppermute | solution.py:483
  6.3 2.6 %collective-permute-start.5 = (bf16[256,128]{1,0:T(8,128)(2,1)S(1)}, bf16[256,128]{1,0:T(8,128)(2,1)S(1)}, u32[]{:S(2)}, u32[]{:S(2)}) collective-permute-start(bf16[256,128]{1,0:T(8,128)(2,1)S(1)} %get-tuple-element.60.refs_0_), channel_id=1, source_target_pairs={{0,16},{4,20},{8,24},{12,28},{16,0},{20,4},{24,8},{28,12},{1,17},{... | collective-permute-start | bytes 196616 | tf_op jit(solution)/shard_map/ppermute | solution.py:483
  9.1 0.7 shard_map.162
  9.8 1.6 %collective-permute-start.3 = (s32[8,256]{1,0:T(8,128)S(1)}, s32[8,256]{1,0:T(8,128)S(1)}, u32[]{:S(2)}, u32[]{:S(2)}) collective-permute-start(s32[8,256]{1,0:T(8,128)S(1)} %get-tuple-element.59), channel_id=1, source_target_pairs={{0,4},{4,0},{8,12},{12,8},{16,20},{20,16},{24,28},{28,24},{1,5},{5... | collective-permute-start | bytes 24584 | tf_op jit(solution)/shard_map/ppermute | solution.py:483
  11.4 2.1 %collective-permute-done.3.row_ref = s32[8,256]{1,0:T(8,128)S(1)} collective-permute-done((s32[8,256]{1,0:T(8,128)S(1)}, s32[8,256]{1,0:T(8,128)S(1)}, u32[]{:S(2)}, u32[]{:S(2)}) %collective-permute-start.3) | collective-permute-done | bytes 8224 | tf_op jit(solution)/shard_map/ppermute | solution.py:483
  14.0 1.0 %collective-permute-done.6.refs_3_ = bf16[256,128]{1,0:T(8,128)(2,1)S(1)} collective-permute-done((bf16[256,128]{1,0:T(8,128)(2,1)S(1)}, bf16[256,128]{1,0:T(8,128)(2,1)S(1)}, u32[]{:S(2)}, u32[]{:S(2)}) %collective-permute-start.6) | collective-permute-done | bytes 65568 | tf_op jit(solution)/shard_map/ppermute | solution.py:483
  15.0 0.6 shard_map.163
  15.6 1.6 %collective-permute-start.7 = (bf16[256,128]{1,0:T(8,128)(2,1)S(1)}, bf16[256,128]{1,0:T(8,128)(2,1)S(1)}, u32[]{:S(2)}, u32[]{:S(2)}) collective-permute-start(bf16[256,128]{1,0:T(8,128)(2,1)S(1)} %get-tuple-element.62), channel_id=1, source_target_pairs={{0,4},{1,5},{2,6},{3,7},{4,0},{5,1},{6,2},{7,3},{8,12},{9,13},{10,... | collective-permute-start | bytes 196616 | tf_op jit(solution)/shard_map/ppermute | solution.py:487
  17.7 1.4 %collective-permute-start.9 = (bf16[256,128]{1,0:T(8,128)(2,1)S(1)}, bf16[256,128]{1,0:T(8,128)(2,1)S(1)}, u32[]{:S(2)}, u32[]{:S(2)}) collective-permute-start(bf16[256,128]{1,0:T(8,128)(2,1)S(1)} %get-tuple-element.62), channel_id=1, source_target_pairs={{0,6},{1,7},{2,4},{3,5},{4,2},{5,3},{6,0},{7,1},{8,14},{9,15},{10,... | collective-permute-start | bytes 196616 | tf_op jit(solution)/shard_map/ppermute | solution.py:487
  19.2 1.5 %collective-permute-done.7.near_ref = bf16[256,128]{1,0:T(8,128)(2,1)S(1)} collective-permute-done((bf16[256,128]{1,0:T(8,128)(2,1)S(1)}, bf16[256,128]{1,0:T(8,128)(2,1)S(1)}, u32[]{:S(2)}, u32[]{:S(2)}) %collective-permute-start.7) | collective-permute-done | bytes 65568 | tf_op jit(solution)/shard_map/ppermute | solution.py:487
  20.6 1.3 %collective-permute-done.8.far_ref = bf16[256,128]{1,0:T(8,128)(2,1)S(1)} collective-permute-done((bf16[256,128]{1,0:T(8,128)(2,1)S(1)}, bf16[256,128]{1,0:T(8,128)(2,1)S(1)}, u32[]{:S(2)}, u32[]{:S(2)}) %collective-permute-start.8) | collective-permute-done | bytes 65568 | tf_op jit(solution)/shard_map/ppermute | solution.py:487
  22.0 1.0 %collective-permute-done.9.cross_ref = bf16[256,128]{1,0:T(8,128)(2,1)S(1)} collective-permute-done((bf16[256,128]{1,0:T(8,128)(2,1)S(1)}, bf16[256,128]{1,0:T(8,128)(2,1)S(1)}, u32[]{:S(2)}, u32[]{:S(2)}) %collective-permute-start.9) | collective-permute-done | bytes 65568 | tf_op jit(solution)/shard_map/ppermute | solution.py:487
  23.5 1.5 %collective-permute-done.1.r_0_.r_6_ = bf16[304,128]{1,0:T(8,128)(2,1)S(1)} collective-permute-done((bf16[304,128]{1,0:T(8,128)(2,1)S(1)}, bf16[304,128]{1,0:T(8,128)(2,1)S(1)}, u32[]{:S(2)}, u32[]{:S(2)}) %collective-permute-start.1) | collective-permute-done | bytes 77856 | tf_op jit(solution)/shard_map/ppermute | solution.py:480
  25.0 1.2 %shard_map.156 = (f32[1024,128]{1,0:T(8,128)S(1)}, s32[7,1024]{1,0:T(8,128)S(1)}, bf16[1024,128]{1,0:T(8,128)(2,1)S(1)}, bf16[256,256]{1,0:T(8,128)(2,1)S(1)}) custom-call(f32[1024,128]{1,0:T(8,128)} %table_ref.1, s32[7,1024]{1,0:T(8,128)} %bitcast.14, bf16[1024,128]{1,0:T(8,128)(2,1)} %r_2_.2, bf16[1024,256]{1,0:T(8,128)(2,1)} %r_3_.2), custom_call_target="tpu_custom_call" | custom-call | tf_op jit(solution)/shard_map/pallas_call | solution.py:60
  26.2 1.2 %shard_map.157 = (bf16[1024,1792]{1,0:T(8,128)(2,1)S(1)}, bf16[896,256]{1,0:T(8,128)(2,1)S(1)}) custom-call(s32[7,1024]{1,0:T(8,128)S(1)} %get-tuple-element.47.r_0_, f32[1024,128]{1,0:T(8,128)S(1)} %get-tuple-element.48.r_1_), custom_call_target="tpu_custom_call" | custom-call | tf_op jit(solution)/shard_map/pallas_call | solution.py:60
  27.4 1.0 %shard_map.160 = (bf16[256,512]{1,0:T(8,128)(2,1)S(1)}, bf16[512,256]{1,0:T(8,128)(2,1)S(1)}) custom-call(bf16[304,128]{1,0:T(8,128)(2,1)S(1)} %shard_map.159.r_0_.r_4_, bf16[304,128]{1,0:T(8,128)(2,1)S(1)} %collective-permute-done.r_1_.r_5_), custom_call_target="tpu_custom_call" | custom-call | tf_op jit(solution)/shard_map/pallas_call | solution.py:60
  28.5 1.0 %shard_map.161 = (bf16[256,512]{1,0:T(8,128)(2,1)S(1)}, bf16[512,256]{1,0:T(8,128)(2,1)S(1)}) custom-call(bf16[304,128]{1,0:T(8,128)(2,1)S(1)} %collective-permute-done.1.r_0_.r_6_, bf16[304,128]{1,0:T(8,128)(2,1)S(1)} %collective-permute-done.2.r_1_.r_7_), custom_call_target="tpu_custom_call" | custom-call | tf_op jit(solution)/shard_map/pallas_call | solution.py:60
  29.5 0.8 %shard_map.165 = (bf16[512,1024]{1,0:T(8,128)(2,1)S(1)}, bf16[128,512]{1,0:T(8,128)(2,1)S(1)}, f32[256,512]{1,0:T(8,128)S(1)}, f32[256,512]{1,0:T(8,128)S(1)}) custom-call(bf16[1024,128]{1,0:T(8,128)(2,1)S(1)} %get-tuple-element.63.r_0_, bf16[1024,128]{1,0:T(8,128)(2,1)S(1)} %collective-permute-done.11.r_1_, ...), custom_call_target="tpu_custom_call" | custom-call | tf_op jit(solution)/shard_map/pallas_call | solution.py:60
  30.4 1.5 %shard_map.166 = (bf16[1792,256]{1,0:T(8,128)(2,1)S(1)}, bf16[256,256]{1,0:T(8,128)(2,1)S(1)}, f32[512,128]{1,0:T(8,128)S(1)}) custom-call(bf16[256,512]{1,0:T(8,128)(2,1)S(1)} %get-tuple-element.54.r_0_, bf16[256,512]{1,0:T(8,128)(2,1)S(1)} %get-tuple-element.55.r_1_, bf16[2,256,128]{2,1,0:T(8,128)(2,1)S(1)} %shard_map.164.r_2_, ...), custom_call_target="tpu_custom_call" | custom-call | tf_op jit(solution)/shard_map/pallas_call | solution.py:60
  31.9 0.8 %shard_map.167 = (f32[512,128]{1,0:T(8,128)S(1)}, f32[2,256,128]{2,1,0:T(8,128)S(1)}, f32[2,256,128]{2,1,0:T(8,128)S(1)}) custom-call(bf16[1024,1792]{1,0:T(8,128)(2,1)S(1)} %get-tuple-element.49.r_8_.oht_ref, bf16[1792,256]{1,0:T(8,128)(2,1)S(1)} %get-tuple-element.70.ig_ref, bf16[256,256]{1,0:T(8,128)(2,1)S(1)} %get-tuple-element.71.bag_ref, ...), custom_call_target="tpu_custom_call" | custom-call | tf_op jit(solution)/shard_map/pallas_call | solution.py:60
  32.7 0.6 collective-permute-start.25
  33.4 1.1 %collective-permute-done.25.got_ref = f32[2,256,128]{2,1,0:T(8,128)S(1)} collective-permute-done((f32[2,256,128]{2,1,0:T(8,128)S(1)}, f32[2,256,128]{2,1,0:T(8,128)S(1)}, u32[]{:S(2)}, u32[]{:S(2)}) %collective-permute-start.25) | collective-permute-done | bytes 262176 | tf_op jit(solution)/shard_map/ppermute | solution.py:480
  34.6 0.5 shard_map.174
  35.1 5.2 %collective-permute-done.26.r_1_ = f32[256,128]{1,0:T(8,128)S(1)} collective-permute-done((f32[256,128]{1,0:T(8,128)S(1)}, f32[256,128]{1,0:T(8,128)S(1)}, u32[]{:S(2)}, u32[]{:S(2)}) %collective-permute-start.26) | collective-permute-done | bytes 131104 | tf_op jit(solution)/shard_map/ppermute | solution.py:480
  40.3 1.0 %shard_map.175 = f32[8,72,128]{2,1,0:T(8,128)} custom-call(f32[256,128]{1,0:T(8,128)S(1)} %get-tuple-element.84.r_0_, f32[256,128]{1,0:T(8,128)S(1)} %collective-permute-done.26.r_1_, bf16[512,256]{1,0:T(8,128)(2,1)S(1)} %get-tuple-element.86.r_2_, f32[64,128]{1,0:T(8,128)S(1)} %get-tuple-element.87.r_3_), custom_call_target="tpu_custom_call" | custom-call | tf_op jit(solution)/shard_map/pallas_call | solution.py:60
  41.3 4.2 %all-to-all-start = ((f32[8,72,128]{2,1,0:T(8,128)}), f32[8,72,128]{2,1,0:T(8,128)S(1)}, u32[]{:S(2)}, u32[]{:S(2)}) async-start(f32[8,72,128]{2,1,0:T(8,128)} %shard_map.175), calls=%async_computation | async-start | bytes 589824 | tf_op jit(solution)/shard_map/all_to_all | solution.py:673
  45.5 0.6 collective-permute-start.15
  46.1 2.0 %collective-permute-start.16 = (f32[4,32,128]{2,1,0:T(8,128)S(1)}, f32[4,32,128]{2,1,0:T(8,128)S(1)}, u32[]{:S(2)}, u32[]{:S(2)}) collective-permute-start(f32[4,32,128]{2,1,0:T(8,128)S(1)} %get-tuple-element.78), channel_id=1, source_target_pairs={{0,4},{1,5},{2,6},{3,7},{4,0},{5,1},{6,2},{7,3},{8,12},{9,13},{10,... | collective-permute-start | bytes 196616 | tf_op jit(solution)/shard_map/ppermute | solution.py:487
  48.1 0.9 %collective-permute-start.17 = (f32[4,32,128]{2,1,0:T(8,128)S(1)}, f32[4,32,128]{2,1,0:T(8,128)S(1)}, u32[]{:S(2)}, u32[]{:S(2)}) collective-permute-start(f32[4,32,128]{2,1,0:T(8,128)S(1)} %get-tuple-element.79), channel_id=1, source_target_pairs={{0,6},{1,7},{2,4},{3,5},{4,2},{5,3},{6,0},{7,1},{8,14},{9,15},{10,... | collective-permute-start | bytes 196616 | tf_op jit(solution)/shard_map/ppermute | solution.py:487
  49.0 1.2 %collective-permute-done.15.b_ref = f32[4,32,128]{2,1,0:T(8,128)S(1)} collective-permute-done((f32[4,32,128]{2,1,0:T(8,128)S(1)}, f32[4,32,128]{2,1,0:T(8,128)S(1)}, u32[]{:S(2)}, u32[]{:S(2)}) %collective-permute-start.15) | collective-permute-done | bytes 65568 | tf_op jit(solution)/shard_map/ppermute | solution.py:487
  50.3 2.1 %collective-permute-done.16.c_ref = f32[4,32,128]{2,1,0:T(8,128)S(1)} collective-permute-done((f32[4,32,128]{2,1,0:T(8,128)S(1)}, f32[4,32,128]{2,1,0:T(8,128)S(1)}, u32[]{:S(2)}, u32[]{:S(2)}) %collective-permute-start.16) | collective-permute-done | bytes 65568 | tf_op jit(solution)/shard_map/ppermute | solution.py:487
  52.4 1.1 %collective-permute-done.17.d_ref = f32[4,32,128]{2,1,0:T(8,128)S(1)} collective-permute-done((f32[4,32,128]{2,1,0:T(8,128)S(1)}, f32[4,32,128]{2,1,0:T(8,128)S(1)}, u32[]{:S(2)}, u32[]{:S(2)}) %collective-permute-start.17) | collective-permute-done | bytes 65568 | tf_op jit(solution)/shard_map/ppermute | solution.py:487
  53.5 1.7 %collective-permute-start.18 = (f32[4,32,128]{2,1,0:T(8,128)S(1)}, f32[4,32,128]{2,1,0:T(8,128)S(1)}, u32[]{:S(2)}, u32[]{:S(2)}) collective-permute-start(f32[4,32,128]{2,1,0:T(8,128)S(1)} %shard_map.169.a_ref), channel_id=1, source_target_pairs={{0,8},{4,12},{8,0},{12,4},{16,24},{20,28},{24,16},{28,20},{1,9},{5... | collective-permute-start | bytes 196616 | tf_op jit(solution)/shard_map/ppermute | solution.py:483
  55.2 2.2 %collective-permute-start.19 = (f32[4,32,128]{2,1,0:T(8,128)S(1)}, f32[4,32,128]{2,1,0:T(8,128)S(1)}, u32[]{:S(2)}, u32[]{:S(2)}) collective-permute-start(f32[4,32,128]{2,1,0:T(8,128)S(1)} %shard_map.169.a_ref), channel_id=1, source_target_pairs={{0,16},{4,20},{8,24},{12,28},{16,0},{20,4},{24,8},{28,12},{1,17},{... | collective-permute-start | bytes 196616 | tf_op jit(solution)/shard_map/ppermute | solution.py:483
  57.4 0.6 collective-permute-start.20
  58.0 3.8 %collective-permute-done.19.c_ref = f32[4,32,128]{2,1,0:T(8,128)S(1)} collective-permute-done((f32[4,32,128]{2,1,0:T(8,128)S(1)}, f32[4,32,128]{2,1,0:T(8,128)S(1)}, u32[]{:S(2)}, u32[]{:S(2)}) %collective-permute-start.19) | collective-permute-done | bytes 65568 | tf_op jit(solution)/shard_map/ppermute | solution.py:483
  61.8 1.7 %collective-permute-done.20.d_ref = f32[4,32,128]{2,1,0:T(8,128)S(1)} collective-permute-done((f32[4,32,128]{2,1,0:T(8,128)S(1)}, f32[4,32,128]{2,1,0:T(8,128)S(1)}, u32[]{:S(2)}, u32[]{:S(2)}) %collective-permute-start.20) | collective-permute-done | bytes 65568 | tf_op jit(solution)/shard_map/ppermute | solution.py:483
  63.4 1.4 %collective-permute-start.21 = (f32[4,32,128]{2,1,0:T(8,128)S(1)}, f32[4,32,128]{2,1,0:T(8,128)S(1)}, u32[]{:S(2)}, u32[]{:S(2)}) collective-permute-start(f32[4,32,128]{2,1,0:T(8,128)S(1)} %shard_map.170.refs_0_), channel_id=1, source_target_pairs={{0,2},{1,3},{2,0},{3,1},{4,6},{5,7},{6,4},{7,5},{8,10},{9,11},{10,... | collective-permute-start | bytes 196616 | tf_op jit(solution)/shard_map/ppermute | solution.py:487
  64.8 0.6 collective-permute-start.22
  65.4 1.6 %collective-permute-start.23 = (f32[4,32,128]{2,1,0:T(8,128)S(1)}, f32[4,32,128]{2,1,0:T(8,128)S(1)}, u32[]{:S(2)}, u32[]{:S(2)}) collective-permute-start(f32[4,32,128]{2,1,0:T(8,128)S(1)} %shard_map.170.refs_0_), channel_id=1, source_target_pairs={{0,6},{1,7},{2,4},{3,5},{4,2},{5,3},{6,0},{7,1},{8,14},{9,15},{10,... | collective-permute-start | bytes 196616 | tf_op jit(solution)/shard_map/ppermute | solution.py:487
  67.0 0.8 %collective-permute-done.21.refs_1_ = f32[4,32,128]{2,1,0:T(8,128)S(1)} collective-permute-done((f32[4,32,128]{2,1,0:T(8,128)S(1)}, f32[4,32,128]{2,1,0:T(8,128)S(1)}, u32[]{:S(2)}, u32[]{:S(2)}) %collective-permute-start.21) | collective-permute-done | bytes 65568 | tf_op jit(solution)/shard_map/ppermute | solution.py:487
  67.8 1.3 %collective-permute-done.22.refs_2_ = f32[4,32,128]{2,1,0:T(8,128)S(1)} collective-permute-done((f32[4,32,128]{2,1,0:T(8,128)S(1)}, f32[4,32,128]{2,1,0:T(8,128)S(1)}, u32[]{:S(2)}, u32[]{:S(2)}) %collective-permute-start.22) | collective-permute-done | bytes 65568 | tf_op jit(solution)/shard_map/ppermute | solution.py:487
  69.1 1.5 %collective-permute-done.23.refs_3_ = f32[4,32,128]{2,1,0:T(8,128)S(1)} collective-permute-done((f32[4,32,128]{2,1,0:T(8,128)S(1)}, f32[4,32,128]{2,1,0:T(8,128)S(1)}, u32[]{:S(2)}, u32[]{:S(2)}) %collective-permute-start.23) | collective-permute-done | bytes 65568 | tf_op jit(solution)/shard_map/ppermute | solution.py:487
  70.7 1.5 %collective-permute-done.24.theirs_ref = f32[512,128]{1,0:T(8,128)S(1)} collective-permute-done((f32[512,128]{1,0:T(8,128)S(1)}, f32[512,128]{1,0:T(8,128)S(1)}, u32[]{:S(2)}, u32[]{:S(2)}) %collective-permute-start.24) | collective-permute-done | bytes 262176 | tf_op jit(solution)/shard_map/ppermute | solution.py:480
  72.2 1.1 %shard_map.172 = (f32[1024,128]{1,0:T(8,128)}, f32[1024,128]{1,0:T(8,128)}) custom-call(f32[512,128]{1,0:T(8,128)S(1)} %bitcast.10, f32[512,128]{1,0:T(8,128)S(1)} %collective-permute-done.24.theirs_ref, f32[1024,128]{1,0:T(8,128)S(1)} %copy-done, f32[1024,128]{1,0:T(8,128)S(1)} %copy-done.1), custom_call_target="tpu_custom_call" | custom-call | tf_op jit(solution)/shard_map/pallas_call | solution.py:60
  73.3 1.1 %shard_map.176 = (f32[256,128]{1,0:T(8,128)}, f32[256,128]{1,0:T(8,128)}) custom-call(f32[8,72,128]{2,1,0:T(8,128)S(1)} %all-to-all-done.r_0_, f32[256,128]{1,0:T(8,128)S(1)} %copy-done.2, f32[256,128]{1,0:T(8,128)S(1)} %copy-done.3), custom_call_target="tpu_custom_call" | custom-call | tf_op jit(solution)/shard_map/pallas_call | solution.py:60
  (37 shorter events, 2.3 us)
Async XLA Ops:
  0.6 12.9 %collective-permute-start.12 = (bf16[1024,128]{1,0:T(8,128)(2,1)}, bf16[1024,128]{1,0:T(8,128)(2,1)S(1)}, u32[]{:S(2)}, u32[]{:S(2)}) collective-permute-start(bf16[1024,128]{1,0:T(8,128)(2,1)} %r_2_.2), channel_id=1, source_target_pairs={{0,2},{1,3},{2,0},{3,1},{4,6},{5,7},{6,4},{7,5},{8,10},{9,11},{10,... | collective-permute-start | bytes 786440 | tf_op jit(solution)/shard_map/ppermute | solution.py:480
  4.7 9.3 %collective-permute-start.4 = (bf16[256,128]{1,0:T(8,128)(2,1)S(1)}, bf16[256,128]{1,0:T(8,128)(2,1)S(1)}, u32[]{:S(2)}, u32[]{:S(2)}) collective-permute-start(bf16[256,128]{1,0:T(8,128)(2,1)S(1)} %get-tuple-element.60.refs_0_), channel_id=1, source_target_pairs={{0,8},{4,12},{8,0},{12,4},{16,24},{20,28},{24,16},{28,20},{1,9},{5... | collective-permute-start | bytes 196616 | tf_op jit(solution)/shard_map/ppermute | solution.py:483
  6.3 7.7 %collective-permute-start.5 = (bf16[256,128]{1,0:T(8,128)(2,1)S(1)}, bf16[256,128]{1,0:T(8,128)(2,1)S(1)}, u32[]{:S(2)}, u32[]{:S(2)}) collective-permute-start(bf16[256,128]{1,0:T(8,128)(2,1)S(1)} %get-tuple-element.60.refs_0_), channel_id=1, source_target_pairs={{0,16},{4,20},{8,24},{12,28},{16,0},{20,4},{24,8},{28,12},{1,17},{... | collective-permute-start | bytes 196616 | tf_op jit(solution)/shard_map/ppermute | solution.py:483
  8.9 6.1 %collective-permute-start.6 = (bf16[256,128]{1,0:T(8,128)(2,1)S(1)}, bf16[256,128]{1,0:T(8,128)(2,1)S(1)}, u32[]{:S(2)}, u32[]{:S(2)}) collective-permute-start(bf16[256,128]{1,0:T(8,128)(2,1)S(1)} %get-tuple-element.60.refs_0_), channel_id=1, source_target_pairs={{0,24},{4,28},{8,16},{12,20},{16,8},{20,12},{24,0},{28,4},{1,25},{... | collective-permute-start | bytes 196616 | tf_op jit(solution)/shard_map/ppermute | solution.py:483
  9.8 3.7 %collective-permute-start.3 = (s32[8,256]{1,0:T(8,128)S(1)}, s32[8,256]{1,0:T(8,128)S(1)}, u32[]{:S(2)}, u32[]{:S(2)}) collective-permute-start(s32[8,256]{1,0:T(8,128)S(1)} %get-tuple-element.59), channel_id=1, source_target_pairs={{0,4},{4,0},{8,12},{12,8},{16,20},{20,16},{24,28},{28,24},{1,5},{5... | collective-permute-start | bytes 24584 | tf_op jit(solution)/shard_map/ppermute | solution.py:483
  13.5 16.0 %collective-permute-start.11 = (bf16[1024,128]{1,0:T(8,128)(2,1)}, bf16[1024,128]{1,0:T(8,128)(2,1)S(1)}, u32[]{:S(2)}, u32[]{:S(2)}) collective-permute-start(bf16[1024,128]{1,0:T(8,128)(2,1)} %r_2_.2), channel_id=1, source_target_pairs={{0,1},{1,0},{2,3},{3,2},{4,5},{5,4},{6,7},{7,6},{8,9},{9,8},{10,11... | collective-permute-start | bytes 786440 | tf_op jit(solution)/shard_map/ppermute | solution.py:480
  13.5 16.0 %collective-permute-start.13 = (bf16[1024,128]{1,0:T(8,128)(2,1)S(1)}, bf16[1024,128]{1,0:T(8,128)(2,1)S(1)}, u32[]{:S(2)}, u32[]{:S(2)}) collective-permute-start(bf16[1024,128]{1,0:T(8,128)(2,1)S(1)} %collective-permute-done.12.r_2_), channel_id=1, source_target_pairs={{0,1},{1,0},{2,3},{3,2},{4,5},{5,4},{6,7},{7,6},{8,9},{9,8},{10,11... | collective-permute-start | bytes 786440 | tf_op jit(solution)/shard_map/ppermute | solution.py:480
  15.6 5.0 %collective-permute-start.7 = (bf16[256,128]{1,0:T(8,128)(2,1)S(1)}, bf16[256,128]{1,0:T(8,128)(2,1)S(1)}, u32[]{:S(2)}, u32[]{:S(2)}) collective-permute-start(bf16[256,128]{1,0:T(8,128)(2,1)S(1)} %get-tuple-element.62), channel_id=1, source_target_pairs={{0,4},{1,5},{2,6},{3,7},{4,0},{5,1},{6,2},{7,3},{8,12},{9,13},{10,... | collective-permute-start | bytes 196616 | tf_op jit(solution)/shard_map/ppermute | solution.py:487
  17.2 4.8 %collective-permute-start.8 = (bf16[256,128]{1,0:T(8,128)(2,1)S(1)}, bf16[256,128]{1,0:T(8,128)(2,1)S(1)}, u32[]{:S(2)}, u32[]{:S(2)}) collective-permute-start(bf16[256,128]{1,0:T(8,128)(2,1)S(1)} %get-tuple-element.61.mine_ref), channel_id=1, source_target_pairs={{0,2},{1,3},{2,0},{3,1},{4,6},{5,7},{6,4},{7,5},{8,10},{9,11},{10,... | collective-permute-start | bytes 196616 | tf_op jit(solution)/shard_map/ppermute | solution.py:487
  17.7 5.2 %collective-permute-start.9 = (bf16[256,128]{1,0:T(8,128)(2,1)S(1)}, bf16[256,128]{1,0:T(8,128)(2,1)S(1)}, u32[]{:S(2)}, u32[]{:S(2)}) collective-permute-start(bf16[256,128]{1,0:T(8,128)(2,1)S(1)} %get-tuple-element.62), channel_id=1, source_target_pairs={{0,6},{1,7},{2,4},{3,5},{4,2},{5,3},{6,0},{7,1},{8,14},{9,15},{10,... | collective-permute-start | bytes 196616 | tf_op jit(solution)/shard_map/ppermute | solution.py:487
  20.6 4.4 %collective-permute-start.1 = (bf16[304,128]{1,0:T(8,128)(2,1)S(1)}, bf16[304,128]{1,0:T(8,128)(2,1)S(1)}, u32[]{:S(2)}, u32[]{:S(2)}) collective-permute-start(bf16[304,128]{1,0:T(8,128)(2,1)S(1)} %shard_map.159.r_0_.r_4_), channel_id=1, source_target_pairs={{0,2},{1,3},{2,0},{3,1},{4,6},{5,7},{6,4},{7,5},{8,10},{9,11},{10,... | collective-permute-start | bytes 233480 | tf_op jit(solution)/shard_map/ppermute | solution.py:480
  23.0 7.4 %collective-permute-start.10 = (bf16[2,256,128]{2,1,0:T(8,128)(2,1)S(1)}, bf16[2,256,128]{2,1,0:T(8,128)(2,1)S(1)}, u32[]{:S(2)}, u32[]{:S(2)}) collective-permute-start(bf16[2,256,128]{2,1,0:T(8,128)(2,1)S(1)} %shard_map.164.r_2_), channel_id=1, source_target_pairs={{0,1},{1,0},{2,3},{3,2},{4,5},{5,4},{6,7},{7,6},{8,9},{9,8},{10,11... | collective-permute-start | bytes 393224 | tf_op jit(solution)/shard_map/ppermute | solution.py:480
  23.0 4.4 %collective-permute-start = (bf16[304,128]{1,0:T(8,128)(2,1)S(1)}, bf16[304,128]{1,0:T(8,128)(2,1)S(1)}, u32[]{:S(2)}, u32[]{:S(2)}) collective-permute-start(bf16[304,128]{1,0:T(8,128)(2,1)S(1)} %shard_map.159.r_0_.r_4_), channel_id=1, source_target_pairs={{0,1},{1,0},{2,3},{3,2},{4,5},{5,4},{6,7},{7,6},{8,9},{9,8},{10,11... | collective-permute-start | bytes 233480 | tf_op jit(solution)/shard_map/ppermute | solution.py:480
  25.0 3.4 %collective-permute-start.2 = (bf16[304,128]{1,0:T(8,128)(2,1)S(1)}, bf16[304,128]{1,0:T(8,128)(2,1)S(1)}, u32[]{:S(2)}, u32[]{:S(2)}) collective-permute-start(bf16[304,128]{1,0:T(8,128)(2,1)S(1)} %collective-permute-done.1.r_0_.r_6_), channel_id=1, source_target_pairs={{0,1},{1,0},{2,3},{3,2},{4,5},{5,4},{6,7},{7,6},{8,9},{9,8},{10,11... | collective-permute-start | bytes 233480 | tf_op jit(solution)/shard_map/ppermute | solution.py:480
  31.9 40.3 %copy-start = (f32[1024,128]{1,0:T(8,128)S(1)}, f32[1024,128]{1,0:T(8,128)}, u32[]{:S(2)}) copy-start(f32[1024,128]{1,0:T(8,128)} %table_ref.1) | copy-start | bytes 1572868
  31.9 40.3 %copy-start.1 = (f32[1024,128]{1,0:T(8,128)S(1)}, f32[1024,128]{1,0:T(8,128)}, u32[]{:S(2)}) copy-start(f32[1024,128]{1,0:T(8,128)} %accum_ref.1) | copy-start | bytes 1572868
  32.7 40.6 %copy-start.2 = (f32[256,128]{1,0:T(8,128)S(1)}, f32[256,128]{1,0:T(8,128)}, u32[]{:S(2)}) copy-start(f32[256,128]{1,0:T(8,128)} %r_1_.1) | copy-start | bytes 393220
  32.7 40.6 %copy-start.3 = (f32[256,128]{1,0:T(8,128)S(1)}, f32[256,128]{1,0:T(8,128)}, u32[]{:S(2)}) copy-start(f32[256,128]{1,0:T(8,128)} %r_2_.3) | copy-start | bytes 393220
  32.7 1.7 %collective-permute-start.25 = (f32[2,256,128]{2,1,0:T(8,128)S(1)}, f32[2,256,128]{2,1,0:T(8,128)S(1)}, u32[]{:S(2)}, u32[]{:S(2)}) collective-permute-start(f32[2,256,128]{2,1,0:T(8,128)S(1)} %get-tuple-element.83), channel_id=1, source_target_pairs={{0,1},{1,0},{2,3},{3,2},{4,5},{5,4},{6,7},{7,6},{8,9},{9,8},{10,11... | collective-permute-start | bytes 786440 | tf_op jit(solution)/shard_map/ppermute | solution.py:480
  33.3 12.2 %collective-permute-start.14 = (f32[512,128]{1,0:T(8,128)S(1)}, f32[512,128]{1,0:T(8,128)S(1)}, u32[]{:S(2)}, u32[]{:S(2)}) collective-permute-start(f32[512,128]{1,0:T(8,128)S(1)} %get-tuple-element.75), channel_id=1, source_target_pairs={{0,1},{1,0},{2,3},{3,2},{4,5},{5,4},{6,7},{7,6},{8,9},{9,8},{10,11... | collective-permute-start | bytes 786440 | tf_op jit(solution)/shard_map/ppermute | solution.py:480
  34.5 5.8 %collective-permute-start.26 = (f32[256,128]{1,0:T(8,128)S(1)}, f32[256,128]{1,0:T(8,128)S(1)}, u32[]{:S(2)}, u32[]{:S(2)}) collective-permute-start(f32[256,128]{1,0:T(8,128)S(1)} %get-tuple-element.85), channel_id=1, source_target_pairs={{0,2},{1,3},{2,0},{3,1},{4,6},{5,7},{6,4},{7,5},{8,10},{9,11},{10,... | collective-permute-start | bytes 393224 | tf_op jit(solution)/shard_map/ppermute | solution.py:480
  41.3 32.0 %all-to-all-start = ((f32[8,72,128]{2,1,0:T(8,128)}), f32[8,72,128]{2,1,0:T(8,128)S(1)}, u32[]{:S(2)}, u32[]{:S(2)}) async-start(f32[8,72,128]{2,1,0:T(8,128)} %shard_map.175), calls=%async_computation | async-start | bytes 589824 | tf_op jit(solution)/shard_map/all_to_all | solution.py:673
  45.5 4.8 %collective-permute-start.15 = (f32[4,32,128]{2,1,0:T(8,128)S(1)}, f32[4,32,128]{2,1,0:T(8,128)S(1)}, u32[]{:S(2)}, u32[]{:S(2)}) collective-permute-start(f32[4,32,128]{2,1,0:T(8,128)S(1)} %get-tuple-element.77), channel_id=1, source_target_pairs={{0,2},{1,3},{2,0},{3,1},{4,6},{5,7},{6,4},{7,5},{8,10},{9,11},{10,... | collective-permute-start | bytes 196616 | tf_op jit(solution)/shard_map/ppermute | solution.py:487
  46.1 6.2 %collective-permute-start.16 = (f32[4,32,128]{2,1,0:T(8,128)S(1)}, f32[4,32,128]{2,1,0:T(8,128)S(1)}, u32[]{:S(2)}, u32[]{:S(2)}) collective-permute-start(f32[4,32,128]{2,1,0:T(8,128)S(1)} %get-tuple-element.78), channel_id=1, source_target_pairs={{0,4},{1,5},{2,6},{3,7},{4,0},{5,1},{6,2},{7,3},{8,12},{9,13},{10,... | collective-permute-start | bytes 196616 | tf_op jit(solution)/shard_map/ppermute | solution.py:487
  48.1 5.4 %collective-permute-start.17 = (f32[4,32,128]{2,1,0:T(8,128)S(1)}, f32[4,32,128]{2,1,0:T(8,128)S(1)}, u32[]{:S(2)}, u32[]{:S(2)}) collective-permute-start(f32[4,32,128]{2,1,0:T(8,128)S(1)} %get-tuple-element.79), channel_id=1, source_target_pairs={{0,6},{1,7},{2,4},{3,5},{4,2},{5,3},{6,0},{7,1},{8,14},{9,15},{10,... | collective-permute-start | bytes 196616 | tf_op jit(solution)/shard_map/ppermute | solution.py:487
  53.5 4.5 %collective-permute-start.18 = (f32[4,32,128]{2,1,0:T(8,128)S(1)}, f32[4,32,128]{2,1,0:T(8,128)S(1)}, u32[]{:S(2)}, u32[]{:S(2)}) collective-permute-start(f32[4,32,128]{2,1,0:T(8,128)S(1)} %shard_map.169.a_ref), channel_id=1, source_target_pairs={{0,8},{4,12},{8,0},{12,4},{16,24},{20,28},{24,16},{28,20},{1,9},{5... | collective-permute-start | bytes 196616 | tf_op jit(solution)/shard_map/ppermute | solution.py:483
  55.2 6.6 %collective-permute-start.19 = (f32[4,32,128]{2,1,0:T(8,128)S(1)}, f32[4,32,128]{2,1,0:T(8,128)S(1)}, u32[]{:S(2)}, u32[]{:S(2)}) collective-permute-start(f32[4,32,128]{2,1,0:T(8,128)S(1)} %shard_map.169.a_ref), channel_id=1, source_target_pairs={{0,16},{4,20},{8,24},{12,28},{16,0},{20,4},{24,8},{28,12},{1,17},{... | collective-permute-start | bytes 196616 | tf_op jit(solution)/shard_map/ppermute | solution.py:483
  57.4 6.1 %collective-permute-start.20 = (f32[4,32,128]{2,1,0:T(8,128)S(1)}, f32[4,32,128]{2,1,0:T(8,128)S(1)}, u32[]{:S(2)}, u32[]{:S(2)}) collective-permute-start(f32[4,32,128]{2,1,0:T(8,128)S(1)} %shard_map.169.a_ref), channel_id=1, source_target_pairs={{0,24},{4,28},{8,16},{12,20},{16,8},{20,12},{24,0},{28,4},{1,25},{... | collective-permute-start | bytes 196616 | tf_op jit(solution)/shard_map/ppermute | solution.py:483
  63.4 4.3 %collective-permute-start.21 = (f32[4,32,128]{2,1,0:T(8,128)S(1)}, f32[4,32,128]{2,1,0:T(8,128)S(1)}, u32[]{:S(2)}, u32[]{:S(2)}) collective-permute-start(f32[4,32,128]{2,1,0:T(8,128)S(1)} %shard_map.170.refs_0_), channel_id=1, source_target_pairs={{0,2},{1,3},{2,0},{3,1},{4,6},{5,7},{6,4},{7,5},{8,10},{9,11},{10,... | collective-permute-start | bytes 196616 | tf_op jit(solution)/shard_map/ppermute | solution.py:487
  64.8 4.3 %collective-permute-start.22 = (f32[4,32,128]{2,1,0:T(8,128)S(1)}, f32[4,32,128]{2,1,0:T(8,128)S(1)}, u32[]{:S(2)}, u32[]{:S(2)}) collective-permute-start(f32[4,32,128]{2,1,0:T(8,128)S(1)} %shard_map.170.refs_0_), channel_id=1, source_target_pairs={{0,4},{1,5},{2,6},{3,7},{4,0},{5,1},{6,2},{7,3},{8,12},{9,13},{10,... | collective-permute-start | bytes 196616 | tf_op jit(solution)/shard_map/ppermute | solution.py:487
  65.4 5.2 %collective-permute-start.23 = (f32[4,32,128]{2,1,0:T(8,128)S(1)}, f32[4,32,128]{2,1,0:T(8,128)S(1)}, u32[]{:S(2)}, u32[]{:S(2)}) collective-permute-start(f32[4,32,128]{2,1,0:T(8,128)S(1)} %shard_map.170.refs_0_), channel_id=1, source_target_pairs={{0,6},{1,7},{2,4},{3,5},{4,2},{5,3},{6,0},{7,1},{8,14},{9,15},{10,... | collective-permute-start | bytes 196616 | tf_op jit(solution)/shard_map/ppermute | solution.py:487
  70.6 1.6 %collective-permute-start.24 = (f32[512,128]{1,0:T(8,128)S(1)}, f32[512,128]{1,0:T(8,128)S(1)}, u32[]{:S(2)}, u32[]{:S(2)}) collective-permute-start(f32[512,128]{1,0:T(8,128)S(1)} %bitcast.9), channel_id=1, source_target_pairs={{0,1},{1,0},{2,3},{3,2},{4,5},{5,4},{6,7},{7,6},{8,9},{9,8},{10,11... | collective-permute-start | bytes 786440 | tf_op jit(solution)/shard_map/ppermute | solution.py:480
